TPU v7x, 32 devices: a whole 2x2x4 slice. The times are simulated.
32 devices in a mesh: table: 4 (over y, core), seq: 8 (over z, x).
Axes of the slice: x: 2, y: 2, z: 4, core: 2. Of those that a mesh axis runs over, the one named last changes fastest.
Arguments:
- item_ids: int32 [4, 2048], P('table', 'seq'), may hold values from 0 to 131071, as said below
- history_len: int32 [4], P('table'), may hold values from 512 to 2048, as said below
- row_place: int32 [131072], replicated, may hold values from 0 to 131071, as said below
- item_table: bfloat16 [131072, 512], P(('table', 'seq')), may hold values from -6 to 6
- input_proj: bfloat16 [512, 2048], replicated, may hold values from -0.25 to 0.25
- output_proj: bfloat16 [512, 512], replicated, may hold values from -0.25 to 0.25
- out_cotangent: bfloat16 [4, 2048, 512], P('table', 'seq'), may hold values from -18 to 18
Outputs:
- layer_out: bfloat16 [4, 2048, 512], P('table', 'seq')
- table_grad: bfloat16 [131072, 512], P(('table', 'seq'))
Inputs may be any that keep to these rules, and one draw needn't show every extreme that they name: `item_ids`: within the 256 positions of one device, at most 24 items are stored in any one owner's block of 4096 table rows (rows o * 4096 to (o + 1) * 4096 - 1); one owner's block receives exactly 24 from the positions of every device. `row_place`: A permutation: every table row holds exactly one item. `history_len`: at least one history fills all 2048 positions.
All inputs are finite; a program needn't handle non-finite values.
Results may differ from a plain program's by a relative error of at most 0.006.
Values may be sent and summed in bfloat16 or wider, within the bound.
No kernel may reach another device: no remote copies, remote signals or barrier semaphores. Data moves between devices by JAX's collectives and lax.ppermute only.
A program may use at most 128 MiB of HBM per device.

v0:
```python
import functools
import math

import jax
import jax.numpy as jnp
from jax import lax
from jax.experimental import pallas as pl
from jax.experimental.pallas import tpu as pltpu
from jax.sharding import Mesh, PartitionSpec as P

HEADS = 8
eps_norm = 1e-05
LANES = 128
ALL = ("t", "o", "i")
GROUP = ("t", "i")
f32 = jnp.float32
bf16 = jnp.bfloat16
i32 = jnp.int32


def vmem():
    return pl.BlockSpec(memory_space=pltpu.VMEM)


def smem():
    return pl.BlockSpec(memory_space=pltpu.SMEM)


def params():
    return pltpu.CompilerParams(vmem_limit_bytes=24 * 1024 * 1024)


def near(array):
    return pltpu.with_memory_space_constraint(array, pltpu.VMEM)


def kernel_call(kernel, outs, args, number=None, scratch=()):
    numbers = [] if number is None else [number]
    return pl.pallas_call(
        kernel,
        out_shape=tuple(pltpu.VMEM(shape, dtype) for shape, dtype in outs),
        in_specs=[smem()] * len(numbers) + [vmem()] * len(args),
        out_specs=tuple(vmem() for unused in outs),
        scratch_shapes=list(scratch),
        compiler_params=params(),
    )(*numbers, *map(near, args))


def dot(lhs, rhs, dims=((1,), (0,))):
    return lax.dot_general(lhs, rhs, (dims, ((), ())), preferred_element_type=f32)


def dsilu_of(inputs):
    sig = 0.5 + 0.5 * jnp.tanh(0.5 * inputs)
    return sig * (1.0 + inputs * (1.0 - sig))


def silu_of(inputs):
    half = 0.5 * inputs
    return half + half * jnp.tanh(half)


def iota(shape, axis):
    return lax.broadcasted_iota(i32, shape, axis)


def to_col(row):
    size = row.shape[1]
    same = iota((size, size), 0) == iota((size, size), 1)
    return jnp.sum(jnp.where(same, row, 0.0), axis=1, keepdims=True)


def to_row(col):
    size = col.shape[0]
    same = iota((size, size), 0) == iota((size, size), 1)
    return jnp.sum(jnp.where(same, col, 0.0), axis=0, keepdims=True)


def request_kernel(
    rows_dev, cap, ids_s, first_s, length_s, ids_ref, place_ref, mail_ref, rows_scr
):
    count = ids_ref.shape[1]

    def fetch(step, unused):
        rows_scr[pl.ds(step, 1), :] = place_ref[pl.ds(ids_s[0, step] >> 7, 1), :]
        return unused

    lax.fori_loop(0, count, fetch, 0, unroll=8)
    lane_col = to_col((ids_ref[...] & (LANES - 1)).astype(f32)).astype(i32)
    lanes = iota((count, LANES), 1)
    stored = jnp.sum(
        jnp.where(lanes == lane_col, rows_scr[...].astype(f32), 0.0), axis=1, keepdims=True
    ).astype(i32)
    shift = rows_dev.bit_length() - 1
    owner = stored >> shift
    local_row = stored & (rows_dev - 1)
    hits = lanes == owner
    hits_f = jnp.where(hits, 1.0, 0.0)
    before = jnp.where(iota((count, count), 1) < iota((count, count), 0), 1.0, 0.0)
    earlier = dot(before.astype(bf16), hits_f.astype(bf16))
    rank = jnp.sum(jnp.where(hits, earlier, 0.0), axis=1, keepdims=True)
    in_rank = lanes == rank.astype(i32)
    asked = local_row + 1
    high = jnp.where(in_rank, (asked >> 7).astype(f32), 0.0).astype(bf16)
    low = jnp.where(in_rank, (asked & 127).astype(f32), 0.0).astype(bf16)
    hits_t = hits_f.T.astype(bf16)
    owners = mail_ref.shape[0]
    wish = dot(hits_t, high) * 128.0 + dot(hits_t, low)
    mail_ref[:, :LANES] = wish[:owners].astype(i32) - 1
    slot = owner.astype(f32) * cap + rank
    live = (first_s[0] + iota((1, count), 1)) < length_s[0]
    note = to_row(slot).astype(i32) * 2 + jnp.where(live, 1, 0)
    mail_ref[:, LANES:] = jnp.broadcast_to(note, (owners, count))


def read_note(twin_s, mail_ref):
    note = mail_ref[pl.ds(twin_s[0], 1), LANES:]
    return note >> 1, (note & 1).astype(f32)


def normalize(inputs):
    centred = inputs - jnp.mean(inputs, axis=-1, keepdims=True)
    spread = jnp.sqrt(jnp.mean(centred * centred, axis=-1, keepdims=True) + eps_norm)
    return (centred / spread, spread)


def project_kernel(
    twin_s, mail_ref, rows_ref, cot_ref, w_ref, wo_ref, send_ref, emb_ref, pre_ref, mgrad_ref
):
    slot_row, live_row = read_note(twin_s, mail_ref)
    count = slot_row.shape[1]
    slots, width = rows_ref.shape
    head = width // HEADS
    slot_col = to_col(slot_row.astype(f32)).astype(i32)
    live_col = to_col(live_row)
    picks = jnp.where(iota((count, slots), 1) == slot_col, 1.0, 0.0).astype(bf16)
    embedded = dot(picks, rows_ref[...])
    emb_ref[...] = embedded.astype(bf16)
    normed, _ = normalize(embedded)
    pre = dot(normed.astype(bf16), w_ref[...])
    pre_ref[...] = pre
    cot = jnp.where(live_col > 0.0, cot_ref[...].astype(f32), 0.0).astype(bf16)
    mgrad = dot(cot, wo_ref[...], ((1,), (1,)))
    mgrad_ref[...] = mgrad
    act = silu_of(pre)
    dz = mgrad * act[:, :width]
    for h in range(HEADS):
        lo = h * head
        send_ref[h] = jnp.concatenate(
            [
                act[:, 2 * width + lo : 2 * width + lo + head],
                act[:, 3 * width + lo : 3 * width + lo + head],
                act[:, width + lo : width + lo + head],
                dz[:, lo : lo + head],
            ],
            axis=1,
        ).astype(bf16)


def weight_tile(keys, queries_t):
    scores = dot(keys, queries_t)
    sig = 0.5 + 0.5 * jnp.tanh(0.5 * scores)
    wgt = scores * sig
    return wgt, sig + wgt * (1.0 - sig)


def causal_mask(rows):
    return iota((rows, rows), 0) <= iota((rows, rows), 1)


def forward_kernel(order, ready, x_ref, att_ref, dz_ref, stat_ref, *refs):
    if ready:
        wgt_ref, slope_ref = refs[:2]
    vt_scr = refs[-1]
    blocks, rows, cols = x_ref.shape
    head = cols // 4
    scale = head ** (-0.5)
    causal = causal_mask(rows)
    place = 0
    for b in range(blocks):
        queries_t = (x_ref[order[b], :, 0:head].astype(f32) * scale).T.astype(bf16)
        vt_scr[b] = x_ref[order[b], :, 2 * head : 3 * head].astype(f32).T.astype(bf16)
        att = jnp.zeros((head, rows), f32)
        for c in range(b + 1):
            wgt, slope = weight_tile(x_ref[order[c], :, head : 2 * head], queries_t)
            if b == c:
                wgt = jnp.where(causal, wgt, 0.0)
                slope = jnp.where(causal, slope, 0.0)
            wgt = wgt.astype(bf16)
            att = att + dot(vt_scr[c], wgt)
            if ready:
                wgt_ref[place] = wgt
                slope_ref[place] = slope
            place += 1
        dz = x_ref[order[b], :, 3 * head :].astype(f32).T
        att_ref[b] = att
        dz_ref[b] = dz
        mean = jnp.sum(att, axis=0, keepdims=True) * (1.0 / head)
        cent = att - mean
        stat_ref[0, b : b + 1, :] = mean
        stat_ref[1, b : b + 1, :] = jnp.sum(cent * cent, axis=0, keepdims=True)
        stat_ref[2, b : b + 1, :] = jnp.sum(dz, axis=0, keepdims=True)
        stat_ref[3, b : b + 1, :] = jnp.sum(cent * dz, axis=0, keepdims=True)


def backward_kernel(copies, order, ready, *refs):
    if ready:
        x_ref, wgt_ref, slope_ref, att_ref, dz_ref, stats_ref, out_ref = refs[:7]
        dq_scr, da_scr, dat_scr, q_scr = refs[7:]
    else:
        x_ref, att_ref, dz_ref, stats_ref, out_ref = refs[:5]
        dq_scr, da_scr, dat_scr, q_scr, qt_scr = refs[5:]
    blocks, rows, cols = x_ref.shape
    head = cols // 4
    scale = head ** (-0.5)
    width = head * HEADS
    heads = range(0, HEADS * copies, copies)
    mean = sum(stats_ref[h, 0] for h in heads) * (1.0 / HEADS)
    square = 0.0
    dz_sum = 0.0
    dz_att = 0.0
    for h in heads:
        off = stats_ref[h, 0] - mean
        square = square + (stats_ref[h, 1] + head * (off * off))
        dz_sum = dz_sum + stats_ref[h, 2]
        dz_att = dz_att + (stats_ref[h, 3] + stats_ref[h, 2] * off)
    inv = 1.0 / jnp.sqrt(square * (1.0 / width) + eps_norm)
    mean_dz = dz_sum * (1.0 / width)
    mean_prod = dz_att * inv * (1.0 / width)
    for b in range(blocks):
        att_n = (att_ref[b] - mean[b : b + 1]) * inv[b : b + 1]
        da_t = (dz_ref[b] - mean_dz[b : b + 1] - att_n * mean_prod[b : b + 1]) * inv[b : b + 1]
        out_ref[order[b], :, 3 * head :] = att_n.T.astype(bf16)
        dat_scr[b] = da_t.astype(bf16)
        da_scr[b] = da_t.T.astype(bf16)
        q = x_ref[order[b], :, 0:head].astype(f32) * scale
        q_scr[b] = q.astype(bf16)
        if not ready:
            qt_scr[b] = q.T.astype(bf16)
    causal = causal_mask(rows)
    for c in range(blocks):
        keys = x_ref[order[c], :, head : 2 * head]
        keys_t = keys.astype(f32).T.astype(bf16)
        values = x_ref[order[c], :, 2 * head : 3 * head]
        dk = jnp.zeros((rows, head), f32)
        dv = jnp.zeros((rows, head), f32)
        for b in range(c, blocks):
            if ready:
                place = b * (b + 1) // 2 + c
                wgt = wgt_ref[place]
                slope = slope_ref[place]
            else:
                wgt, slope = weight_tile(keys, qt_scr[b])
                if b == c:
                    wgt = jnp.where(causal, wgt, 0.0)
                    slope = jnp.where(causal, slope, 0.0)
                wgt = wgt.astype(bf16)
            sgrad = (dot(values, dat_scr[b]) * slope).astype(bf16)
            dv = dv + dot(wgt, da_scr[b])
            dk = dk + dot(sgrad, q_scr[b])
            part = dot(keys_t, sgrad)
            if c == 0:
                dq_scr[b] = part
            else:
                dq_scr[b] = dq_scr[b] + part
        out_ref[order[c], :, head : 2 * head] = dk.astype(bf16)
        out_ref[order[c], :, 2 * head : 3 * head] = dv.astype(bf16)
        out_ref[order[c], :, 0:head] = (dq_scr[c] * scale).T.astype(bf16)


def head_columns(grad_ref, copies, part, head):
    return jnp.concatenate(
        [
            grad_ref[h * copies, :, part * head : (part + 1) * head].astype(f32)
            for h in range(HEADS)
        ],
        axis=1,
    )


def finish_kernel(
    copies,
    twin_s,
    mail_ref,
    grad_ref,
    pre_ref,
    mgrad_ref,
    emb_ref,
    cot_ref,
    w_ref,
    wo_ref,
    out_ref,
    layer_ref,
):
    slot_row, live_row = read_note(twin_s, mail_ref)
    count, width = emb_ref.shape
    slots = out_ref.shape[0]
    head = width // HEADS
    live_col = to_col(live_row)
    columns = functools.partial(head_columns, grad_ref, copies, head=head)
    att_n = columns(3)
    mixed = (att_n * silu_of(pre_ref[:, :width])).astype(bf16)
    branch = dot(mixed, wo_ref[...])
    embedded = emb_ref[...].astype(f32)
    layer_ref[...] = (live_col * (embedded + branch)).astype(bf16)
    act_grad = jnp.concatenate(
        [mgrad_ref[...] * att_n, columns(2), columns(0), columns(1)], axis=1
    )
    pre_grad = (act_grad * dsilu_of(pre_ref[...])).astype(bf16)
    norm_grad = dot(pre_grad, w_ref[...], ((1,), (1,)))
    normed, spread = normalize(embedded)
    mean_grad = jnp.mean(norm_grad, axis=-1, keepdims=True)
    mean_prod = jnp.mean(norm_grad * normed, axis=-1, keepdims=True)
    cot = jnp.where(live_col > 0.0, cot_ref[...].astype(f32), 0.0)
    emb_grad = cot + (norm_grad - mean_grad - normed * mean_prod) / spread
    places = jnp.where(iota((slots, count), 0) == slot_row, 1.0, 0.0).astype(bf16)
    out_ref[...] = dot(places, emb_grad.astype(bf16)).astype(bf16)


def table_kernel(asked_ref, arrived_ref, out_ref):
    rows = out_ref.shape[0]
    slots = arrived_ref.shape[0]
    local_row = asked_ref[...] - pl.program_id(0) * rows
    part = math.gcd(rows, 256)
    ramp = iota((part, slots), 0).astype(f32).astype(bf16)
    for start in range(0, rows, part):
        near_row = local_row - start
        inside = (near_row >= 0) & (near_row < part)
        near_row = jnp.where(inside, near_row, -1).astype(f32)
        near_row = jnp.broadcast_to(near_row, (16, slots)).astype(bf16)[0:1]
        picks = jnp.where(ramp == near_row, jnp.ones((), bf16), jnp.zeros((), bf16))
        out_ref[start : start + part, :] = dot(picks, arrived_ref[...]).astype(bf16)


def all_to_all(pieces, axes):
    return lax.all_to_all(pieces, axes, split_axis=0, concat_axis=0, tiled=True)


def local(item_ids, history_len, row_place, item_table, input_proj, output_proj, out_cotangent):
    count = item_ids.shape[1]
    rows_dev, width = item_table.shape
    users = lax.axis_size("t")
    inner = lax.axis_size("i")
    owners = users * users * inner
    group = users * inner
    copies = group // HEADS
    cap = 3 * count // owners
    slots = owners * cap
    head = width // HEADS
    half = users // 2
    forth = [(a % 2) * half + a // 2 for a in range(users)]
    swap = [
        (a * users + b, forth[b] * users + forth.index(a))
        for a in range(users)
        for b in range(users)
    ]
    order = tuple(forth[b // inner] * inner + b % inner for b in range(group))
    moved = functools.partial(lax.ppermute, axis_name=("t", "o"), perm=swap)

    def swapped(pieces):
        shape = pieces.shape
        parts = pieces.reshape((2, half, half, 2, inner) + shape[1:])
        return jnp.transpose(parts, (3, 2, 1, 0, 4, 5)).reshape(shape)

    cot = moved(out_cotangent[0])
    first = (lax.axis_index("o") * inner + lax.axis_index("i")) * count
    mail = pl.pallas_call(
        functools.partial(request_kernel, rows_dev, cap),
        out_shape=pltpu.VMEM((owners, LANES + count), i32),
        in_specs=[smem(), smem(), smem(), vmem(), vmem()],
        out_specs=vmem(),
        scratch_shapes=[pltpu.VMEM((count, LANES), i32)],
        compiler_params=params(),
        name="requests",
    )(
        item_ids,
        first.reshape(1).astype(i32),
        history_len,
        item_ids,
        row_place.reshape(-1, LANES),
    )
    mail = all_to_all(mail, ALL)
    wanted = swapped(mail[:, :cap]).reshape(slots)
    old_t = (lax.axis_index("o") % 2) * half + lax.axis_index("o") // 2
    old_o = (lax.axis_index("t") % half) * 2 + lax.axis_index("t") // half
    twin = (old_t * users + old_o) * inner + lax.axis_index("i")
    twin = twin.reshape(1).astype(i32)
    rows = item_table[jnp.maximum(wanted, 0)]
    rows = all_to_all(rows.reshape(owners, cap, width), ALL).reshape(slots, width)

    send, emb, pre, mgrad = kernel_call(
        project_kernel,
        (
            ((HEADS, count, 4 * head), bf16),
            ((count, width), bf16),
            ((count, 4 * width), f32),
            ((count, width), f32),
        ),
        (mail, rows, cot, input_proj, output_proj), twin,
    )
    if copies > 1:
        send = jnp.repeat(send, copies, axis=0)
    mine = all_to_all(send, GROUP)
    tiles = group * (group + 1) // 2
    ready = tiles * count * count * 6 <= 16 * 1024 * 1024
    att, dz, stat, *weights = kernel_call(
        functools.partial(forward_kernel, order, ready),
        (
            ((group, head, count), f32),
            ((group, head, count), f32),
            ((4, group, count), f32),
        )
        + (((tiles, count, count), bf16), ((tiles, count, count), f32)) * ready,
        (mine,),
        scratch=[pltpu.VMEM((group, head, count), bf16)],
    )
    stats = all_to_all(jnp.broadcast_to(stat[None], (group,) + stat.shape), GROUP)
    scratch = [
        pltpu.VMEM((group, head, count), f32),
        pltpu.VMEM((group, count, head), bf16),
        pltpu.VMEM((group, head, count), bf16),
        pltpu.VMEM((group, count, head), bf16),
    ]
    if not ready:
        scratch.append(pltpu.VMEM((group, head, count), bf16))
    (grads,) = kernel_call(
        functools.partial(backward_kernel, copies, order, ready),
        (((group, count, 4 * head), bf16),),
        (mine, *weights, att, dz, stats),
        scratch=scratch,
    )
    back = all_to_all(grads, GROUP)
    outgoing, layer_out = kernel_call(
        functools.partial(finish_kernel, copies),
        (((slots, width), bf16), ((count, width), bf16)),
        (mail, back, pre, mgrad, emb, cot, input_proj, output_proj),
        twin,
    )
    arrived = all_to_all(outgoing.reshape(owners, cap, width), ALL).reshape(slots, width)
    layer_out = moved(layer_out)
    tile = min(rows_dev, 512)
    table_grad = pl.pallas_call(
        table_kernel,
        out_shape=jax.ShapeDtypeStruct((rows_dev, width), bf16),
        grid=(rows_dev // tile,),
        in_specs=[vmem(), vmem()],
        out_specs=pl.BlockSpec((tile, width), lambda r: (r, 0)),
        compiler_params=params(),
        name="table_grad",
    )(near(wanted.reshape(1, slots)), near(arrived))
    return (layer_out[None], table_grad)


def solution(mesh):
    users = mesh.shape["table"]
    inner = mesh.shape["seq"] // users
    if mesh.shape["seq"] % users or (users * inner) % HEADS:
        raise ValueError("unsupported mesh")
    finer = Mesh(mesh.devices.reshape(users, users, inner), ("t", "o", "i"))
    placed = (
        P("t", ("o", "i")),
        P("t"),
        P(),
        P(("t", "o", "i"), None),
        P(),
        P(),
        P("t", ("o", "i"), None),
    )

    return jax.shard_map(
        local,
        mesh=finer,
        in_specs=placed,
        out_specs=(P("t", ("o", "i"), None), P(("t", "o", "i"), None)),
        check_vma=False,
    )
```

profile of v0, /device:TPU:1, one launch (start us, length us, event | category | flops | bytes accessed | tf_op | source)
XLA Modules:
  0.0 150.9 jit_solution(7473325068366087512)
XLA Ops:
  1.3 0.0 copy-start.2
  1.3 1.0 copy-done.2
  2.3 0.0 copy-start.3
  2.3 0.7 copy-done.3
  3.0 1.6 %requests.1 = s32[32,384]{1,0:T(8,128)S(1)} custom-call(s32[1,256]{1,0:T(1,128)S(1)} %copy-done.3, s32[1]{0:T(128)} %bitcast.1.first_s, s32[1]{0:T(128)S(6)} %copy.20.length_s, s32[1,256]{1,0:T(1,128)S(1)} %copy-done.3, s32[1024,128]{1,0:T(8,128)S(1)} %bitcast.24), custom_call_target="tpu_custom_call" | custom-call | tf_op jit(solution)/shard_map/requests/pallas_call | solution.py:367
  4.6 0.1 copy.10
  4.7 14.0 %all_to_all.36 = s32[32,1,384]{2,1,0:T(1,128)S(1)} all-to-all(s32[32,1,384]{2,1,0:T(1,128)S(1)} %copy.10), channel_id=1, replica_groups=mesh['t'=4,'o'=4,'i'=2] {'t','o','i'}, dimensions={0} | all-to-all | bytes 98304 | tf_op jit(solution)/shard_map/all_to_all | solution.py:336
  18.7 0.1 reshape.53
  18.8 0.0 copy-start
  18.8 0.0 copy-start.1
  18.9 6.2 %gather_fusion = bf16[768,512]{1,0:T(8,128)(2,1)} fusion(bf16[4096,512]{1,0:T(8,128)(2,1)} %param.10, s32[1024]{0:T(1024)S(1)} %pad_clamp_fusion), kind=kCustom, calls=%fused_computation | custom fusion | bytes 1575936 | tf_op jit(solution)/shard_map/gather | solution.py:388
  25.1 2.6 %all-to-all-start.1 = ((bf16[32,24,512]{2,1,0:T(8,128)(2,1)}), bf16[32,24,512]{2,1,0:T(8,128)(2,1)S(1)}, u32[]{:S(2)}, u32[]{:S(2)}) async-start(bf16[32,24,512]{2,1,0:T(8,128)(2,1)} %bitcast.26), calls=%async_computation.1 | async-start | bytes 1572864 | tf_op jit(solution)/shard_map/all_to_all | solution.py:336
  27.7 4.6 %collective-permute-start = (bf16[256,512]{1,0:T(8,128)(2,1)}, bf16[256,512]{1,0:T(8,128)(2,1)}, u32[]{:S(2)}, u32[]{:S(2)}) collective-permute-start(bf16[256,512]{1,0:T(8,128)(2,1)} %bitcast.31), channel_id=1, source_target_pairs={{0,0},{2,16},{4,8},{6,24},{8,4},{10,20},{12,12},{14,28},{16,2},{18... | collective-permute-start | bytes 786440 | tf_op jit(solution)/shard_map/ppermute | solution.py:365
  32.3 21.4 %collective-permute-done.cot_ref = bf16[256,512]{1,0:T(8,128)(2,1)} collective-permute-done((bf16[256,512]{1,0:T(8,128)(2,1)}, bf16[256,512]{1,0:T(8,128)(2,1)}, u32[]{:S(2)}, u32[]{:S(2)}) %collective-permute-start) | collective-permute-done | bytes 262176 | tf_op jit(solution)/shard_map/ppermute | solution.py:365
  53.7 0.0 all-to-all-done.1
  53.7 0.0 copy-done
  53.7 0.0 copy-done.1
  53.7 2.7 %shard_map.86 = (bf16[8,256,256]{2,1,0:T(8,128)(2,1)S(1)}, bf16[256,512]{1,0:T(8,128)(2,1)S(1)}, f32[256,2048]{1,0:T(8,128)S(1)}, f32[256,512]{1,0:T(8,128)S(1)}) custom-call(s32[1]{0:T(128)} %bitcast.twin_s, s32[32,384]{1,0:T(8,128)S(1)} %bitcast.22, bf16[768,512]{1,0:T(8,128)(2,1)S(1)} %bitcast.20, bf16[256,512]{1,0:T(8,128)(2,1)} %collective-permute-done.cot_ref, ...), custom_call_target="tpu_custom_call" | custom-call | tf_op jit(solution)/shard_map/pallas_call | solution.py:39
  56.5 17.0 %all_to_all.37.x_ref.refs_0_ = bf16[8,256,256]{2,1,0:T(8,128)(2,1)S(1)} all-to-all(bf16[8,256,256]{2,1,0:T(8,128)(2,1)S(1)} %get-tuple-element.13), channel_id=1, replica_groups=mesh['t'=4,'o'=4,'i'=2] {'t','i'}, dimensions={0} | all-to-all | bytes 2097152 | tf_op jit(solution)/shard_map/all_to_all | solution.py:336
  73.5 4.7 %shard_map.87 = (f32[8,64,256]{2,1,0:T(8,128)S(1)}, f32[8,64,256]{2,1,0:T(8,128)S(1)}, f32[4,8,256]{2,1,0:T(8,128)S(1)}, bf16[36,256,256]{2,1,0:T(8,128)(2,1)S(1)}, f32[36,256,256]{2,1,0:T(8,128)S(1)}) custom-call(bf16[8,256,256]{2,1,0:T(8,128)(2,1)S(1)} %all_to_all.37.x_ref.refs_0_), custom_call_target="tpu_custom_call" | custom-call | tf_op jit(solution)/shard_map/pallas_call | solution.py:39
  78.2 8.7 %all_to_all.38.refs_5_ = f32[8,4,8,256]{3,2,1,0:T(8,128)S(1)} all-to-all(f32[8,4,8,256]{3,2,1,0:T(8,128)S(1)} %broadcast_in_dim.4), channel_id=1, replica_groups=mesh['t'=4,'o'=4,'i'=2] {'t','i'}, dimensions={0} | all-to-all | bytes 524288 | tf_op jit(solution)/shard_map/all_to_all | solution.py:336
  86.9 6.4 %shard_map.88 = bf16[8,256,256]{2,1,0:T(8,128)(2,1)S(1)} custom-call(bf16[8,256,256]{2,1,0:T(8,128)(2,1)S(1)} %all_to_all.37.x_ref.refs_0_, bf16[36,256,256]{2,1,0:T(8,128)(2,1)S(1)} %get-tuple-element.14.refs_1_, f32[36,256,256]{2,1,0:T(8,128)S(1)} %get-tuple-element.15.refs_2_, f32[8,64,256]{2,1,0:T(8,128)S(1)} %get-tuple-element.16.refs_3_, ...), custom_call_target="tpu_custom_call" | custom-call | tf_op jit(solution)/shard_map/pallas_call | solution.py:39
  93.3 17.2 %all_to_all.39.grad_ref = bf16[8,256,256]{2,1,0:T(8,128)(2,1)S(1)} all-to-all(bf16[8,256,256]{2,1,0:T(8,128)(2,1)S(1)} %shard_map.88), channel_id=1, replica_groups=mesh['t'=4,'o'=4,'i'=2] {'t','i'}, dimensions={0} | all-to-all | bytes 2097152 | tf_op jit(solution)/shard_map/all_to_all | solution.py:336
  110.5 4.0 %shard_map.89 = (bf16[768,512]{1,0:T(8,128)(2,1)}, bf16[256,512]{1,0:T(8,128)(2,1)S(1)}) custom-call(s32[1]{0:T(128)} %bitcast.twin_s, s32[32,384]{1,0:T(8,128)S(1)} %bitcast.23, bf16[8,256,256]{2,1,0:T(8,128)(2,1)S(1)} %all_to_all.39.grad_ref, f32[256,2048]{1,0:T(8,128)S(1)} %get-tuple-element.19.pre_ref, f32[256,512]{1,0:T(8,128)S(1)} %get-tuple-element.20.mgrad_ref, ...), custom_call_target="tpu_custom_call" | custom-call | tf_op jit(solution)/shard_map/pallas_call | solution.py:39
  114.5 3.9 %all-to-all-start.5 = ((bf16[32,24,512]{2,1,0:T(8,128)(2,1)}), bf16[32,24,512]{2,1,0:T(8,128)(2,1)S(1)}, u32[]{:S(2)}, u32[]{:S(2)}) async-start(bf16[32,24,512]{2,1,0:T(8,128)(2,1)} %bitcast.10), calls=%async_computation.5 | async-start | bytes 1572864 | tf_op jit(solution)/shard_map/all_to_all | solution.py:336
  118.4 4.4 %collective-permute-start.1 = (bf16[256,512]{1,0:T(8,128)(2,1)S(1)}, bf16[256,512]{1,0:T(8,128)(2,1)S(1)}, u32[]{:S(2)}, u32[]{:S(2)}) collective-permute-start(bf16[256,512]{1,0:T(8,128)(2,1)S(1)} %get-tuple-element.22), channel_id=1, source_target_pairs={{0,0},{2,16},{4,8},{6,24},{8,4},{10,20},{12,12},{14,28},{16,2},{18... | collective-permute-start | bytes 786440 | tf_op jit(solution)/shard_map/ppermute | solution.py:440
  122.9 0.1 reshape_reshape_reshape.3.asked_ref
  123.0 21.2 %collective-permute-done.1 = bf16[256,512]{1,0:T(8,128)(2,1)S(1)} collective-permute-done((bf16[256,512]{1,0:T(8,128)(2,1)S(1)}, bf16[256,512]{1,0:T(8,128)(2,1)S(1)}, u32[]{:S(2)}, u32[]{:S(2)}) %collective-permute-start.1) | collective-permute-done | bytes 262176 | tf_op jit(solution)/shard_map/ppermute | solution.py:440
  144.2 0.0 all-to-all-done.5
  144.2 6.0 %table_grad.1 = bf16[4096,512]{1,0:T(8,128)(2,1)} custom-call(s32[1,768]{1,0:T(1,128)S(1)} %reshape_reshape_reshape.3.asked_ref, bf16[768,512]{1,0:T(8,128)(2,1)S(1)} %bitcast.19), custom_call_target="tpu_custom_call" | custom-call | tf_op jit(solution)/shard_map/table_grad/pallas_call | solution.py:442
  150.2 0.7 copy.21
  (6 shorter events, 0.1 us)
Async XLA Ops:
  1.3 1.0 copy-start.2
  2.3 0.7 copy-start.3
  18.8 34.9 %copy-start = (bf16[512,2048]{1,0:T(8,128)(2,1)S(1)}, bf16[512,2048]{1,0:T(8,128)(2,1)}, u32[]{:S(2)}) copy-start(bf16[512,2048]{1,0:T(8,128)(2,1)} %w_ref.3) | copy-start | bytes 6291460
  18.8 34.9 %copy-start.1 = (bf16[512,512]{1,0:T(8,128)(2,1)S(1)}, bf16[512,512]{1,0:T(8,128)(2,1)}, u32[]{:S(2)}) copy-start(bf16[512,512]{1,0:T(8,128)(2,1)} %wo_ref.3) | copy-start | bytes 1572868
  25.1 28.6 %all-to-all-start.1 = ((bf16[32,24,512]{2,1,0:T(8,128)(2,1)}), bf16[32,24,512]{2,1,0:T(8,128)(2,1)S(1)}, u32[]{:S(2)}, u32[]{:S(2)}) async-start(bf16[32,24,512]{2,1,0:T(8,128)(2,1)} %bitcast.26), calls=%async_computation.1 | async-start | bytes 1572864 | tf_op jit(solution)/shard_map/all_to_all | solution.py:336
  27.7 26.0 %collective-permute-start = (bf16[256,512]{1,0:T(8,128)(2,1)}, bf16[256,512]{1,0:T(8,128)(2,1)}, u32[]{:S(2)}, u32[]{:S(2)}) collective-permute-start(bf16[256,512]{1,0:T(8,128)(2,1)} %bitcast.31), channel_id=1, source_target_pairs={{0,0},{2,16},{4,8},{6,24},{8,4},{10,20},{12,12},{14,28},{16,2},{18... | collective-permute-start | bytes 786440 | tf_op jit(solution)/shard_map/ppermute | solution.py:365
  114.5 29.7 %all-to-all-start.5 = ((bf16[32,24,512]{2,1,0:T(8,128)(2,1)}), bf16[32,24,512]{2,1,0:T(8,128)(2,1)S(1)}, u32[]{:S(2)}, u32[]{:S(2)}) async-start(bf16[32,24,512]{2,1,0:T(8,128)(2,1)} %bitcast.10), calls=%async_computation.5 | async-start | bytes 1572864 | tf_op jit(solution)/shard_map/all_to_all | solution.py:336
  118.4 25.8 %collective-permute-start.1 = (bf16[256,512]{1,0:T(8,128)(2,1)S(1)}, bf16[256,512]{1,0:T(8,128)(2,1)S(1)}, u32[]{:S(2)}, u32[]{:S(2)}) collective-permute-start(bf16[256,512]{1,0:T(8,128)(2,1)S(1)} %get-tuple-element.22), channel_id=1, source_target_pairs={{0,0},{2,16},{4,8},{6,24},{8,4},{10,20},{12,12},{14,28},{16,2},{18... | collective-permute-start | bytes 786440 | tf_op jit(solution)/shard_map/ppermute | solution.py:440
where the time goes:
time: 152 us; the launch traced here: 151 us
  blocking collectives  56.9 us (37%)
  waiting for transfers between devices  42.6 us (28%)
  Pallas kernels  25.4 us (17%)
  starting transfers between devices  15.5 us (10%)
  local copies, waits for them, and re-layouts  8.94 us (6%)
    all_to_all x4, blocking collectives, all_to_all(): return lax.all_to_all(pieces, axes, split_axis=0, concat_axis=0, tiled=True)  56.9 us
    ppermute x1, waiting for transfers between devices, local(): cot = moved(out_cotangent[0])  21.4 us
    ppermute x1, waiting for transfers between devices, local(): layer_out = moved(layer_out)  21.2 us
    pallas_call x4, Pallas kernels, kernel_call(): pl.pallas_call(kernel, out_shape=tuple((pltpu.VMEM(shape, dtype) for shap...  17.8 us
    all_to_all x2, starting transfers between devices, all_to_all(): return lax.all_to_all(pieces, axes, split_axis=0, concat_axis=0, tiled=True)  6.53 us
    gather x1, local copies, waits for them, and re-layouts, local(): rows = item_table[jnp.maximum(wanted, 0)]  6.24 us
    pallas_call x1, Pallas kernels, local(): pl.pallas_call(table_kernel, out_shape=jax.ShapeDtypeStruct((rows_dev, wi...  6.04 us
    ppermute x1, starting transfers between devices, local(): cot = moved(out_cotangent[0])  4.57 us
  transfers between devices with their start and end apart: 4, of which 2 were waited for; matrix products, arithmetic and copies ran while one was open for 0% of the time, Pallas kernels for 0%

commit v1 on v0

v1 whole, which is shorter than its diff:
```python
import functools
import math

import jax
import jax.numpy as jnp
from jax import lax
from jax.experimental import pallas as pl
from jax.experimental.pallas import tpu as pltpu
from jax.sharding import Mesh, PartitionSpec as P

HEADS = 8
eps_norm = 1e-05
LANES = 128
ALL = ("a", "b", "c", "d")
GROUP = ("b", "d")
SWAPPED = ("b", "c")
f32 = jnp.float32
bf16 = jnp.bfloat16
i32 = jnp.int32


def vmem():
    return pl.BlockSpec(memory_space=pltpu.VMEM)


def smem():
    return pl.BlockSpec(memory_space=pltpu.SMEM)


def params():
    return pltpu.CompilerParams(vmem_limit_bytes=24 * 1024 * 1024)


def near(array):
    return pltpu.with_memory_space_constraint(array, pltpu.VMEM)


def far(array):
    return pltpu.with_memory_space_constraint(array, pltpu.HBM)


def hbm():
    return pl.BlockSpec(memory_space=pltpu.HBM)


def kernel_call(kernel, outs, args, scratch=()):
    return pl.pallas_call(
        kernel,
        out_shape=tuple(pltpu.VMEM(shape, dtype) for shape, dtype in outs),
        in_specs=[vmem()] * len(args),
        out_specs=tuple(vmem() for unused in outs),
        scratch_shapes=list(scratch),
        compiler_params=params(),
    )(*map(near, args))


def dot(lhs, rhs, dims=((1,), (0,))):
    return lax.dot_general(lhs, rhs, (dims, ((), ())), preferred_element_type=f32)


def iota(shape, axis):
    return lax.broadcasted_iota(i32, shape, axis)


def to_col(row):
    size = row.shape[1]
    same = iota((size, size), 0) == iota((size, size), 1)
    return jnp.sum(jnp.where(same, row, 0.0), axis=1, keepdims=True)


def to_row(col):
    size = col.shape[0]
    same = iota((size, size), 0) == iota((size, size), 1)
    return jnp.sum(jnp.where(same, col, 0.0), axis=0, keepdims=True)


def request_kernel(
    rows_dev,
    cap,
    first_s,
    twin_s,
    length_s,
    ids_hbm,
    place_hbm,
    mail_ref,
    ids_s,
    ids_ref,
    place_ref,
    rows_scr,
    sems,
):
    count = ids_ref.shape[1]
    copies = [
        pltpu.make_async_copy(source, target, sems.at[n])
        for n, (source, target) in enumerate(
            [(place_hbm, place_ref), (ids_hbm, ids_s), (ids_hbm, ids_ref)]
        )
    ]
    for copy in copies:
        copy.start()
    for copy in copies:
        copy.wait()

    def fetch(step, unused):
        rows_scr[pl.ds(step, 1), :] = place_ref[pl.ds(ids_s[0, step] >> 7, 1), :]
        return unused

    lax.fori_loop(0, count, fetch, 0, unroll=8)
    lane_col = to_col((ids_ref[...] & (LANES - 1)).astype(f32)).astype(i32)
    lanes = iota((count, LANES), 1)
    stored = jnp.sum(
        jnp.where(lanes == lane_col, rows_scr[...].astype(f32), 0.0), axis=1, keepdims=True
    ).astype(i32)
    shift = rows_dev.bit_length() - 1
    owner = stored >> shift
    local_row = stored & (rows_dev - 1)
    hits = lanes == owner
    hits_f = jnp.where(hits, 1.0, 0.0)
    before = jnp.where(iota((count, count), 1) < iota((count, count), 0), 1.0, 0.0)
    earlier = dot(before.astype(bf16), hits_f.astype(bf16))
    rank = jnp.sum(jnp.where(hits, earlier, 0.0), axis=1, keepdims=True)
    in_rank = lanes == rank.astype(i32)
    asked = local_row + 1
    high = jnp.where(in_rank, (asked >> 7).astype(f32), 0.0).astype(bf16)
    low = jnp.where(in_rank, (asked & 127).astype(f32), 0.0).astype(bf16)
    hits_t = hits_f.T.astype(bf16)
    owners = mail_ref.shape[0]
    wish = dot(hits_t, high) * 128.0 + dot(hits_t, low)
    mail_ref[:, :LANES] = wish[:owners].astype(i32) - 1
    slot = owner.astype(f32) * cap + rank
    live = (first_s[0] + iota((1, count), 1)) < length_s[0]
    note = to_row(slot).astype(i32) * 2 + jnp.where(live, 1, 0)
    mail_ref[:, LANES:] = jnp.where(iota((owners, count), 0) == twin_s[0], note, 0)


def read_note(mail_ref):
    note = jnp.sum(mail_ref[:, LANES:].astype(f32), axis=0, keepdims=True).astype(i32)
    return note >> 1, (note & 1).astype(f32)


def normalize(inputs):
    centred = inputs - jnp.mean(inputs, axis=-1, keepdims=True)
    spread = jnp.sqrt(jnp.mean(centred * centred, axis=-1, keepdims=True) + eps_norm)
    return (centred / spread, spread)


def project_kernel(
    mail_ref, rows_ref, cot_ref, w_ref, wo_ref, send_ref, emb_ref, slope_ref, gate_ref, mgrad_ref
):
    slot_row, live_row = read_note(mail_ref)
    count = slot_row.shape[1]
    slots, width = rows_ref.shape
    head = width // HEADS
    slot_col = to_col(slot_row.astype(f32)).astype(i32)
    live_col = to_col(live_row)
    picks = jnp.where(iota((count, slots), 1) == slot_col, 1.0, 0.0).astype(bf16)
    embedded = dot(picks, rows_ref[...])
    emb_ref[...] = embedded.astype(bf16)
    normed, _ = normalize(embedded)
    pre = dot(normed.astype(bf16), w_ref[...])
    cot = jnp.where(live_col > 0.0, cot_ref[...].astype(f32), 0.0).astype(bf16)
    mgrad = dot(cot, wo_ref[...], ((1,), (1,)))
    mgrad_ref[...] = mgrad
    half = 0.5 * pre
    tanh = jnp.tanh(half)
    twice_sig = 1.0 + tanh
    act = half * twice_sig
    slope_ref[...] = 0.5 * (twice_sig + act * (1.0 - tanh))
    gate = act[:, :width]
    gate_ref[...] = gate
    dz = mgrad * gate
    for h in range(HEADS):
        lo = h * head
        send_ref[h] = jnp.concatenate(
            [
                act[:, 2 * width + lo : 2 * width + lo + head],
                act[:, 3 * width + lo : 3 * width + lo + head],
                act[:, width + lo : width + lo + head],
                dz[:, lo : lo + head],
            ],
            axis=1,
        ).astype(bf16)


def weight_tile(keys, half_queries_t):
    half = dot(keys, half_queries_t)
    tanh = jnp.tanh(half)
    twice_sig = 1.0 + tanh
    wgt = half * twice_sig
    return wgt, twice_sig + wgt * (1.0 - tanh)


def causal_mask(rows):
    return iota((rows, rows), 0) <= iota((rows, rows), 1)


def forward_kernel(ready, x_ref, att_ref, dz_ref, share_ref, *refs):
    if ready:
        wgt_ref, slope_ref = refs[:2]
    vt_scr, stat_ref = refs[-2:]
    blocks, rows, cols = x_ref.shape
    head = cols // 4
    scale = head ** (-0.5)
    causal = causal_mask(rows)
    place = 0
    for b in range(blocks):
        queries_t = (x_ref[b, :, 0:head].astype(f32) * (0.5 * scale)).T.astype(bf16)
        vt_scr[b] = x_ref[b, :, 2 * head : 3 * head].astype(f32).T.astype(bf16)
        att = jnp.zeros((head, rows), f32)
        for c in range(b + 1):
            wgt, slope = weight_tile(x_ref[c, :, head : 2 * head], queries_t)
            if b == c:
                wgt = jnp.where(causal, wgt, 0.0)
                slope = jnp.where(causal, slope, 0.0)
            wgt = wgt.astype(bf16)
            att = att + dot(vt_scr[c], wgt)
            if ready:
                wgt_ref[place] = wgt
                slope_ref[place] = slope
            place += 1
        dz = x_ref[b, :, 3 * head :].astype(f32).T
        att_ref[b] = att
        dz_ref[b] = dz
        mean = jnp.sum(att, axis=0, keepdims=True) * (1.0 / head)
        cent = att - mean
        stat_ref[0, b : b + 1, :] = mean
        stat_ref[1, b : b + 1, :] = jnp.sum(cent * cent, axis=0, keepdims=True)
        stat_ref[2, b : b + 1, :] = jnp.sum(dz, axis=0, keepdims=True)
        stat_ref[3, b : b + 1, :] = jnp.sum(cent * dz, axis=0, keepdims=True)
    mean = stat_ref[0]
    high = mean.astype(bf16)
    low = (mean - high.astype(f32)).astype(bf16)
    others = [stat_ref[n].astype(bf16) for n in range(1, 4)]
    for g in range(blocks):
        for n, stat in enumerate([high, low] + others):
            share_ref[g, n] = stat


def backward_kernel(copies, ready, *refs):
    if ready:
        x_ref, wgt_ref, slope_ref, att_ref, dz_ref, stats_ref, out_ref = refs[:7]
        dq_scr, da_scr, dat_scr, q_scr = refs[7:]
    else:
        x_ref, att_ref, dz_ref, stats_ref, out_ref = refs[:5]
        dq_scr, da_scr, dat_scr, q_scr, qt_scr = refs[5:]
    blocks, rows, cols = x_ref.shape
    head = cols // 4
    scale = head ** (-0.5)
    width = head * HEADS
    heads = range(0, HEADS * copies, copies)

    def stat_of(h, n):
        return stats_ref[h, n].astype(f32)

    means = {h: stat_of(h, 0) + stat_of(h, 1) for h in heads}
    mean = sum(means.values()) * (1.0 / HEADS)
    square = 0.0
    dz_sum = 0.0
    dz_att = 0.0
    for h in heads:
        off = means[h] - mean
        square = square + (stat_of(h, 2) + head * (off * off))
        dz_sum = dz_sum + stat_of(h, 3)
        dz_att = dz_att + (stat_of(h, 4) + stat_of(h, 3) * off)
    inv = 1.0 / jnp.sqrt(square * (1.0 / width) + eps_norm)
    mean_dz = dz_sum * (1.0 / width)
    mean_prod = dz_att * inv * (1.0 / width)
    for b in range(blocks):
        att_n = (att_ref[b] - mean[b : b + 1]) * inv[b : b + 1]
        da_t = (dz_ref[b] - mean_dz[b : b + 1] - att_n * mean_prod[b : b + 1]) * inv[b : b + 1]
        out_ref[b, :, 3 * head :] = att_n.T.astype(bf16)
        dat_scr[b] = (0.5 * da_t).astype(bf16)
        da_scr[b] = da_t.T.astype(bf16)
        q = x_ref[b, :, 0:head].astype(f32) * scale
        q_scr[b] = q.astype(bf16)
        if not ready:
            qt_scr[b] = (0.5 * q).T.astype(bf16)
    causal = causal_mask(rows)
    for c in range(blocks):
        keys = x_ref[c, :, head : 2 * head]
        keys_t = keys.astype(f32).T.astype(bf16)
        values = x_ref[c, :, 2 * head : 3 * head]
        dk = jnp.zeros((rows, head), f32)
        dv = jnp.zeros((rows, head), f32)
        for b in range(c, blocks):
            if ready:
                place = b * (b + 1) // 2 + c
                wgt = wgt_ref[place]
                slope = slope_ref[place]
            else:
                wgt, slope = weight_tile(keys, qt_scr[b])
                if b == c:
                    wgt = jnp.where(causal, wgt, 0.0)
                    slope = jnp.where(causal, slope, 0.0)
                wgt = wgt.astype(bf16)
            sgrad = (dot(values, dat_scr[b]) * slope).astype(bf16)
            dv = dv + dot(wgt, da_scr[b])
            dk = dk + dot(sgrad, q_scr[b])
            part = dot(keys_t, sgrad)
            if c == 0:
                dq_scr[b] = part
            else:
                dq_scr[b] = dq_scr[b] + part
        out_ref[c, :, head : 2 * head] = dk.astype(bf16)
        out_ref[c, :, 2 * head : 3 * head] = dv.astype(bf16)
        out_ref[c, :, 0:head] = (dq_scr[c] * scale).T.astype(bf16)


def head_columns(grad_ref, copies, part, head):
    return jnp.concatenate(
        [
            grad_ref[h * copies, :, part * head : (part + 1) * head].astype(f32)
            for h in range(HEADS)
        ],
        axis=1,
    )


def finish_kernel(
    copies,
    mail_ref,
    grad_ref,
    slope_ref,
    gate_ref,
    mgrad_ref,
    emb_ref,
    cot_ref,
    w_ref,
    wo_ref,
    out_ref,
    layer_ref,
):
    slot_row, live_row = read_note(mail_ref)
    count, width = emb_ref.shape
    slots = out_ref.shape[0]
    head = width // HEADS
    live_col = to_col(live_row)
    columns = functools.partial(head_columns, grad_ref, copies, head=head)
    att_n = columns(3)
    mixed = (att_n * gate_ref[...]).astype(bf16)
    branch = dot(mixed, wo_ref[...])
    embedded = emb_ref[...].astype(f32)
    layer_ref[...] = (live_col * (embedded + branch)).astype(bf16)
    act_grad = jnp.concatenate(
        [mgrad_ref[...] * att_n, columns(2), columns(0), columns(1)], axis=1
    )
    pre_grad = (act_grad * slope_ref[...]).astype(bf16)
    norm_grad = dot(pre_grad, w_ref[...], ((1,), (1,)))
    normed, spread = normalize(embedded)
    mean_grad = jnp.mean(norm_grad, axis=-1, keepdims=True)
    mean_prod = jnp.mean(norm_grad * normed, axis=-1, keepdims=True)
    cot = jnp.where(live_col > 0.0, cot_ref[...].astype(f32), 0.0)
    emb_grad = cot + (norm_grad - mean_grad - normed * mean_prod) / spread
    places = jnp.where(iota((slots, count), 0) == slot_row, 1.0, 0.0).astype(bf16)
    out_ref[...] = dot(places, emb_grad.astype(bf16)).astype(bf16)


def pick_kernel(
    cap, part, askers, mail_ref, table_hbm, out_ref, table_ref, lane_scr, block_scr, sems
):
    chunks, chunk, width = table_ref.shape
    slots = out_ref.shape[0]

    def fetch(n):
        return pltpu.make_async_copy(
            table_hbm.at[pl.ds(n * chunk, chunk), :], table_ref.at[n], sems.at[n]
        )

    for n in range(chunks):
        fetch(n).start()
    wish = mail_ref[:, :LANES].astype(f32).T
    for taker, asker in enumerate(askers):
        column = jnp.maximum(wish[:cap, asker : asker + 1], 0.0)
        block = jnp.floor(column * (1.0 / part))
        place = slice(taker * cap, (taker + 1) * cap)
        block_scr[place, :] = jnp.broadcast_to(block, (cap, part))
        lane_scr[place, :] = jnp.broadcast_to(column - block * part, (cap, part))
    block = block_scr[...].astype(bf16)
    ramp = iota((slots, part), 1).astype(f32).astype(bf16)
    one = jnp.ones((), bf16)
    zero = jnp.zeros((), bf16)
    lanes = jnp.where(lane_scr[...].astype(bf16) == ramp, one, zero)
    total = jnp.zeros((slots, width), f32)
    for n in range(chunks):
        fetch(n).wait()
        for m in range(chunk // part):
            picks = jnp.where(block == n * (chunk // part) + m, lanes, zero)
            total = total + dot(picks, table_ref[n, m * part : (m + 1) * part, :])
    out_ref[...] = total.astype(bf16)


def table_kernel(part, asked_ref, arrived_ref, layer_ref, out_ref, copy_ref, picks_scr):
    rows = out_ref.shape[0]
    slots = arrived_ref.shape[0]

    @pl.when(pl.program_id(0) == 0)
    def unused():
        copy_ref[...] = layer_ref[...]

    local_row = asked_ref[...] - pl.program_id(0) * rows
    ramp = iota((part, slots), 0).astype(f32).astype(bf16)
    for start in range(0, rows, part):
        near_row = local_row - start
        inside = (near_row >= 0) & (near_row < part)
        near_row = jnp.where(inside, near_row, -1).astype(f32)
        near_row = jnp.broadcast_to(near_row, (16, slots)).astype(bf16)[0:1]
        picks = jnp.where(ramp == near_row, jnp.ones((), bf16), jnp.zeros((), bf16))
        picks_scr[start : start + part, :] = picks
    out_ref[...] = dot(picks_scr[...], arrived_ref[...]).astype(bf16)


def all_to_all(pieces, axes):
    return lax.all_to_all(pieces, axes, split_axis=0, concat_axis=0, tiled=True)


def local(item_ids, history_len, row_place, item_table, input_proj, output_proj, out_cotangent):
    count = item_ids.shape[1]
    rows_dev, width = item_table.shape
    outer = lax.axis_size("a")
    inner = lax.axis_size("d")
    owners = 4 * outer * inner
    group = 2 * inner
    copies = group // HEADS
    cap = 3 * count // owners
    slots = owners * cap
    head = width // HEADS
    part = math.gcd(rows_dev, 256)
    moved = functools.partial(
        lax.ppermute, axis_name=SWAPPED, perm=[(0, 0), (1, 2), (2, 1), (3, 3)]
    )
    askers = tuple(
        ((a * 2 + c) * 2 + b) * inner + d
        for a in range(outer)
        for b in range(2)
        for c in range(2)
        for d in range(inner)
    )
    at_a, at_b, at_c, at_d = (lax.axis_index(name) for name in ALL)

    def number(value):
        return value.reshape(1).astype(i32)

    def swapped(pieces):
        shape = pieces.shape
        parts = pieces.reshape((outer, 2, 2, inner) + shape[1:])
        return jnp.swapaxes(parts, 1, 2).reshape(shape)

    cot = moved(out_cotangent[0])
    mail = pl.pallas_call(
        functools.partial(request_kernel, rows_dev, cap),
        out_shape=pltpu.VMEM((owners, LANES + count), i32),
        in_specs=[smem()] * 3 + [hbm()] * 2,
        out_specs=vmem(),
        scratch_shapes=[
            pltpu.SMEM((1, count), i32),
            pltpu.VMEM((1, count), i32),
            pltpu.VMEM((row_place.shape[0] // LANES, LANES), i32),
            pltpu.VMEM((count, LANES), i32),
            pltpu.SemaphoreType.DMA((3,)),
        ],
        compiler_params=params(),
        name="requests",
    )(
        number((at_c * inner + at_d) * count),
        number(((at_a * 2 + at_c) * 2 + at_b) * inner + at_d),
        history_len,
        far(item_ids),
        far(row_place.reshape(-1, LANES)),
    )
    mail = all_to_all(mail, ALL)
    wanted = swapped(mail[:, :cap]).reshape(1, slots)
    chunks = min(4, rows_dev // part)
    rows = pl.pallas_call(
        functools.partial(pick_kernel, cap, part, askers),
        out_shape=pltpu.VMEM((slots, width), bf16),
        in_specs=[vmem(), hbm()],
        out_specs=vmem(),
        scratch_shapes=[
            pltpu.VMEM((chunks, rows_dev // chunks, width), bf16),
            pltpu.VMEM((slots, part), f32),
            pltpu.VMEM((slots, part), f32),
            pltpu.SemaphoreType.DMA((chunks,)),
        ],
        compiler_params=params(),
        name="pick",
    )(near(mail), far(item_table))
    rows = all_to_all(rows.reshape(owners, cap, width), ALL).reshape(slots, width)

    send, emb, slope, gate, mgrad = kernel_call(
        project_kernel,
        (
            ((HEADS, count, 4 * head), bf16),
            ((count, width), bf16),
            ((count, 4 * width), f32),
            ((count, width), f32),
            ((count, width), f32),
        ),
        (mail, rows, cot, input_proj, output_proj),
    )
    if copies > 1:
        send = jnp.repeat(send, copies, axis=0)
    mine = all_to_all(send, GROUP)
    tiles = group * (group + 1) // 2
    ready = tiles * count * count * 6 <= 16 * 1024 * 1024
    att, dz, share, *weights = kernel_call(
        functools.partial(forward_kernel, ready),
        (
            ((group, head, count), f32),
            ((group, head, count), f32),
            ((group, 5, group, count), bf16),
        )
        + (((tiles, count, count), bf16), ((tiles, count, count), f32)) * ready,
        (mine,),
        scratch=[
            pltpu.VMEM((group, head, count), bf16),
            pltpu.VMEM((4, group, count), f32),
        ],
    )
    stats = all_to_all(share, GROUP)
    scratch = [
        pltpu.VMEM((group, head, count), f32),
        pltpu.VMEM((group, count, head), bf16),
        pltpu.VMEM((group, head, count), bf16),
        pltpu.VMEM((group, count, head), bf16),
    ]
    if not ready:
        scratch.append(pltpu.VMEM((group, head, count), bf16))
    (grads,) = kernel_call(
        functools.partial(backward_kernel, copies, ready),
        (((group, count, 4 * head), bf16),),
        (mine, *weights, att, dz, stats),
        scratch=scratch,
    )
    back = all_to_all(grads, GROUP)
    outgoing, layer_out = kernel_call(
        functools.partial(finish_kernel, copies),
        (((slots, width), bf16), ((count, width), bf16)),
        (mail, back, slope, gate, mgrad, emb, cot, input_proj, output_proj),
    )
    arrived = all_to_all(outgoing.reshape(owners, cap, width), ALL).reshape(slots, width)
    layer_out = moved(layer_out)
    tile = math.gcd(rows_dev, 1024)
    table_grad, layer_out = pl.pallas_call(
        functools.partial(table_kernel, part),
        out_shape=(
            jax.ShapeDtypeStruct((rows_dev, width), bf16),
            jax.ShapeDtypeStruct((count, width), bf16),
        ),
        grid=(rows_dev // tile,),
        in_specs=[vmem(), vmem(), vmem()],
        out_specs=(
            pl.BlockSpec((tile, width), lambda r: (r, 0)),
            pl.BlockSpec((count, width), lambda r: (0, 0)),
        ),
        scratch_shapes=[pltpu.VMEM((tile, slots), bf16)],
        compiler_params=params(),
        name="table_grad",
    )(near(wanted), near(arrived), near(layer_out))
    return (layer_out[None], table_grad)


def solution(mesh):
    table, seq = mesh.shape["table"], mesh.shape["seq"]
    if table % 2 or seq % 2 or seq % HEADS:
        raise ValueError("unsupported mesh")
    finer = Mesh(mesh.devices.reshape(table // 2, 2, 2, seq // 2), ALL)
    placed = (
        P(("a", "b"), ("c", "d")),
        P(("a", "b")),
        P(),
        P(ALL, None),
        P(),
        P(),
        P(("a", "b"), ("c", "d"), None),
    )

    return jax.shard_map(
        local,
        mesh=finer,
        in_specs=placed,
        out_specs=(P(("a", "b"), ("c", "d"), None), P(ALL, None)),
        check_vma=False,
    )
```

time: 152 us -> 146 us (0.961)
  local copies, waits for them, and re-layouts: 8.94 us -> 2.69 us
    gather x1 -> x0, local copies, waits for them, and re-layouts: 6.24 us -> none  [local(): rows = item_table[jnp.maximum(wanted, 0)]]
    pallas_call x1 -> x2, Pallas kernels: 6.04 us -> 9.77 us  [the longest x1 4.94 us: local(): pl.pallas_call(functools.partial(table_kernel, part), out_shape=(jax.Shap...]
    pallas_call x4, Pallas kernels: 17.8 us -> 15 us  [kernel_call(): pl.pallas_call(kernel, out_shape=tuple((pltpu.VMEM(shape, dtype) for shap...]
where the time goes in v1:
time: 146 us
  blocking collectives  56.7 us (39%)
  waiting for transfers between devices  42.5 us (29%)
  Pallas kernels  26.9 us (18%)
  starting transfers between devices  15.2 us (10%)
  local copies, waits for them, and re-layouts  2.69 us (2%)
  between operations  1.57 us (1%)
    all_to_all x4, blocking collectives, all_to_all(): return lax.all_to_all(pieces, axes, split_axis=0, concat_axis=0, tiled=True)  56.7 us
    ppermute x1, waiting for transfers between devices, local(): cot = moved(out_cotangent[0])  21.3 us
    ppermute x1, waiting for transfers between devices, local(): layer_out = moved(layer_out)  21.2 us
    pallas_call x4, Pallas kernels, kernel_call(): pl.pallas_call(kernel, out_shape=tuple((pltpu.VMEM(shape, dtype) for shap...  15 us
    all_to_all x2, starting transfers between devices, all_to_all(): return lax.all_to_all(pieces, axes, split_axis=0, concat_axis=0, tiled=True)  6.23 us
    pallas_call x1, Pallas kernels, local(): pl.pallas_call(functools.partial(table_kernel, part), out_shape=(jax.Shap...  4.94 us
    pallas_call x1, Pallas kernels, local(): pl.pallas_call(functools.partial(pick_kernel, cap, part, askers), out_sha...  4.82 us
    ppermute x1, starting transfers between devices, local(): cot = moved(out_cotangent[0])  4.57 us
  transfers between devices with their start and end apart: 4, of which 2 were waited for; matrix products, arithmetic and copies ran while one was open for 0% of the time, Pallas kernels for 0%

profile of v1, /device:TPU:1, one launch (start us, length us, event | category | flops | bytes accessed | tf_op | source)
XLA Modules:
  0.0 145.7 jit_solution(11507555554378237785)
XLA Ops:
  0.6 0.0 copy-start
  0.6 0.0 copy-start.2
  1.5 2.2 %requests.1 = s32[32,384]{1,0:T(8,128)S(1)} custom-call(s32[1]{0:T(128)} %bitcast.first_s, s32[1]{0:T(128)} %bitcast.1.twin_s, s32[1]{0:T(128)S(6)} %copy.17.length_s, s32[1,256]{1,0:T(1,128)} %ids_hbm.1, s32[1024,128]{1,0:T(8,128)} %bitcast.25), custom_call_target="tpu_custom_call" | custom-call | tf_op jit(solution)/shard_map/requests/pallas_call | solution.py:449
  3.6 0.1 copy.10
  3.7 14.0 %all_to_all.36 = s32[32,1,384]{2,1,0:T(1,128)S(1)} all-to-all(s32[32,1,384]{2,1,0:T(1,128)S(1)} %copy.10), channel_id=1, replica_groups=mesh['a'=2,'b'=2,'c'=2,'d'=4] {'a','b','c','d'}, dimensions={0} | all-to-all | bytes 98304 | tf_op jit(solution)/shard_map/all_to_all | solution.py:413
  17.7 4.8 %pick.1 = bf16[768,512]{1,0:T(8,128)(2,1)S(1)} custom-call(s32[32,384]{1,0:T(8,128)S(1)} %bitcast.20, bf16[4096,512]{1,0:T(8,128)(2,1)} %table_hbm.1), custom_call_target="tpu_custom_call" | custom-call | tf_op jit(solution)/shard_map/pick/pallas_call | solution.py:473
  22.5 0.0 copy-start.1
  22.5 0.9 copy-done.1
  23.4 2.6 %all-to-all-start.1 = ((bf16[32,24,512]{2,1,0:T(8,128)(2,1)}), bf16[32,24,512]{2,1,0:T(8,128)(2,1)S(1)}, u32[]{:S(2)}, u32[]{:S(2)}) async-start(bf16[32,24,512]{2,1,0:T(8,128)(2,1)} %bitcast.18), calls=%async_computation.1 | async-start | bytes 1572864 | tf_op jit(solution)/shard_map/all_to_all | solution.py:413
  26.0 4.6 %collective-permute-start = (bf16[256,512]{1,0:T(8,128)(2,1)}, bf16[256,512]{1,0:T(8,128)(2,1)S(1)}, u32[]{:S(2)}, u32[]{:S(2)}) collective-permute-start(bf16[256,512]{1,0:T(8,128)(2,1)} %bitcast.28), channel_id=1, source_target_pairs={{0,0},{4,8},{8,4},{12,12},{1,1},{5,9},{9,5},{13,13},{2,2},{6,10},{... | collective-permute-start | bytes 786440 | tf_op jit(solution)/shard_map/ppermute | solution.py:448
  30.6 21.3 %collective-permute-done.cot_ref = bf16[256,512]{1,0:T(8,128)(2,1)S(1)} collective-permute-done((bf16[256,512]{1,0:T(8,128)(2,1)}, bf16[256,512]{1,0:T(8,128)(2,1)S(1)}, u32[]{:S(2)}, u32[]{:S(2)}) %collective-permute-start) | collective-permute-done | bytes 262176 | tf_op jit(solution)/shard_map/ppermute | solution.py:448
  51.9 0.0 copy-start.3
  51.9 0.7 copy-done.3
  52.6 0.0 all-to-all-done.1
  52.6 0.0 copy-done
  52.6 0.0 copy-done.2
  52.7 0.0 copy-start.4
  52.7 0.9 copy-done.4
  53.6 1.9 %shard_map.86 = (bf16[8,256,256]{2,1,0:T(8,128)(2,1)S(1)}, bf16[256,512]{1,0:T(8,128)(2,1)S(1)}, f32[256,2048]{1,0:T(8,128)S(1)}, f32[256,512]{1,0:T(8,128)S(1)}, f32[256,512]{1,0:T(8,128)S(1)}) custom-call(s32[32,384]{1,0:T(8,128)S(1)} %bitcast.21, bf16[768,512]{1,0:T(8,128)(2,1)S(1)} %bitcast.17, bf16[256,512]{1,0:T(8,128)(2,1)S(1)} %copy-done.4, ...), custom_call_target="tpu_custom_call" | custom-call | tf_op jit(solution)/shard_map/pallas_call | solution.py:47
  55.5 17.3 %all_to_all.37.x_ref.refs_0_ = bf16[8,256,256]{2,1,0:T(8,128)(2,1)S(1)} all-to-all(bf16[8,256,256]{2,1,0:T(8,128)(2,1)S(1)} %get-tuple-element.16), channel_id=1, replica_groups=mesh['a'=2,'b'=2,'c'=2,'d'=4] {'b','d'}, dimensions={0} | all-to-all | bytes 2097152 | tf_op jit(solution)/shard_map/all_to_all | solution.py:413
  72.8 4.2 %shard_map.87 = (f32[8,64,256]{2,1,0:T(8,128)S(1)}, f32[8,64,256]{2,1,0:T(8,128)S(1)}, bf16[8,5,8,256]{3,2,1,0:T(8,128)(2,1)S(1)}, bf16[36,256,256]{2,1,0:T(8,128)(2,1)S(1)}, f32[36,256,256]{2,1,0:T(8,128)S(1)}) custom-call(bf16[8,256,256]{2,1,0:T(8,128)(2,1)S(1)} %all_to_all.37.x_ref.refs_0_), custom_call_target="tpu_custom_call" | custom-call | tf_op jit(solution)/shard_map/pallas_call | solution.py:47
  77.0 8.0 %all_to_all.38.refs_5_ = bf16[8,5,8,256]{3,2,1,0:T(8,128)(2,1)S(1)} all-to-all(bf16[8,5,8,256]{3,2,1,0:T(8,128)(2,1)S(1)} %get-tuple-element.21), channel_id=1, replica_groups=mesh['a'=2,'b'=2,'c'=2,'d'=4] {'b','d'}, dimensions={0} | all-to-all | bytes 327680 | tf_op jit(solution)/shard_map/all_to_all | solution.py:413
  85.0 0.0 copy-start.5
  85.0 6.4 %shard_map.88 = bf16[8,256,256]{2,1,0:T(8,128)(2,1)S(1)} custom-call(bf16[8,256,256]{2,1,0:T(8,128)(2,1)S(1)} %all_to_all.37.x_ref.refs_0_, bf16[36,256,256]{2,1,0:T(8,128)(2,1)S(1)} %get-tuple-element.17.refs_1_, f32[36,256,256]{2,1,0:T(8,128)S(1)} %get-tuple-element.18.refs_2_, f32[8,64,256]{2,1,0:T(8,128)S(1)} %get-tuple-element.19.refs_3_, ...), custom_call_target="tpu_custom_call" | custom-call | tf_op jit(solution)/shard_map/pallas_call | solution.py:47
  91.4 17.5 %all_to_all.39.grad_ref = bf16[8,256,256]{2,1,0:T(8,128)(2,1)S(1)} all-to-all(bf16[8,256,256]{2,1,0:T(8,128)(2,1)S(1)} %shard_map.88), channel_id=1, replica_groups=mesh['a'=2,'b'=2,'c'=2,'d'=4] {'b','d'}, dimensions={0} | all-to-all | bytes 2097152 | tf_op jit(solution)/shard_map/all_to_all | solution.py:413
  108.9 0.0 copy-done.5
  108.9 2.5 %shard_map.89 = (bf16[768,512]{1,0:T(8,128)(2,1)}, bf16[256,512]{1,0:T(8,128)(2,1)S(1)}) custom-call(s32[32,384]{1,0:T(8,128)S(1)} %bitcast.22, bf16[8,256,256]{2,1,0:T(8,128)(2,1)S(1)} %all_to_all.39.grad_ref, f32[256,2048]{1,0:T(8,128)S(1)} %get-tuple-element.22.slope_ref, f32[256,512]{1,0:T(8,128)S(1)} %get-tuple-element.23.gate_ref, ...), custom_call_target="tpu_custom_call" | custom-call | tf_op jit(solution)/shard_map/pallas_call | solution.py:47
  111.4 3.6 %all-to-all-start.5 = ((bf16[32,24,512]{2,1,0:T(8,128)(2,1)}), bf16[32,24,512]{2,1,0:T(8,128)(2,1)S(1)}, u32[]{:S(2)}, u32[]{:S(2)}) async-start(bf16[32,24,512]{2,1,0:T(8,128)(2,1)} %bitcast.9), calls=%async_computation.5 | async-start | bytes 1572864 | tf_op jit(solution)/shard_map/all_to_all | solution.py:413
  115.0 4.4 %collective-permute-start.1 = (bf16[256,512]{1,0:T(8,128)(2,1)S(1)}, bf16[256,512]{1,0:T(8,128)(2,1)S(1)}, u32[]{:S(2)}, u32[]{:S(2)}) collective-permute-start(bf16[256,512]{1,0:T(8,128)(2,1)S(1)} %get-tuple-element.27), channel_id=1, source_target_pairs={{0,0},{4,8},{8,4},{12,12},{1,1},{5,9},{9,5},{13,13},{2,2},{6,10},{... | collective-permute-start | bytes 786440 | tf_op jit(solution)/shard_map/ppermute | solution.py:541
  119.4 0.1 reshape_reshape.3.asked_ref
  119.5 21.2 %collective-permute-done.1.layer_ref = bf16[256,512]{1,0:T(8,128)(2,1)S(1)} collective-permute-done((bf16[256,512]{1,0:T(8,128)(2,1)S(1)}, bf16[256,512]{1,0:T(8,128)(2,1)S(1)}, u32[]{:S(2)}, u32[]{:S(2)}) %collective-permute-start.1) | collective-permute-done | bytes 262176 | tf_op jit(solution)/shard_map/ppermute | solution.py:541
  140.7 0.0 all-to-all-done.5
  140.7 4.9 %table_grad.1 = (bf16[4096,512]{1,0:T(8,128)(2,1)}, bf16[256,512]{1,0:T(8,128)(2,1)}) custom-call(s32[1,768]{1,0:T(1,128)S(1)} %reshape_reshape.3.asked_ref, bf16[768,512]{1,0:T(8,128)(2,1)S(1)} %bitcast.19, bf16[256,512]{1,0:T(8,128)(2,1)S(1)} %collective-permute-done.1.layer_ref), custom_call_target="tpu_custom_call" | custom-call | tf_op jit(solution)/shard_map/table_grad/pallas_call | solution.py:543
  (3 shorter events, 0.0 us)
Async XLA Ops:
  0.6 52.0 %copy-start = (bf16[512,2048]{1,0:T(8,128)(2,1)S(1)}, bf16[512,2048]{1,0:T(8,128)(2,1)}, u32[]{:S(2)}) copy-start(bf16[512,2048]{1,0:T(8,128)(2,1)} %w_ref.3) | copy-start | bytes 6291460
  0.6 52.0 %copy-start.2 = (bf16[512,512]{1,0:T(8,128)(2,1)S(1)}, bf16[512,512]{1,0:T(8,128)(2,1)}, u32[]{:S(2)}) copy-start(bf16[512,512]{1,0:T(8,128)(2,1)} %wo_ref.3) | copy-start | bytes 1572868
  22.5 0.9 copy-start.1
  23.4 29.2 %all-to-all-start.1 = ((bf16[32,24,512]{2,1,0:T(8,128)(2,1)}), bf16[32,24,512]{2,1,0:T(8,128)(2,1)S(1)}, u32[]{:S(2)}, u32[]{:S(2)}) async-start(bf16[32,24,512]{2,1,0:T(8,128)(2,1)} %bitcast.18), calls=%async_computation.1 | async-start | bytes 1572864 | tf_op jit(solution)/shard_map/all_to_all | solution.py:413
  26.0 25.9 %collective-permute-start = (bf16[256,512]{1,0:T(8,128)(2,1)}, bf16[256,512]{1,0:T(8,128)(2,1)S(1)}, u32[]{:S(2)}, u32[]{:S(2)}) collective-permute-start(bf16[256,512]{1,0:T(8,128)(2,1)} %bitcast.28), channel_id=1, source_target_pairs={{0,0},{4,8},{8,4},{12,12},{1,1},{5,9},{9,5},{13,13},{2,2},{6,10},{... | collective-permute-start | bytes 786440 | tf_op jit(solution)/shard_map/ppermute | solution.py:448
  51.9 0.7 copy-start.3
  52.7 1.0 copy-start.4
  85.0 23.9 %copy-start.5 = (bf16[256,512]{1,0:T(8,128)(2,1)S(1)}, bf16[256,512]{1,0:T(8,128)(2,1)}, u32[]{:S(2)}) copy-start(bf16[256,512]{1,0:T(8,128)(2,1)} %copy-done.3) | copy-start | bytes 786436
  111.4 29.4 %all-to-all-start.5 = ((bf16[32,24,512]{2,1,0:T(8,128)(2,1)}), bf16[32,24,512]{2,1,0:T(8,128)(2,1)S(1)}, u32[]{:S(2)}, u32[]{:S(2)}) async-start(bf16[32,24,512]{2,1,0:T(8,128)(2,1)} %bitcast.9), calls=%async_computation.5 | async-start | bytes 1572864 | tf_op jit(solution)/shard_map/all_to_all | solution.py:413
  115.0 25.8 %collective-permute-start.1 = (bf16[256,512]{1,0:T(8,128)(2,1)S(1)}, bf16[256,512]{1,0:T(8,128)(2,1)S(1)}, u32[]{:S(2)}, u32[]{:S(2)}) collective-permute-start(bf16[256,512]{1,0:T(8,128)(2,1)S(1)} %get-tuple-element.27), channel_id=1, source_target_pairs={{0,0},{4,8},{8,4},{12,12},{1,1},{5,9},{9,5},{13,13},{2,2},{6,10},{... | collective-permute-start | bytes 786440 | tf_op jit(solution)/shard_map/ppermute | solution.py:541

commit v2 on v1

--- a/solution.py
+++ b/solution.py
@@ -11,6 +11,7 @@
 HEADS = 8
 eps_norm = 1e-05
 LANES = 128
+TILE = 1024
 ALL = ("a", "b", "c", "d")
 GROUP = ("b", "d")
 SWAPPED = ("b", "c")
@@ -43,15 +44,15 @@
     return pl.BlockSpec(memory_space=pltpu.HBM)
 
 
-def kernel_call(kernel, outs, args, scratch=()):
+def kernel_call(kernel, outs, args, scratch=(), numbers=()):
     return pl.pallas_call(
         kernel,
         out_shape=tuple(pltpu.VMEM(shape, dtype) for shape, dtype in outs),
-        in_specs=[vmem()] * len(args),
+        in_specs=[smem()] * len(numbers) + [vmem()] * len(args),
         out_specs=tuple(vmem() for unused in outs),
         scratch_shapes=list(scratch),
         compiler_params=params(),
-    )(*map(near, args))
+    )(*numbers, *map(near, args))
 
 
 def dot(lhs, rhs, dims=((1,), (0,))):
@@ -77,12 +78,15 @@
 def request_kernel(
     rows_dev,
     cap,
-    first_s,
+    unused_s,
+    block_s,
     twin_s,
     length_s,
     ids_hbm,
     place_hbm,
+    table_hbm,
     mail_ref,
+    table_ref,
     ids_s,
     ids_ref,
     place_ref,
@@ -93,12 +97,17 @@
     copies = [
         pltpu.make_async_copy(source, target, sems.at[n])
         for n, (source, target) in enumerate(
-            [(place_hbm, place_ref), (ids_hbm, ids_s), (ids_hbm, ids_ref)]
+            [
+                (ids_hbm, ids_s),
+                (ids_hbm, ids_ref),
+                (place_hbm, place_ref),
+                (table_hbm, table_ref),
+            ]
         )
     ]
     for copy in copies:
         copy.start()
-    for copy in copies:
+    for copy in copies[:3]:
         copy.wait()
 
     def fetch(step, unused):
@@ -128,9 +137,10 @@
     wish = dot(hits_t, high) * 128.0 + dot(hits_t, low)
     mail_ref[:, :LANES] = wish[:owners].astype(i32) - 1
     slot = owner.astype(f32) * cap + rank
-    live = (first_s[0] + iota((1, count), 1)) < length_s[0]
+    live = (block_s[0] * count + iota((1, count), 1)) < length_s[0]
     note = to_row(slot).astype(i32) * 2 + jnp.where(live, 1, 0)
     mail_ref[:, LANES:] = jnp.where(iota((owners, count), 0) == twin_s[0], note, 0)
+    copies[3].wait()
 
 
 def read_note(mail_ref):
@@ -144,9 +154,20 @@
     return (centred / spread, spread)
 
 
+def hand_out(me_s, pieces, source_ref, copies=1):
+    for k, piece in enumerate(pieces):
+        piece[...] = source_ref[jnp.bitwise_xor(me_s[0], k) // copies]
+
+
+def take_in(me_s, pieces, target_ref):
+    for k, piece in enumerate(pieces):
+        target_ref[jnp.bitwise_xor(me_s[0], k)] = piece[...]
+
+
 def project_kernel(
-    mail_ref, rows_ref, cot_ref, w_ref, wo_ref, send_ref, emb_ref, slope_ref, gate_ref, mgrad_ref
+    copies, me_s, mail_ref, rows_ref, cot_ref, w_ref, wo_ref, emb_ref, slope_ref, gate_ref, mgrad_ref, *refs
 ):
+    pieces, send_ref = refs[:-1], refs[-1]
     slot_row, live_row = read_note(mail_ref)
     count = slot_row.shape[1]
     slots, width = rows_ref.shape
@@ -180,6 +201,7 @@
             ],
             axis=1,
         ).astype(bf16)
+    hand_out(me_s, pieces, send_ref, copies)
 
 
 def weight_tile(keys, half_queries_t):
@@ -194,30 +216,34 @@
     return iota((rows, rows), 0) <= iota((rows, rows), 1)
 
 
-def forward_kernel(ready, x_ref, att_ref, dz_ref, share_ref, *refs):
-    if ready:
-        wgt_ref, slope_ref = refs[:2]
-    vt_scr, stat_ref = refs[-2:]
+def forward_kernel(ready, group, me_s, *refs):
+    pieces, refs = refs[:group], refs[group:]
+    x_ref, att_ref, dz_ref, share_ref, wgt_ref = refs[:5]
+    slope_ref = refs[5] if ready else None
+    vt_scr, keys_scr, stat_ref = refs[-3:]
+    take_in(me_s, pieces, x_ref)
     blocks, rows, cols = x_ref.shape
     head = cols // 4
     scale = head ** (-0.5)
     causal = causal_mask(rows)
-    place = 0
+    for b in range(blocks):
+        span = slice(b * rows, (b + 1) * rows)
+        keys_scr[span, :] = x_ref[b, :, head : 2 * head]
+        vt_scr[:, span] = x_ref[b, :, 2 * head : 3 * head].astype(f32).T.astype(bf16)
     for b in range(blocks):
         queries_t = (x_ref[b, :, 0:head].astype(f32) * (0.5 * scale)).T.astype(bf16)
-        vt_scr[b] = x_ref[b, :, 2 * head : 3 * head].astype(f32).T.astype(bf16)
-        att = jnp.zeros((head, rows), f32)
-        for c in range(b + 1):
-            wgt, slope = weight_tile(x_ref[c, :, head : 2 * head], queries_t)
-            if b == c:
-                wgt = jnp.where(causal, wgt, 0.0)
-                slope = jnp.where(causal, slope, 0.0)
-            wgt = wgt.astype(bf16)
-            att = att + dot(vt_scr[c], wgt)
-            if ready:
-                wgt_ref[place] = wgt
-                slope_ref[place] = slope
-            place += 1
+        above = b * rows
+        upto = above + rows
+        wgt, slope = weight_tile(keys_scr[:upto, :], queries_t)
+        place = b * (b + 1) // 2 * rows
+        if above:
+            wgt_ref[place : place + above, :] = wgt[:above].astype(bf16)
+        wgt_ref[place + above : place + upto, :] = jnp.where(causal, wgt[above:], 0.0).astype(bf16)
+        if ready:
+            if above:
+                slope_ref[place : place + above, :] = slope[:above]
+            slope_ref[place + above : place + upto, :] = jnp.where(causal, slope[above:], 0.0)
+        att = dot(vt_scr[:, :upto], wgt_ref[place : place + upto, :])
         dz = x_ref[b, :, 3 * head :].astype(f32).T
         att_ref[b] = att
         dz_ref[b] = dz
@@ -236,13 +262,17 @@
             share_ref[g, n] = stat
 
 
-def backward_kernel(copies, ready, *refs):
+def backward_kernel(copies, ready, group, me_s, *refs):
     if ready:
-        x_ref, wgt_ref, slope_ref, att_ref, dz_ref, stats_ref, out_ref = refs[:7]
-        dq_scr, da_scr, dat_scr, q_scr = refs[7:]
+        x_ref, wgt_ref, slope_ref, att_ref, dz_ref, stats_ref = refs[:6]
     else:
-        x_ref, att_ref, dz_ref, stats_ref, out_ref = refs[:5]
-        dq_scr, da_scr, dat_scr, q_scr, qt_scr = refs[5:]
+        x_ref, wgt_ref, att_ref, dz_ref, stats_ref = refs[:5]
+        qt_scr = refs[-1]
+    refs = refs[5 + ready :]
+    pieces = refs[:group]
+    out_ref, da_scr, dat_scr, q_scr, keys_scr, keyst_scr, values_scr, dk_scr, dv_scr = refs[
+        group : group + 9
+    ]
     blocks, rows, cols = x_ref.shape
     head = cols // 4
     scale = head ** (-0.5)
@@ -276,34 +306,40 @@
         if not ready:
             qt_scr[b] = (0.5 * q).T.astype(bf16)
     causal = causal_mask(rows)
-    for c in range(blocks):
-        keys = x_ref[c, :, head : 2 * head]
-        keys_t = keys.astype(f32).T.astype(bf16)
-        values = x_ref[c, :, 2 * head : 3 * head]
-        dk = jnp.zeros((rows, head), f32)
-        dv = jnp.zeros((rows, head), f32)
-        for b in range(c, blocks):
-            if ready:
-                place = b * (b + 1) // 2 + c
-                wgt = wgt_ref[place]
-                slope = slope_ref[place]
-            else:
-                wgt, slope = weight_tile(keys, qt_scr[b])
-                if b == c:
-                    wgt = jnp.where(causal, wgt, 0.0)
-                    slope = jnp.where(causal, slope, 0.0)
-                wgt = wgt.astype(bf16)
-            sgrad = (dot(values, dat_scr[b]) * slope).astype(bf16)
-            dv = dv + dot(wgt, da_scr[b])
-            dk = dk + dot(sgrad, q_scr[b])
-            part = dot(keys_t, sgrad)
-            if c == 0:
-                dq_scr[b] = part
-            else:
-                dq_scr[b] = dq_scr[b] + part
-        out_ref[c, :, head : 2 * head] = dk.astype(bf16)
-        out_ref[c, :, 2 * head : 3 * head] = dv.astype(bf16)
-        out_ref[c, :, 0:head] = (dq_scr[c] * scale).T.astype(bf16)
+    for b in range(blocks):
+        span = slice(b * rows, (b + 1) * rows)
+        keys = x_ref[b, :, head : 2 * head]
+        keys_scr[span, :] = keys
+        keyst_scr[:, span] = keys.astype(f32).T.astype(bf16)
+        values_scr[span, :] = x_ref[b, :, 2 * head : 3 * head]
+    for b in range(blocks):
+        above = b * rows
+        upto = above + rows
+        place = b * (b + 1) // 2 * rows
+        wgt = wgt_ref[place : place + upto, :]
+        if ready:
+            slope = slope_ref[place : place + upto, :]
+        else:
+            _, slope = weight_tile(keys_scr[:upto, :], qt_scr[b])
+        sgrad = dot(values_scr[:upto, :], dat_scr[b]) * slope
+        if not ready:
+            mask = iota((upto, rows), 0) <= iota((upto, rows), 1) + above
+            sgrad = jnp.where(mask, sgrad, 0.0)
+        sgrad = sgrad.astype(bf16)
+        dv = dot(wgt, da_scr[b])
+        dk = dot(sgrad, q_scr[b])
+        if above:
+            dv_scr[:above, :] = dv_scr[:above, :] + dv[:above]
+            dk_scr[:above, :] = dk_scr[:above, :] + dk[:above]
+        dv_scr[above:upto, :] = dv[above:]
+        dk_scr[above:upto, :] = dk[above:]
+        dq = dot(keyst_scr[:, :upto], sgrad)
+        out_ref[b, :, 0:head] = (dq * scale).T.astype(bf16)
+    for b in range(blocks):
+        span = slice(b * rows, (b + 1) * rows)
+        out_ref[b, :, head : 2 * head] = dk_scr[span, :].astype(bf16)
+        out_ref[b, :, 2 * head : 3 * head] = dv_scr[span, :].astype(bf16)
+    hand_out(me_s, pieces, out_ref)
 
 
 def head_columns(grad_ref, copies, part, head):
@@ -316,20 +352,11 @@
     )
 
 
-def finish_kernel(
-    copies,
-    mail_ref,
-    grad_ref,
-    slope_ref,
-    gate_ref,
-    mgrad_ref,
-    emb_ref,
-    cot_ref,
-    w_ref,
-    wo_ref,
-    out_ref,
-    layer_ref,
-):
+def finish_kernel(copies, group, me_s, *refs):
+    pieces, refs = refs[:group], refs[group:]
+    mail_ref, slope_ref, gate_ref, mgrad_ref, emb_ref, cot_ref, w_ref, wo_ref = refs[:8]
+    out_ref, layer_ref, grad_ref = refs[8:]
+    take_in(me_s, pieces, grad_ref)
     slot_row, live_row = read_note(mail_ref)
     count, width = emb_ref.shape
     slots = out_ref.shape[0]
@@ -355,19 +382,9 @@
     out_ref[...] = dot(places, emb_grad.astype(bf16)).astype(bf16)
 
 
-def pick_kernel(
-    cap, part, askers, mail_ref, table_hbm, out_ref, table_ref, lane_scr, block_scr, sems
-):
-    chunks, chunk, width = table_ref.shape
+def pick_kernel(cap, part, askers, mail_ref, table_ref, out_ref, lane_scr, block_scr):
+    rows, width = table_ref.shape
     slots = out_ref.shape[0]
-
-    def fetch(n):
-        return pltpu.make_async_copy(
-            table_hbm.at[pl.ds(n * chunk, chunk), :], table_ref.at[n], sems.at[n]
-        )
-
-    for n in range(chunks):
-        fetch(n).start()
     wish = mail_ref[:, :LANES].astype(f32).T
     for taker, asker in enumerate(askers):
         column = jnp.maximum(wish[:cap, asker : asker + 1], 0.0)
@@ -381,32 +398,36 @@
     zero = jnp.zeros((), bf16)
     lanes = jnp.where(lane_scr[...].astype(bf16) == ramp, one, zero)
     total = jnp.zeros((slots, width), f32)
+    for n in range(rows // part):
+        picks = jnp.where(block == n, lanes, zero)
+        total = total + dot(picks, table_ref[n * part : (n + 1) * part, :])
+    out_ref[...] = total.astype(bf16)
+
+
+def table_kernel(part, asked_ref, arrived_ref, layer_ref, out_hbm, copy_hbm, out_scr, picks_scr, sems):
+    chunks, chunk, _ = out_scr.shape
+    slots = arrived_ref.shape[0]
+    finished = pltpu.make_async_copy(layer_ref, copy_hbm, sems.at[chunks])
+    finished.start()
+    ramp = iota((part, slots), 0).astype(f32).astype(bf16)
+    copies = []
     for n in range(chunks):
-        fetch(n).wait()
-        for m in range(chunk // part):
-            picks = jnp.where(block == n * (chunk // part) + m, lanes, zero)
-            total = total + dot(picks, table_ref[n, m * part : (m + 1) * part, :])
-    out_ref[...] = total.astype(bf16)
-
-
-def table_kernel(part, asked_ref, arrived_ref, layer_ref, out_ref, copy_ref, picks_scr):
-    rows = out_ref.shape[0]
-    slots = arrived_ref.shape[0]
-
-    @pl.when(pl.program_id(0) == 0)
-    def unused():
-        copy_ref[...] = layer_ref[...]
-
-    local_row = asked_ref[...] - pl.program_id(0) * rows
-    ramp = iota((part, slots), 0).astype(f32).astype(bf16)
-    for start in range(0, rows, part):
-        near_row = local_row - start
-        inside = (near_row >= 0) & (near_row < part)
-        near_row = jnp.where(inside, near_row, -1).astype(f32)
-        near_row = jnp.broadcast_to(near_row, (16, slots)).astype(bf16)[0:1]
-        picks = jnp.where(ramp == near_row, jnp.ones((), bf16), jnp.zeros((), bf16))
-        picks_scr[start : start + part, :] = picks
-    out_ref[...] = dot(picks_scr[...], arrived_ref[...]).astype(bf16)
+        for start in range(0, chunk, part):
+            near_row = asked_ref[...] - (n * chunk + start)
+            inside = (near_row >= 0) & (near_row < part)
+            near_row = jnp.where(inside, near_row, -1).astype(f32)
+            near_row = jnp.broadcast_to(near_row, (16, slots)).astype(bf16)[0:1]
+            picks = jnp.where(ramp == near_row, jnp.ones((), bf16), jnp.zeros((), bf16))
+            picks_scr[n % 2, start : start + part, :] = picks
+        out_scr[n] = dot(picks_scr[n % 2], arrived_ref[...]).astype(bf16)
+        copy = pltpu.make_async_copy(
+            out_scr.at[n], out_hbm.at[pl.ds(n * chunk, chunk), :], sems.at[n]
+        )
+        copy.start()
+        copies.append(copy)
+    for copy in copies:
+        copy.wait()
+    finished.wait()
 
 
 def all_to_all(pieces, axes):
@@ -440,119 +461,136 @@
     def number(value):
         return value.reshape(1).astype(i32)
 
+    me = number(at_b * inner + at_d)
+
     def swapped(pieces):
         shape = pieces.shape
         parts = pieces.reshape((outer, 2, 2, inner) + shape[1:])
         return jnp.swapaxes(parts, 1, 2).reshape(shape)
 
     cot = moved(out_cotangent[0])
-    mail = pl.pallas_call(
+    mail, table = pl.pallas_call(
         functools.partial(request_kernel, rows_dev, cap),
-        out_shape=pltpu.VMEM((owners, LANES + count), i32),
-        in_specs=[smem()] * 3 + [hbm()] * 2,
-        out_specs=vmem(),
+        out_shape=(
+            pltpu.VMEM((owners, LANES + count), i32),
+            pltpu.VMEM(item_table.shape, bf16),
+        ),
+        in_specs=[smem()] * 4 + [hbm()] * 3,
+        out_specs=(vmem(), vmem()),
         scratch_shapes=[
             pltpu.SMEM((1, count), i32),
             pltpu.VMEM((1, count), i32),
             pltpu.VMEM((row_place.shape[0] // LANES, LANES), i32),
             pltpu.VMEM((count, LANES), i32),
-            pltpu.SemaphoreType.DMA((3,)),
+            pltpu.SemaphoreType.DMA((4,)),
         ],
         compiler_params=params(),
         name="requests",
     )(
-        number((at_c * inner + at_d) * count),
+        me,
+        number(at_c * inner + at_d),
         number(((at_a * 2 + at_c) * 2 + at_b) * inner + at_d),
         history_len,
         far(item_ids),
         far(row_place.reshape(-1, LANES)),
+        far(item_table),
     )
     mail = all_to_all(mail, ALL)
     wanted = swapped(mail[:, :cap]).reshape(1, slots)
-    chunks = min(4, rows_dev // part)
-    rows = pl.pallas_call(
+    (rows,) = kernel_call(
         functools.partial(pick_kernel, cap, part, askers),
-        out_shape=pltpu.VMEM((slots, width), bf16),
-        in_specs=[vmem(), hbm()],
-        out_specs=vmem(),
-        scratch_shapes=[
-            pltpu.VMEM((chunks, rows_dev // chunks, width), bf16),
-            pltpu.VMEM((slots, part), f32),
-            pltpu.VMEM((slots, part), f32),
-            pltpu.SemaphoreType.DMA((chunks,)),
-        ],
-        compiler_params=params(),
-        name="pick",
-    )(near(mail), far(item_table))
+        (((slots, width), bf16),),
+        (mail, table),
+        scratch=[pltpu.VMEM((slots, part), f32), pltpu.VMEM((slots, part), f32)],
+    )
     rows = all_to_all(rows.reshape(owners, cap, width), ALL).reshape(slots, width)
 
-    send, emb, slope, gate, mgrad = kernel_call(
-        project_kernel,
+    piece = ((count, 4 * head), bf16)
+    whole = pltpu.VMEM((group, count, 4 * head), bf16)
+
+    def exchange(pieces):
+        return [pieces[0]] + [
+            lax.ppermute(pieces[k], GROUP, [(g, g ^ k) for g in range(group)])
+            for k in range(1, group)
+        ]
+
+    emb, slope, gate, mgrad, *sent = kernel_call(
+        functools.partial(project_kernel, copies),
         (
-            ((HEADS, count, 4 * head), bf16),
             ((count, width), bf16),
             ((count, 4 * width), f32),
             ((count, width), f32),
             ((count, width), f32),
-        ),
+        )
+        + (piece,) * group,
         (mail, rows, cot, input_proj, output_proj),
-    )
-    if copies > 1:
-        send = jnp.repeat(send, copies, axis=0)
-    mine = all_to_all(send, GROUP)
-    tiles = group * (group + 1) // 2
-    ready = tiles * count * count * 6 <= 16 * 1024 * 1024
-    att, dz, share, *weights = kernel_call(
-        functools.partial(forward_kernel, ready),
+        scratch=[pltpu.VMEM((HEADS, count, 4 * head), bf16)],
+        numbers=(me,),
+    )
+    mine = exchange(sent)
+    length = group * count
+    tiles = group * (group + 1) // 2 * count
+    ready = tiles * count * 6 <= 16 * 1024 * 1024
+    x, att, dz, share, *weights = kernel_call(
+        functools.partial(forward_kernel, ready, group),
         (
+            ((group, count, 4 * head), bf16),
             ((group, head, count), f32),
             ((group, head, count), f32),
             ((group, 5, group, count), bf16),
         )
-        + (((tiles, count, count), bf16), ((tiles, count, count), f32)) * ready,
-        (mine,),
+        + (((tiles, count), bf16),)
+        + (((tiles, count), f32),) * ready,
+        mine,
         scratch=[
-            pltpu.VMEM((group, head, count), bf16),
+            pltpu.VMEM((head, length), bf16),
+            pltpu.VMEM((length, head), bf16),
             pltpu.VMEM((4, group, count), f32),
         ],
+        numbers=(me,),
     )
     stats = all_to_all(share, GROUP)
     scratch = [
-        pltpu.VMEM((group, head, count), f32),
+        whole,
         pltpu.VMEM((group, count, head), bf16),
         pltpu.VMEM((group, head, count), bf16),
         pltpu.VMEM((group, count, head), bf16),
+        pltpu.VMEM((length, head), bf16),
+        pltpu.VMEM((head, length), bf16),
+        pltpu.VMEM((length, head), bf16),
+        pltpu.VMEM((length, head), f32),
+        pltpu.VMEM((length, head), f32),
     ]
     if not ready:
         scratch.append(pltpu.VMEM((group, head, count), bf16))
-    (grads,) = kernel_call(
-        functools.partial(backward_kernel, copies, ready),
-        (((group, count, 4 * head), bf16),),
-        (mine, *weights, att, dz, stats),
+    grads = kernel_call(
+        functools.partial(backward_kernel, copies, ready, group),
+        (piece,) * group,
+        (x, *weights, att, dz, stats),
         scratch=scratch,
-    )
-    back = all_to_all(grads, GROUP)
+        numbers=(me,),
+    )
+    back = exchange(grads)
     outgoing, layer_out = kernel_call(
-        functools.partial(finish_kernel, copies),
+        functools.partial(finish_kernel, copies, group),
         (((slots, width), bf16), ((count, width), bf16)),
-        (mail, back, slope, gate, mgrad, emb, cot, input_proj, output_proj),
+        (*back, mail, slope, gate, mgrad, emb, cot, input_proj, output_proj),
+        scratch=[whole],
+        numbers=(me,),
     )
     arrived = all_to_all(outgoing.reshape(owners, cap, width), ALL).reshape(slots, width)
     layer_out = moved(layer_out)
-    tile = math.gcd(rows_dev, 1024)
+    tile = math.gcd(rows_dev, TILE)
     table_grad, layer_out = pl.pallas_call(
         functools.partial(table_kernel, part),
-        out_shape=(
-            jax.ShapeDtypeStruct((rows_dev, width), bf16),
-            jax.ShapeDtypeStruct((count, width), bf16),
-        ),
-        grid=(rows_dev // tile,),
+        out_shape=(pltpu.HBM((rows_dev, width), bf16), pltpu.HBM((count, width), bf16)),
         in_specs=[vmem(), vmem(), vmem()],
-        out_specs=(
-            pl.BlockSpec((tile, width), lambda r: (r, 0)),
-            pl.BlockSpec((count, width), lambda r: (0, 0)),
-        ),
-        scratch_shapes=[pltpu.VMEM((tile, slots), bf16)],
+        out_specs=(hbm(), hbm()),
+        scratch_shapes=[
+            pltpu.VMEM((rows_dev // tile, tile, width), bf16),
+            pltpu.VMEM((2, tile, slots), bf16),
+            pltpu.SemaphoreType.DMA((rows_dev // tile + 1,)),
+        ],
         compiler_params=params(),
         name="table_grad",
     )(near(wanted), near(arrived), near(layer_out))
@@ -561,7 +599,7 @@
 
 def solution(mesh):
     table, seq = mesh.shape["table"], mesh.shape["seq"]
-    if table % 2 or seq % 2 or seq % HEADS:
+    if table % 2 or seq % 2 or seq % HEADS or seq & (seq - 1):
         raise ValueError("unsupported mesh")
     finer = Mesh(mesh.devices.reshape(table // 2, 2, 2, seq // 2), ALL)
     placed = (

time: 146 us -> 137 us (0.938)
  blocking collectives: 56.7 us -> 22.2 us
  waiting for transfers between devices: 42.5 us -> 62.4 us
  starting transfers between devices: 15.2 us -> 23.7 us
  Pallas kernels: 26.9 us -> 25.3 us
    all_to_all x4 -> x2, blocking collectives: 56.7 us -> 22.2 us  [all_to_all(): return lax.all_to_all(pieces, axes, split_axis=0, concat_axis=0, tiled=True)]
    ppermute x0 -> x14, waiting for transfers between devices: none -> 19.9 us  [exchange(): lax.ppermute(pieces[k], GROUP, [(g, g ^ k) for g in range(group)])]
    ppermute x0 -> x14, starting transfers between devices: none -> 9.14 us  [exchange(): lax.ppermute(pieces[k], GROUP, [(g, g ^ k) for g in range(group)])]
    pallas_call x2 -> x1, Pallas kernels: 9.77 us -> 4.44 us  [local(): pl.pallas_call(functools.partial(table_kernel, part), out_shape=(pltpu.HB...]
    pallas_call x4 -> x5, Pallas kernels: 15 us -> 18.5 us  [kernel_call(): pl.pallas_call(kernel, out_shape=tuple((pltpu.VMEM(shape, dtype) for shap...]
  transfers between devices with their start and end apart: 4 -> 18, of which waited for: 2 -> 10; matrix products, arithmetic and copies ran while one was open for 0% -> 0% of each run, Pallas kernels for 0% -> 0%
where the time goes in v2:
time: 137 us
  waiting for transfers between devices  62.4 us (46%)
  Pallas kernels  25.3 us (18%)
  starting transfers between devices  23.7 us (17%)
  blocking collectives  22.2 us (16%)
  local copies, waits for them, and re-layouts  1.81 us (1%)
  between operations  1.59 us (1%)
    all_to_all x2, blocking collectives, all_to_all(): return lax.all_to_all(pieces, axes, split_axis=0, concat_axis=0, tiled=True)  22.2 us
    ppermute x1, waiting for transfers between devices, local(): cot = moved(out_cotangent[0])  21.3 us
    ppermute x1, waiting for transfers between devices, local(): layer_out = moved(layer_out)  21.2 us
    ppermute x14, waiting for transfers between devices, exchange(): lax.ppermute(pieces[k], GROUP, [(g, g ^ k) for g in range(group)])  19.9 us
    pallas_call x5, Pallas kernels, kernel_call(): pl.pallas_call(kernel, out_shape=tuple((pltpu.VMEM(shape, dtype) for shap...  18.5 us
    ppermute x14, starting transfers between devices, exchange(): lax.ppermute(pieces[k], GROUP, [(g, g ^ k) for g in range(group)])  9.14 us
    all_to_all x2, starting transfers between devices, all_to_all(): return lax.all_to_all(pieces, axes, split_axis=0, concat_axis=0, tiled=True)  5.55 us
    ppermute x1, starting transfers between devices, local(): cot = moved(out_cotangent[0])  4.57 us
  transfers between devices with their start and end apart: 18, of which 10 were waited for; matrix products, arithmetic and copies ran while one was open for 0% of the time, Pallas kernels for 0%

profile of v2, /device:TPU:1, one launch (start us, length us, event | category | flops | bytes accessed | tf_op | source)
XLA Modules:
  0.0 137.0 jit_solution(4892049832965674430)
XLA Ops:
  1.3 2.4 %requests.1 = (s32[32,384]{1,0:T(8,128)S(1)}, bf16[4096,512]{1,0:T(8,128)(2,1)S(1)}) custom-call(s32[1]{0:T(128)} %bitcast.unused_s.me_s, s32[1]{0:T(128)} %bitcast.1.block_s, s32[1]{0:T(128)} %bitcast.2.twin_s, s32[1]{0:T(128)S(6)} %copy.17.length_s, s32[1,256]{1,0:T(1,128)} %ids_hbm.1, s32[1024,128]{1,0:T(8,128)} %bitcast.25, bf16[4096,512]{1,0:T(8,128)(2,1)} %table_hbm.1), custom_call_target="tpu_custom_call" | custom-call | tf_op jit(solution)/shard_map/requests/pallas_call | solution.py:472
  3.7 0.0 copy-start
  3.7 0.0 copy-start.1
  3.7 0.1 copy.10
  3.8 14.0 %all_to_all.26 = s32[32,1,384]{2,1,0:T(1,128)S(1)} all-to-all(s32[32,1,384]{2,1,0:T(1,128)S(1)} %copy.10), channel_id=1, replica_groups=mesh['a'=2,'b'=2,'c'=2,'d'=4] {'a','b','c','d'}, dimensions={0} | all-to-all | bytes 98304 | tf_op jit(solution)/shard_map/all_to_all | solution.py:434
  17.8 4.4 %shard_map.86 = bf16[768,512]{1,0:T(8,128)(2,1)} custom-call(s32[32,384]{1,0:T(8,128)S(1)} %bitcast.20, bf16[4096,512]{1,0:T(8,128)(2,1)S(1)} %get-tuple-element.35.table_ref), custom_call_target="tpu_custom_call" | custom-call | tf_op jit(solution)/shard_map/pallas_call | solution.py:48
  22.2 2.6 %all-to-all-start.1 = ((bf16[32,24,512]{2,1,0:T(8,128)(2,1)}), bf16[32,24,512]{2,1,0:T(8,128)(2,1)S(1)}, u32[]{:S(2)}, u32[]{:S(2)}) async-start(bf16[32,24,512]{2,1,0:T(8,128)(2,1)} %bitcast.7), calls=%async_computation.1 | async-start | bytes 1572864 | tf_op jit(solution)/shard_map/all_to_all | solution.py:434
  24.8 4.6 %collective-permute-start = (bf16[256,512]{1,0:T(8,128)(2,1)}, bf16[256,512]{1,0:T(8,128)(2,1)S(1)}, u32[]{:S(2)}, u32[]{:S(2)}) collective-permute-start(bf16[256,512]{1,0:T(8,128)(2,1)} %bitcast.28), channel_id=1, source_target_pairs={{0,0},{4,8},{8,4},{12,12},{1,1},{5,9},{9,5},{13,13},{2,2},{6,10},{... | collective-permute-start | bytes 786440 | tf_op jit(solution)/shard_map/ppermute | solution.py:471
  29.4 21.3 %collective-permute-done.cot_ref.refs_13_ = bf16[256,512]{1,0:T(8,128)(2,1)S(1)} collective-permute-done((bf16[256,512]{1,0:T(8,128)(2,1)}, bf16[256,512]{1,0:T(8,128)(2,1)S(1)}, u32[]{:S(2)}, u32[]{:S(2)}) %collective-permute-start) | collective-permute-done | bytes 262176 | tf_op jit(solution)/shard_map/ppermute | solution.py:471
  50.7 0.0 copy-start.2
  50.7 0.7 copy-done.2
  51.4 0.0 all-to-all-done.1
  51.4 0.0 copy-done
  51.4 0.0 copy-done.1
  51.4 0.0 copy-start.3
  51.4 0.9 copy-done.3
  52.4 2.0 %shard_map.87 = (bf16[256,512]{1,0:T(8,128)(2,1)S(1)}, f32[256,2048]{1,0:T(8,128)S(1)}, f32[256,512]{1,0:T(8,128)S(1)}, f32[256,512]{1,0:T(8,128)S(1)}, bf16[256...) custom-call(s32[1]{0:T(128)} %bitcast.unused_s.me_s, ...), custom_call_target="tpu_custom_call" | custom-call | tf_op jit(solution)/shard_map/pallas_call | solution.py:48
  54.4 1.3 collective-permute-start.1
  55.7 0.0 collective-permute-start.2
  55.7 1.4 %collective-permute-start.3 = (bf16[256,256]{1,0:T(8,128)(2,1)S(1)}, bf16[256,256]{1,0:T(8,128)(2,1)S(1)}, u32[]{:S(2)}, u32[]{:S(2)}) collective-permute-start(bf16[256,256]{1,0:T(8,128)(2,1)S(1)} %get-tuple-element.39), channel_id=1, source_target_pairs={{0,3},{1,2},{2,1},{3,0},{8,11},{9,10},{10,9},{11,8},{4,7},{5,6},{6... | collective-permute-start | bytes 393224 | tf_op jit(solution)/shard_map/ppermute | solution.py:513
  57.1 0.0 collective-permute-start.4
  57.1 1.6 %collective-permute-start.5 = (bf16[256,256]{1,0:T(8,128)(2,1)S(1)}, bf16[256,256]{1,0:T(8,128)(2,1)S(1)}, u32[]{:S(2)}, u32[]{:S(2)}) collective-permute-start(bf16[256,256]{1,0:T(8,128)(2,1)S(1)} %get-tuple-element.41), channel_id=1, source_target_pairs={{0,9},{1,8},{2,11},{3,10},{8,1},{9,0},{10,3},{11,2},{4,13},{5,12},... | collective-permute-start | bytes 393224 | tf_op jit(solution)/shard_map/ppermute | solution.py:513
  58.7 0.0 collective-permute-done.1.refs_1_
  58.7 0.0 collective-permute-start.6
  58.7 2.4 %collective-permute-done.2.refs_2_ = bf16[256,256]{1,0:T(8,128)(2,1)S(1)} collective-permute-done((bf16[256,256]{1,0:T(8,128)(2,1)S(1)}, bf16[256,256]{1,0:T(8,128)(2,1)S(1)}, u32[]{:S(2)}, u32[]{:S(2)}) %collective-permute-start.2) | collective-permute-done | bytes 131104 | tf_op jit(solution)/shard_map/ppermute | solution.py:513
  61.1 0.4 collective-permute-start.7
  61.5 1.5 %collective-permute-done.3.refs_3_ = bf16[256,256]{1,0:T(8,128)(2,1)S(1)} collective-permute-done((bf16[256,256]{1,0:T(8,128)(2,1)S(1)}, bf16[256,256]{1,0:T(8,128)(2,1)S(1)}, u32[]{:S(2)}, u32[]{:S(2)}) %collective-permute-start.3) | collective-permute-done | bytes 131104 | tf_op jit(solution)/shard_map/ppermute | solution.py:513
  63.0 0.0 collective-permute-done.4.refs_4_
  63.0 2.4 %collective-permute-done.5.refs_5_ = bf16[256,256]{1,0:T(8,128)(2,1)S(1)} collective-permute-done((bf16[256,256]{1,0:T(8,128)(2,1)S(1)}, bf16[256,256]{1,0:T(8,128)(2,1)S(1)}, u32[]{:S(2)}, u32[]{:S(2)}) %collective-permute-start.5) | collective-permute-done | bytes 131104 | tf_op jit(solution)/shard_map/ppermute | solution.py:513
  65.5 0.0 collective-permute-done.6.refs_6_
  65.5 3.2 %collective-permute-done.7.refs_7_ = bf16[256,256]{1,0:T(8,128)(2,1)S(1)} collective-permute-done((bf16[256,256]{1,0:T(8,128)(2,1)S(1)}, bf16[256,256]{1,0:T(8,128)(2,1)S(1)}, u32[]{:S(2)}, u32[]{:S(2)}) %collective-permute-start.7) | collective-permute-done | bytes 131104 | tf_op jit(solution)/shard_map/ppermute | solution.py:513
  68.7 4.2 %shard_map.88 = (bf16[8,256,256]{2,1,0:T(8,128)(2,1)S(1)}, f32[8,64,256]{2,1,0:T(8,128)S(1)}, f32[8,64,256]{2,1,0:T(8,128)S(1)}, bf16[8,5,8,256]{3,2,1,0:T(8,128...) custom-call(s32[1]{0:T(128)} %bitcast.unused_s.me_s, bf16[256,256]{1,0:T(8,128)(2,1)S(1)} %get-tuple-element.36.refs_0_, ...), custom_call_target="tpu_custom_call" | custom-call | tf_op jit(solution)/shard_map/pallas_call | solution.py:48
  72.9 8.2 %all_to_all.27.refs_5_ = bf16[8,5,8,256]{3,2,1,0:T(8,128)(2,1)S(1)} all-to-all(bf16[8,5,8,256]{3,2,1,0:T(8,128)(2,1)S(1)} %get-tuple-element.49), channel_id=1, replica_groups=mesh['a'=2,'b'=2,'c'=2,'d'=4] {'b','d'}, dimensions={0} | all-to-all | bytes 327680 | tf_op jit(solution)/shard_map/all_to_all | solution.py:434
  81.0 5.4 %shard_map.89 = (bf16[256,256]{1,0:T(8,128)(2,1)S(1)}, bf16[256,256]{1,0:T(8,128)(2,1)S(1)}, bf16[256,256]{1,0:T(8,128)(2,1)S(1)}, bf16[256,256]{1,0:T(8,128)(2,...) custom-call(s32[1]{0:T(128)} %bitcast.unused_s.me_s, ...), custom_call_target="tpu_custom_call" | custom-call | tf_op jit(solution)/shard_map/pallas_call | solution.py:48
  86.4 0.3 collective-permute-start.10
  86.7 0.8 collective-permute-start.11
  87.5 1.2 collective-permute-start.12
  88.7 1.4 collective-permute-start.13
  90.1 0.2 collective-permute-start.14
  90.3 1.8 %collective-permute-done.10.refs_3_ = bf16[256,256]{1,0:T(8,128)(2,1)S(1)} collective-permute-done((bf16[256,256]{1,0:T(8,128)(2,1)S(1)}, bf16[256,256]{1,0:T(8,128)(2,1)S(1)}, u32[]{:S(2)}, u32[]{:S(2)}) %collective-permute-start.10) | collective-permute-done | bytes 131104 | tf_op jit(solution)/shard_map/ppermute | solution.py:513
  92.1 0.0 collective-permute-start.8
  92.1 0.0 collective-permute-done.11.refs_4_
  92.1 0.5 collective-permute-start.9
  92.6 4.0 %collective-permute-done.12.refs_5_ = bf16[256,256]{1,0:T(8,128)(2,1)S(1)} collective-permute-done((bf16[256,256]{1,0:T(8,128)(2,1)S(1)}, bf16[256,256]{1,0:T(8,128)(2,1)S(1)}, u32[]{:S(2)}, u32[]{:S(2)}) %collective-permute-start.12) | collective-permute-done | bytes 131104 | tf_op jit(solution)/shard_map/ppermute | solution.py:513
  96.6 0.0 collective-permute-done.13.refs_6_
  96.6 2.5 %collective-permute-done.14.refs_7_ = bf16[256,256]{1,0:T(8,128)(2,1)S(1)} collective-permute-done((bf16[256,256]{1,0:T(8,128)(2,1)S(1)}, bf16[256,256]{1,0:T(8,128)(2,1)S(1)}, u32[]{:S(2)}, u32[]{:S(2)}) %collective-permute-start.14) | collective-permute-done | bytes 131104 | tf_op jit(solution)/shard_map/ppermute | solution.py:513
  99.2 2.0 %collective-permute-done.8.refs_1_ = bf16[256,256]{1,0:T(8,128)(2,1)S(1)} collective-permute-done((bf16[256,256]{1,0:T(8,128)(2,1)S(1)}, bf16[256,256]{1,0:T(8,128)(2,1)S(1)}, u32[]{:S(2)}, u32[]{:S(2)}) %collective-permute-start.8) | collective-permute-done | bytes 131104 | tf_op jit(solution)/shard_map/ppermute | solution.py:513
  101.2 0.0 collective-permute-done.9.refs_2_
  101.2 2.5 %shard_map.90 = (bf16[768,512]{1,0:T(8,128)(2,1)}, bf16[256,512]{1,0:T(8,128)(2,1)S(1)}) custom-call(s32[1]{0:T(128)} %bitcast.unused_s.me_s, bf16[256,256]{1,0:T(8,128)(2,1)S(1)} %get-tuple-element.50.refs_0_, bf16[256,256]{1,0:T(8,128)(2,1)S(1)} %collective-permute-done.8.refs_1_, bf16[256,256]{1,0:T(8,128)(2,1)S(1)} %collective-permute-done.9.refs_2_, ...), custom_call_target="tpu_custom_call" | custom-call | tf_op jit(solution)/shard_map/pallas_call | solution.py:48
  103.7 2.9 %all-to-all-start.3 = ((bf16[32,24,512]{2,1,0:T(8,128)(2,1)}), bf16[32,24,512]{2,1,0:T(8,128)(2,1)S(1)}, u32[]{:S(2)}, u32[]{:S(2)}) async-start(bf16[32,24,512]{2,1,0:T(8,128)(2,1)} %bitcast.10), calls=%async_computation.3 | async-start | bytes 1572864 | tf_op jit(solution)/shard_map/all_to_all | solution.py:434
  106.6 4.4 %collective-permute-start.15 = (bf16[256,512]{1,0:T(8,128)(2,1)S(1)}, bf16[256,512]{1,0:T(8,128)(2,1)S(1)}, u32[]{:S(2)}, u32[]{:S(2)}) collective-permute-start(bf16[256,512]{1,0:T(8,128)(2,1)S(1)} %get-tuple-element.63), channel_id=1, source_target_pairs={{0,0},{4,8},{8,4},{12,12},{1,1},{5,9},{9,5},{13,13},{2,2},{6,10},{... | collective-permute-start | bytes 786440 | tf_op jit(solution)/shard_map/ppermute | solution.py:582
  111.1 0.1 reshape_reshape.3.asked_ref
  111.2 21.2 %collective-permute-done.15.layer_ref = bf16[256,512]{1,0:T(8,128)(2,1)S(1)} collective-permute-done((bf16[256,512]{1,0:T(8,128)(2,1)S(1)}, bf16[256,512]{1,0:T(8,128)(2,1)S(1)}, u32[]{:S(2)}, u32[]{:S(2)}) %collective-permute-start.15) | collective-permute-done | bytes 262176 | tf_op jit(solution)/shard_map/ppermute | solution.py:582
  132.4 0.0 all-to-all-done.3
  132.4 4.4 %table_grad.1 = (bf16[4096,512]{1,0:T(8,128)(2,1)}, bf16[256,512]{1,0:T(8,128)(2,1)}) custom-call(s32[1,768]{1,0:T(1,128)S(1)} %reshape_reshape.3.asked_ref, bf16[768,512]{1,0:T(8,128)(2,1)S(1)} %bitcast.18, bf16[256,512]{1,0:T(8,128)(2,1)S(1)} %collective-permute-done.15.layer_ref), custom_call_target="tpu_custom_call" | custom-call | tf_op jit(solution)/shard_map/table_grad/pallas_call | solution.py:584
  (3 shorter events, 0.0 us)
Async XLA Ops:
  3.7 47.7 %copy-start = (bf16[512,2048]{1,0:T(8,128)(2,1)S(1)}, bf16[512,2048]{1,0:T(8,128)(2,1)}, u32[]{:S(2)}) copy-start(bf16[512,2048]{1,0:T(8,128)(2,1)} %refs_14_.1) | copy-start | bytes 6291460
  3.7 47.7 %copy-start.1 = (bf16[512,512]{1,0:T(8,128)(2,1)S(1)}, bf16[512,512]{1,0:T(8,128)(2,1)}, u32[]{:S(2)}) copy-start(bf16[512,512]{1,0:T(8,128)(2,1)} %refs_15_.1) | copy-start | bytes 1572868
  22.2 29.2 %all-to-all-start.1 = ((bf16[32,24,512]{2,1,0:T(8,128)(2,1)}), bf16[32,24,512]{2,1,0:T(8,128)(2,1)S(1)}, u32[]{:S(2)}, u32[]{:S(2)}) async-start(bf16[32,24,512]{2,1,0:T(8,128)(2,1)} %bitcast.7), calls=%async_computation.1 | async-start | bytes 1572864 | tf_op jit(solution)/shard_map/all_to_all | solution.py:434
  24.8 25.9 %collective-permute-start = (bf16[256,512]{1,0:T(8,128)(2,1)}, bf16[256,512]{1,0:T(8,128)(2,1)S(1)}, u32[]{:S(2)}, u32[]{:S(2)}) collective-permute-start(bf16[256,512]{1,0:T(8,128)(2,1)} %bitcast.28), channel_id=1, source_target_pairs={{0,0},{4,8},{8,4},{12,12},{1,1},{5,9},{9,5},{13,13},{2,2},{6,10},{... | collective-permute-start | bytes 786440 | tf_op jit(solution)/shard_map/ppermute | solution.py:471
  50.7 0.7 copy-start.2
  51.4 1.0 copy-start.3
  54.4 4.3 %collective-permute-start.1 = (bf16[256,256]{1,0:T(8,128)(2,1)S(1)}, bf16[256,256]{1,0:T(8,128)(2,1)S(1)}, u32[]{:S(2)}, u32[]{:S(2)}) collective-permute-start(bf16[256,256]{1,0:T(8,128)(2,1)S(1)} %get-tuple-element.37), channel_id=1, source_target_pairs={{0,1},{1,0},{2,3},{3,2},{8,9},{9,8},{10,11},{11,10},{4,5},{5,4},{6... | collective-permute-start | bytes 393224 | tf_op jit(solution)/shard_map/ppermute | solution.py:513
  55.7 5.5 %collective-permute-start.2 = (bf16[256,256]{1,0:T(8,128)(2,1)S(1)}, bf16[256,256]{1,0:T(8,128)(2,1)S(1)}, u32[]{:S(2)}, u32[]{:S(2)}) collective-permute-start(bf16[256,256]{1,0:T(8,128)(2,1)S(1)} %get-tuple-element.38), channel_id=1, source_target_pairs={{0,2},{1,3},{2,0},{3,1},{8,10},{9,11},{10,8},{11,9},{4,6},{5,7},{6... | collective-permute-start | bytes 393224 | tf_op jit(solution)/shard_map/ppermute | solution.py:513
  55.7 7.4 %collective-permute-start.3 = (bf16[256,256]{1,0:T(8,128)(2,1)S(1)}, bf16[256,256]{1,0:T(8,128)(2,1)S(1)}, u32[]{:S(2)}, u32[]{:S(2)}) collective-permute-start(bf16[256,256]{1,0:T(8,128)(2,1)S(1)} %get-tuple-element.39), channel_id=1, source_target_pairs={{0,3},{1,2},{2,1},{3,0},{8,11},{9,10},{10,9},{11,8},{4,7},{5,6},{6... | collective-permute-start | bytes 393224 | tf_op jit(solution)/shard_map/ppermute | solution.py:513
  57.1 5.9 %collective-permute-start.4 = (bf16[256,256]{1,0:T(8,128)(2,1)S(1)}, bf16[256,256]{1,0:T(8,128)(2,1)S(1)}, u32[]{:S(2)}, u32[]{:S(2)}) collective-permute-start(bf16[256,256]{1,0:T(8,128)(2,1)S(1)} %get-tuple-element.40), channel_id=1, source_target_pairs={{0,8},{1,9},{2,10},{3,11},{8,0},{9,1},{10,2},{11,3},{4,12},{5,13},... | collective-permute-start | bytes 393224 | tf_op jit(solution)/shard_map/ppermute | solution.py:513
  57.1 8.4 %collective-permute-start.5 = (bf16[256,256]{1,0:T(8,128)(2,1)S(1)}, bf16[256,256]{1,0:T(8,128)(2,1)S(1)}, u32[]{:S(2)}, u32[]{:S(2)}) collective-permute-start(bf16[256,256]{1,0:T(8,128)(2,1)S(1)} %get-tuple-element.41), channel_id=1, source_target_pairs={{0,9},{1,8},{2,11},{3,10},{8,1},{9,0},{10,3},{11,2},{4,13},{5,12},... | collective-permute-start | bytes 393224 | tf_op jit(solution)/shard_map/ppermute | solution.py:513
  58.7 6.8 %collective-permute-start.6 = (bf16[256,256]{1,0:T(8,128)(2,1)S(1)}, bf16[256,256]{1,0:T(8,128)(2,1)S(1)}, u32[]{:S(2)}, u32[]{:S(2)}) collective-permute-start(bf16[256,256]{1,0:T(8,128)(2,1)S(1)} %get-tuple-element.42), channel_id=1, source_target_pairs={{0,10},{1,11},{2,8},{3,9},{8,2},{9,3},{10,0},{11,1},{4,14},{5,15},... | collective-permute-start | bytes 393224 | tf_op jit(solution)/shard_map/ppermute | solution.py:513
  61.1 7.5 %collective-permute-start.7 = (bf16[256,256]{1,0:T(8,128)(2,1)S(1)}, bf16[256,256]{1,0:T(8,128)(2,1)S(1)}, u32[]{:S(2)}, u32[]{:S(2)}) collective-permute-start(bf16[256,256]{1,0:T(8,128)(2,1)S(1)} %get-tuple-element.43), channel_id=1, source_target_pairs={{0,11},{1,10},{2,9},{3,8},{8,3},{9,2},{10,1},{11,0},{4,15},{5,14},... | collective-permute-start | bytes 393224 | tf_op jit(solution)/shard_map/ppermute | solution.py:513
  86.4 5.7 %collective-permute-start.10 = (bf16[256,256]{1,0:T(8,128)(2,1)S(1)}, bf16[256,256]{1,0:T(8,128)(2,1)S(1)}, u32[]{:S(2)}, u32[]{:S(2)}) collective-permute-start(bf16[256,256]{1,0:T(8,128)(2,1)S(1)} %get-tuple-element.53), channel_id=1, source_target_pairs={{0,3},{1,2},{2,1},{3,0},{8,11},{9,10},{10,9},{11,8},{4,7},{5,6},{6... | collective-permute-start | bytes 393224 | tf_op jit(solution)/shard_map/ppermute | solution.py:513
  86.7 5.4 %collective-permute-start.11 = (bf16[256,256]{1,0:T(8,128)(2,1)S(1)}, bf16[256,256]{1,0:T(8,128)(2,1)S(1)}, u32[]{:S(2)}, u32[]{:S(2)}) collective-permute-start(bf16[256,256]{1,0:T(8,128)(2,1)S(1)} %get-tuple-element.54), channel_id=1, source_target_pairs={{0,8},{1,9},{2,10},{3,11},{8,0},{9,1},{10,2},{11,3},{4,12},{5,13},... | collective-permute-start | bytes 393224 | tf_op jit(solution)/shard_map/ppermute | solution.py:513
  87.5 9.1 %collective-permute-start.12 = (bf16[256,256]{1,0:T(8,128)(2,1)S(1)}, bf16[256,256]{1,0:T(8,128)(2,1)S(1)}, u32[]{:S(2)}, u32[]{:S(2)}) collective-permute-start(bf16[256,256]{1,0:T(8,128)(2,1)S(1)} %get-tuple-element.55), channel_id=1, source_target_pairs={{0,9},{1,8},{2,11},{3,10},{8,1},{9,0},{10,3},{11,2},{4,13},{5,12},... | collective-permute-start | bytes 393224 | tf_op jit(solution)/shard_map/ppermute | solution.py:513
  88.7 7.9 %collective-permute-start.13 = (bf16[256,256]{1,0:T(8,128)(2,1)S(1)}, bf16[256,256]{1,0:T(8,128)(2,1)S(1)}, u32[]{:S(2)}, u32[]{:S(2)}) collective-permute-start(bf16[256,256]{1,0:T(8,128)(2,1)S(1)} %get-tuple-element.56), channel_id=1, source_target_pairs={{0,10},{1,11},{2,8},{3,9},{8,2},{9,3},{10,0},{11,1},{4,14},{5,15},... | collective-permute-start | bytes 393224 | tf_op jit(solution)/shard_map/ppermute | solution.py:513
  90.1 9.1 %collective-permute-start.14 = (bf16[256,256]{1,0:T(8,128)(2,1)S(1)}, bf16[256,256]{1,0:T(8,128)(2,1)S(1)}, u32[]{:S(2)}, u32[]{:S(2)}) collective-permute-start(bf16[256,256]{1,0:T(8,128)(2,1)S(1)} %get-tuple-element.57), channel_id=1, source_target_pairs={{0,11},{1,10},{2,9},{3,8},{8,3},{9,2},{10,1},{11,0},{4,15},{5,14},... | collective-permute-start | bytes 393224 | tf_op jit(solution)/shard_map/ppermute | solution.py:513
  92.1 9.1 %collective-permute-start.8 = (bf16[256,256]{1,0:T(8,128)(2,1)S(1)}, bf16[256,256]{1,0:T(8,128)(2,1)S(1)}, u32[]{:S(2)}, u32[]{:S(2)}) collective-permute-start(bf16[256,256]{1,0:T(8,128)(2,1)S(1)} %get-tuple-element.51), channel_id=1, source_target_pairs={{0,1},{1,0},{2,3},{3,2},{8,9},{9,8},{10,11},{11,10},{4,5},{5,4},{6... | collective-permute-start | bytes 393224 | tf_op jit(solution)/shard_map/ppermute | solution.py:513
  92.1 9.1 %collective-permute-start.9 = (bf16[256,256]{1,0:T(8,128)(2,1)S(1)}, bf16[256,256]{1,0:T(8,128)(2,1)S(1)}, u32[]{:S(2)}, u32[]{:S(2)}) collective-permute-start(bf16[256,256]{1,0:T(8,128)(2,1)S(1)} %get-tuple-element.52), channel_id=1, source_target_pairs={{0,2},{1,3},{2,0},{3,1},{8,10},{9,11},{10,8},{11,9},{4,6},{5,7},{6... | collective-permute-start | bytes 393224 | tf_op jit(solution)/shard_map/ppermute | solution.py:513
  103.7 28.7 %all-to-all-start.3 = ((bf16[32,24,512]{2,1,0:T(8,128)(2,1)}), bf16[32,24,512]{2,1,0:T(8,128)(2,1)S(1)}, u32[]{:S(2)}, u32[]{:S(2)}) async-start(bf16[32,24,512]{2,1,0:T(8,128)(2,1)} %bitcast.10), calls=%async_computation.3 | async-start | bytes 1572864 | tf_op jit(solution)/shard_map/all_to_all | solution.py:434
  106.6 25.8 %collective-permute-start.15 = (bf16[256,512]{1,0:T(8,128)(2,1)S(1)}, bf16[256,512]{1,0:T(8,128)(2,1)S(1)}, u32[]{:S(2)}, u32[]{:S(2)}) collective-permute-start(bf16[256,512]{1,0:T(8,128)(2,1)S(1)} %get-tuple-element.63), channel_id=1, source_target_pairs={{0,0},{4,8},{8,4},{12,12},{1,1},{5,9},{9,5},{13,13},{2,2},{6,10},{... | collective-permute-start | bytes 786440 | tf_op jit(solution)/shard_map/ppermute | solution.py:582

commit v3 on v2

--- a/solution.py
+++ b/solution.py
@@ -249,6 +249,7 @@
         dz_ref[b] = dz
         mean = jnp.sum(att, axis=0, keepdims=True) * (1.0 / head)
         cent = att - mean
+        share_ref[b, 5 * blocks :, :] = cent.astype(bf16)
         stat_ref[0, b : b + 1, :] = mean
         stat_ref[1, b : b + 1, :] = jnp.sum(cent * cent, axis=0, keepdims=True)
         stat_ref[2, b : b + 1, :] = jnp.sum(dz, axis=0, keepdims=True)
@@ -259,7 +260,54 @@
     others = [stat_ref[n].astype(bf16) for n in range(1, 4)]
     for g in range(blocks):
         for n, stat in enumerate([high, low] + others):
-            share_ref[g, n] = stat
+            share_ref[g, n * blocks : (n + 1) * blocks, :] = stat
+
+
+def combine(stats_ref, copies, blocks, head):
+    heads = range(0, HEADS * copies, copies)
+    width = head * HEADS
+
+    def stat_of(h, n):
+        return stats_ref[h, n * blocks : (n + 1) * blocks, :].astype(f32)
+
+    means = [stat_of(h, 0) + stat_of(h, 1) for h in heads]
+    mean = sum(means) * (1.0 / HEADS)
+    offs = [part - mean for part in means]
+    square = 0.0
+    dz_sum = 0.0
+    dz_att = 0.0
+    for h, off in zip(heads, offs):
+        square = square + (stat_of(h, 2) + head * (off * off))
+        dz_sum = dz_sum + stat_of(h, 3)
+        dz_att = dz_att + (stat_of(h, 4) + stat_of(h, 3) * off)
+    inv = 1.0 / jnp.sqrt(square * (1.0 / width) + eps_norm)
+    return mean, offs, inv, dz_sum * (1.0 / width), dz_att * inv * (1.0 / width)
+
+
+def output_kernel(
+    copies, me_s, share_ref, mail_ref, gate_ref, emb_ref, wo_ref, norm_ref, layer_ref, row_scr
+):
+    group = share_ref.shape[0]
+    width = emb_ref.shape[1]
+    head = width // HEADS
+    unused, offs, inv, *others = combine(share_ref, copies, group, head)
+    for n, rows in enumerate(offs + [inv]):
+        row_scr[n] = rows
+    mine = pl.ds(me_s[0], 1)
+    inv = row_scr[HEADS, mine, :]
+    att_t = jnp.concatenate(
+        [
+            (share_ref[h * copies, 5 * group :, :].astype(f32) + row_scr[h, mine, :]) * inv
+            for h in range(HEADS)
+        ],
+        axis=0,
+    )
+    att_n = att_t.T
+    norm_ref[...] = att_n
+    unused, live_row = read_note(mail_ref)
+    mixed = (att_n * gate_ref[...]).astype(bf16)
+    branch = dot(mixed, wo_ref[...])
+    layer_ref[...] = (to_col(live_row) * (emb_ref[...].astype(f32) + branch)).astype(bf16)
 
 
 def backward_kernel(copies, ready, group, me_s, *refs):
@@ -270,35 +318,20 @@
         qt_scr = refs[-1]
     refs = refs[5 + ready :]
     pieces = refs[:group]
-    out_ref, da_scr, dat_scr, q_scr, keys_scr, keyst_scr, values_scr, dk_scr, dv_scr = refs[
-        group : group + 9
+    out_ref, da_scr, dat_scr, q_scr, keys_scr, keyst_scr, values_scr, dq_scr, dk_scr, dv_scr = refs[
+        group : group + 10
     ]
     blocks, rows, cols = x_ref.shape
     head = cols // 4
     scale = head ** (-0.5)
-    width = head * HEADS
-    heads = range(0, HEADS * copies, copies)
-
-    def stat_of(h, n):
-        return stats_ref[h, n].astype(f32)
-
-    means = {h: stat_of(h, 0) + stat_of(h, 1) for h in heads}
-    mean = sum(means.values()) * (1.0 / HEADS)
-    square = 0.0
-    dz_sum = 0.0
-    dz_att = 0.0
-    for h in heads:
-        off = means[h] - mean
-        square = square + (stat_of(h, 2) + head * (off * off))
-        dz_sum = dz_sum + stat_of(h, 3)
-        dz_att = dz_att + (stat_of(h, 4) + stat_of(h, 3) * off)
-    inv = 1.0 / jnp.sqrt(square * (1.0 / width) + eps_norm)
-    mean_dz = dz_sum * (1.0 / width)
-    mean_prod = dz_att * inv * (1.0 / width)
+
+    def span_of(b):
+        return slice(b * rows, (b + 1) * rows)
+
+    mean, _, inv, mean_dz, mean_prod = combine(stats_ref, copies, blocks, head)
     for b in range(blocks):
         att_n = (att_ref[b] - mean[b : b + 1]) * inv[b : b + 1]
         da_t = (dz_ref[b] - mean_dz[b : b + 1] - att_n * mean_prod[b : b + 1]) * inv[b : b + 1]
-        out_ref[b, :, 3 * head :] = att_n.T.astype(bf16)
         dat_scr[b] = (0.5 * da_t).astype(bf16)
         da_scr[b] = da_t.T.astype(bf16)
         q = x_ref[b, :, 0:head].astype(f32) * scale
@@ -334,46 +367,47 @@
         dv_scr[above:upto, :] = dv[above:]
         dk_scr[above:upto, :] = dk[above:]
         dq = dot(keyst_scr[:, :upto], sgrad)
-        out_ref[b, :, 0:head] = (dq * scale).T.astype(bf16)
+        dq_scr[span_of(b), :] = (dq * scale).T
+    half = rows // 2
     for b in range(blocks):
-        span = slice(b * rows, (b + 1) * rows)
-        out_ref[b, :, head : 2 * head] = dk_scr[span, :].astype(bf16)
-        out_ref[b, :, 2 * head : 3 * head] = dv_scr[span, :].astype(bf16)
+        span = span_of(b)
+        pair = jnp.concatenate([dq_scr[span, :], dk_scr[span, :]], axis=1)
+        out_ref[b, :rows, :] = pair.astype(bf16)
+        low = dv_scr[b * rows : b * rows + half, :]
+        high = dv_scr[b * rows + half : (b + 1) * rows, :]
+        out_ref[b, rows:, :] = jnp.concatenate([low, high], axis=1).astype(bf16)
     hand_out(me_s, pieces, out_ref)
-
-
-def head_columns(grad_ref, copies, part, head):
-    return jnp.concatenate(
-        [
-            grad_ref[h * copies, :, part * head : (part + 1) * head].astype(f32)
-            for h in range(HEADS)
-        ],
-        axis=1,
-    )
 
 
 def finish_kernel(copies, group, me_s, *refs):
     pieces, refs = refs[:group], refs[group:]
-    mail_ref, slope_ref, gate_ref, mgrad_ref, emb_ref, cot_ref, w_ref, wo_ref = refs[:8]
-    out_ref, layer_ref, grad_ref = refs[8:]
+    mail_ref, slope_ref, norm_ref, mgrad_ref, emb_ref, cot_ref, w_ref, out_ref, grad_ref = refs
     take_in(me_s, pieces, grad_ref)
     slot_row, live_row = read_note(mail_ref)
     count, width = emb_ref.shape
     slots = out_ref.shape[0]
     head = width // HEADS
     live_col = to_col(live_row)
-    columns = functools.partial(head_columns, grad_ref, copies, head=head)
-    att_n = columns(3)
-    mixed = (att_n * gate_ref[...]).astype(bf16)
-    branch = dot(mixed, wo_ref[...])
-    embedded = emb_ref[...].astype(f32)
-    layer_ref[...] = (live_col * (embedded + branch)).astype(bf16)
-    act_grad = jnp.concatenate(
-        [mgrad_ref[...] * att_n, columns(2), columns(0), columns(1)], axis=1
-    )
+    heads = range(0, HEADS * copies, copies)
+
+    def part(h, span, lanes):
+        return grad_ref[h, span, lanes].astype(f32)
+
+    top, low, high = slice(0, count), slice(0, head), slice(head, 2 * head)
+    rest = slice(count, count + count // 2)
+    queries = jnp.concatenate([part(h, top, low) for h in heads], axis=1)
+    keys = jnp.concatenate([part(h, top, high) for h in heads], axis=1)
+    values = jnp.concatenate(
+        [
+            jnp.concatenate([part(h, rest, lanes) for h in heads], axis=1)
+            for lanes in (low, high)
+        ],
+        axis=0,
+    )
+    act_grad = jnp.concatenate([mgrad_ref[...] * norm_ref[...], values, queries, keys], axis=1)
     pre_grad = (act_grad * slope_ref[...]).astype(bf16)
     norm_grad = dot(pre_grad, w_ref[...], ((1,), (1,)))
-    normed, spread = normalize(embedded)
+    normed, spread = normalize(emb_ref[...].astype(f32))
     mean_grad = jnp.mean(norm_grad, axis=-1, keepdims=True)
     mean_prod = jnp.mean(norm_grad * normed, axis=-1, keepdims=True)
     cot = jnp.where(live_col > 0.0, cot_ref[...].astype(f32), 0.0)
@@ -382,10 +416,12 @@
     out_ref[...] = dot(places, emb_grad.astype(bf16)).astype(bf16)
 
 
-def pick_kernel(cap, part, askers, mail_ref, table_ref, out_ref, lane_scr, block_scr):
+def pick_kernel(cap, part, askers, mail_ref, table_ref, out_ref, asked_ref, lane_scr, block_scr):
     rows, width = table_ref.shape
     slots = out_ref.shape[0]
-    wish = mail_ref[:, :LANES].astype(f32).T
+    wish = mail_ref[:, :LANES].astype(f32)
+    asked_ref[...] = jnp.concatenate([wish[n : n + 1, :cap] for n in askers], axis=1)
+    wish = wish.T
     for taker, asker in enumerate(askers):
         column = jnp.maximum(wish[:cap, asker : asker + 1], 0.0)
         block = jnp.floor(column * (1.0 / part))
@@ -415,7 +451,7 @@
         for start in range(0, chunk, part):
             near_row = asked_ref[...] - (n * chunk + start)
             inside = (near_row >= 0) & (near_row < part)
-            near_row = jnp.where(inside, near_row, -1).astype(f32)
+            near_row = jnp.where(inside, near_row, -1.0)
             near_row = jnp.broadcast_to(near_row, (16, slots)).astype(bf16)[0:1]
             picks = jnp.where(ramp == near_row, jnp.ones((), bf16), jnp.zeros((), bf16))
             picks_scr[n % 2, start : start + part, :] = picks
@@ -463,18 +499,10 @@
 
     me = number(at_b * inner + at_d)
 
-    def swapped(pieces):
-        shape = pieces.shape
-        parts = pieces.reshape((outer, 2, 2, inner) + shape[1:])
-        return jnp.swapaxes(parts, 1, 2).reshape(shape)
-
     cot = moved(out_cotangent[0])
     mail, table = pl.pallas_call(
         functools.partial(request_kernel, rows_dev, cap),
-        out_shape=(
-            pltpu.VMEM((owners, LANES + count), i32),
-            pltpu.VMEM(item_table.shape, bf16),
-        ),
+        out_shape=(pltpu.VMEM((owners, LANES + count), i32), pltpu.VMEM(item_table.shape, bf16)),
         in_specs=[smem()] * 4 + [hbm()] * 3,
         out_specs=(vmem(), vmem()),
         scratch_shapes=[
@@ -496,17 +524,16 @@
         far(item_table),
     )
     mail = all_to_all(mail, ALL)
-    wanted = swapped(mail[:, :cap]).reshape(1, slots)
-    (rows,) = kernel_call(
+    rows, wanted = kernel_call(
         functools.partial(pick_kernel, cap, part, askers),
-        (((slots, width), bf16),),
+        (((slots, width), bf16), ((1, slots), f32)),
         (mail, table),
         scratch=[pltpu.VMEM((slots, part), f32), pltpu.VMEM((slots, part), f32)],
     )
     rows = all_to_all(rows.reshape(owners, cap, width), ALL).reshape(slots, width)
 
     piece = ((count, 4 * head), bf16)
-    whole = pltpu.VMEM((group, count, 4 * head), bf16)
+    back_piece = ((count * 3 // 2, 2 * head), bf16)
 
     def exchange(pieces):
         return [pieces[0]] + [
@@ -537,7 +564,7 @@
             ((group, count, 4 * head), bf16),
             ((group, head, count), f32),
             ((group, head, count), f32),
-            ((group, 5, group, count), bf16),
+            ((group, 5 * group + head, count), bf16),
         )
         + (((tiles, count), bf16),)
         + (((tiles, count), f32),) * ready,
@@ -550,8 +577,16 @@
         numbers=(me,),
     )
     stats = all_to_all(share, GROUP)
+    att_n, layer_out = kernel_call(
+        functools.partial(output_kernel, copies),
+        (((count, width), f32), ((count, width), bf16)),
+        (stats, mail, gate, emb, output_proj),
+        scratch=[pltpu.VMEM((HEADS + 1, group, count), f32)],
+        numbers=(me,),
+    )
+    layer_out = moved(layer_out)
     scratch = [
-        whole,
+        pltpu.VMEM((group, *back_piece[0]), bf16),
         pltpu.VMEM((group, count, head), bf16),
         pltpu.VMEM((group, head, count), bf16),
         pltpu.VMEM((group, count, head), bf16),
@@ -560,26 +595,26 @@
         pltpu.VMEM((length, head), bf16),
         pltpu.VMEM((length, head), f32),
         pltpu.VMEM((length, head), f32),
+        pltpu.VMEM((length, head), f32),
     ]
     if not ready:
         scratch.append(pltpu.VMEM((group, head, count), bf16))
     grads = kernel_call(
         functools.partial(backward_kernel, copies, ready, group),
-        (piece,) * group,
+        (back_piece,) * group,
         (x, *weights, att, dz, stats),
         scratch=scratch,
         numbers=(me,),
     )
     back = exchange(grads)
-    outgoing, layer_out = kernel_call(
+    (outgoing,) = kernel_call(
         functools.partial(finish_kernel, copies, group),
-        (((slots, width), bf16), ((count, width), bf16)),
-        (*back, mail, slope, gate, mgrad, emb, cot, input_proj, output_proj),
-        scratch=[whole],
+        (((slots, width), bf16),),
+        (*back, mail, slope, att_n, mgrad, emb, cot, input_proj),
+        scratch=[pltpu.VMEM((group, *back_piece[0]), bf16)],
         numbers=(me,),
     )
     arrived = all_to_all(outgoing.reshape(owners, cap, width), ALL).reshape(slots, width)
-    layer_out = moved(layer_out)
     tile = math.gcd(rows_dev, TILE)
     table_grad, layer_out = pl.pallas_call(
         functools.partial(table_kernel, part),

time: 137 us -> 138 us (level)
  waiting for transfers between devices: 62.4 us -> 56.6 us
  starting transfers between devices: 23.7 us -> 27.2 us
  blocking collectives: 22.2 us -> 25 us
    ppermute x14, waiting for transfers between devices: 19.9 us -> 13.9 us  [exchange(): lax.ppermute(pieces[k], GROUP, [(g, g ^ k) for g in range(group)])]
    ppermute x14, starting transfers between devices: 9.14 us -> 12.2 us  [exchange(): lax.ppermute(pieces[k], GROUP, [(g, g ^ k) for g in range(group)])]
    all_to_all x2, blocking collectives: 22.2 us -> 25 us  [all_to_all(): return lax.all_to_all(pieces, axes, split_axis=0, concat_axis=0, tiled=True)]
    pallas_call x5 -> x6, Pallas kernels: 18.5 us -> 17.9 us  [kernel_call(): pl.pallas_call(kernel, out_shape=tuple((pltpu.VMEM(shape, dtype) for shap...]
  transfers between devices with their start and end apart: 18 -> 18, of which waited for: 10 -> 9; matrix products, arithmetic and copies ran while one was open for 0% -> 0% of each run, Pallas kernels for 0% -> 0%
where the time goes in v3:
time: 138 us
  waiting for transfers between devices  56.6 us (41%)
  starting transfers between devices  27.2 us (20%)
  blocking collectives  25 us (18%)
  Pallas kernels  24.8 us (18%)
  local copies, waits for them, and re-layouts  2.59 us (2%)
  between operations  1.61 us (1%)
    all_to_all x2, blocking collectives, all_to_all(): return lax.all_to_all(pieces, axes, split_axis=0, concat_axis=0, tiled=True)  25 us
    ppermute x1, waiting for transfers between devices, local(): cot = moved(out_cotangent[0])  21.3 us
    ppermute x1, waiting for transfers between devices, local(): layer_out = moved(layer_out)  21.3 us
    pallas_call x6, Pallas kernels, kernel_call(): pl.pallas_call(kernel, out_shape=tuple((pltpu.VMEM(shape, dtype) for shap...  17.9 us
    ppermute x14, waiting for transfers between devices, exchange(): lax.ppermute(pieces[k], GROUP, [(g, g ^ k) for g in range(group)])  13.9 us
    ppermute x14, starting transfers between devices, exchange(): lax.ppermute(pieces[k], GROUP, [(g, g ^ k) for g in range(group)])  12.2 us
    all_to_all x2, starting transfers between devices, all_to_all(): return lax.all_to_all(pieces, axes, split_axis=0, concat_axis=0, tiled=True)  6.01 us
    ppermute x1, starting transfers between devices, local(): cot = moved(out_cotangent[0])  4.57 us
  transfers between devices with their start and end apart: 18, of which 9 were waited for; matrix products, arithmetic and copies ran while one was open for 0% of the time, Pallas kernels for 0%

profile of v3, /device:TPU:1, one launch (start us, length us, event | category | flops | bytes accessed | tf_op | source)
XLA Modules:
  0.0 137.8 jit_solution(4579498378221848125)
XLA Ops:
  1.3 2.4 %requests.1 = (s32[32,384]{1,0:T(8,128)S(1)}, bf16[4096,512]{1,0:T(8,128)(2,1)S(1)}) custom-call(s32[1]{0:T(128)} %bitcast.unused_s.me_s, s32[1]{0:T(128)} %bitcast.1.block_s, s32[1]{0:T(128)} %bitcast.2.twin_s, s32[1]{0:T(128)S(6)} %copy.13.length_s, s32[1,256]{1,0:T(1,128)} %ids_hbm.1, s32[1024,128]{1,0:T(8,128)} %bitcast.22, bf16[4096,512]{1,0:T(8,128)(2,1)} %table_hbm.1), custom_call_target="tpu_custom_call" | custom-call | tf_op jit(solution)/shard_map/requests/pallas_call | solution.py:503
  3.7 0.0 copy-start
  3.7 0.0 copy-start.1
  3.7 0.1 copy.9
  3.8 14.0 %all_to_all.26 = s32[32,1,384]{2,1,0:T(1,128)S(1)} all-to-all(s32[32,1,384]{2,1,0:T(1,128)S(1)} %copy.9), channel_id=1, replica_groups=mesh['a'=2,'b'=2,'c'=2,'d'=4] {'a','b','c','d'}, dimensions={0} | all-to-all | bytes 98304 | tf_op jit(solution)/shard_map/all_to_all | solution.py:470
  17.8 3.5 %shard_map.86 = (bf16[768,512]{1,0:T(8,128)(2,1)S(1)}, f32[1,768]{1,0:T(1,128)S(1)}) custom-call(s32[32,384]{1,0:T(8,128)S(1)} %bitcast.16, bf16[4096,512]{1,0:T(8,128)(2,1)S(1)} %get-tuple-element.37.table_ref), custom_call_target="tpu_custom_call" | custom-call | tf_op jit(solution)/shard_map/pallas_call | solution.py:48
  21.3 0.0 copy-start.4
  21.3 0.9 copy-done.4
  22.2 2.6 %all-to-all-start.1 = ((bf16[32,24,512]{2,1,0:T(8,128)(2,1)}), bf16[32,24,512]{2,1,0:T(8,128)(2,1)S(1)}, u32[]{:S(2)}, u32[]{:S(2)}) async-start(bf16[32,24,512]{2,1,0:T(8,128)(2,1)} %bitcast.20), calls=%async_computation.1 | async-start | bytes 1572864 | tf_op jit(solution)/shard_map/all_to_all | solution.py:470
  24.8 4.6 %collective-permute-start = (bf16[256,512]{1,0:T(8,128)(2,1)}, bf16[256,512]{1,0:T(8,128)(2,1)S(1)}, u32[]{:S(2)}, u32[]{:S(2)}) collective-permute-start(bf16[256,512]{1,0:T(8,128)(2,1)} %bitcast.23), channel_id=1, source_target_pairs={{0,0},{4,8},{8,4},{12,12},{1,1},{5,9},{9,5},{13,13},{2,2},{6,10},{... | collective-permute-start | bytes 786440 | tf_op jit(solution)/shard_map/ppermute | solution.py:502
  29.4 21.3 %collective-permute-done.cot_ref.refs_13_ = bf16[256,512]{1,0:T(8,128)(2,1)S(1)} collective-permute-done((bf16[256,512]{1,0:T(8,128)(2,1)}, bf16[256,512]{1,0:T(8,128)(2,1)S(1)}, u32[]{:S(2)}, u32[]{:S(2)}) %collective-permute-start) | collective-permute-done | bytes 262176 | tf_op jit(solution)/shard_map/ppermute | solution.py:502
  50.7 0.0 copy-start.2
  50.7 0.7 copy-done.2
  51.4 0.0 all-to-all-done.1
  51.4 0.0 copy-done
  51.5 0.0 copy-done.1
  51.5 0.0 copy-start.3
  51.5 0.9 copy-done.3
  52.4 2.0 %shard_map.87 = (bf16[256,512]{1,0:T(8,128)(2,1)S(1)}, f32[256,2048]{1,0:T(8,128)S(1)}, f32[256,512]{1,0:T(8,128)S(1)}, f32[256,512]{1,0:T(8,128)S(1)}, bf16[256...) custom-call(s32[1]{0:T(128)} %bitcast.unused_s.me_s, ...), custom_call_target="tpu_custom_call" | custom-call | tf_op jit(solution)/shard_map/pallas_call | solution.py:48
  54.5 1.3 collective-permute-start.1
  55.7 0.0 collective-permute-start.2
  55.7 1.4 %collective-permute-start.3 = (bf16[256,256]{1,0:T(8,128)(2,1)S(1)}, bf16[256,256]{1,0:T(8,128)(2,1)S(1)}, u32[]{:S(2)}, u32[]{:S(2)}) collective-permute-start(bf16[256,256]{1,0:T(8,128)(2,1)S(1)} %get-tuple-element.43), channel_id=1, source_target_pairs={{0,3},{1,2},{2,1},{3,0},{8,11},{9,10},{10,9},{11,8},{4,7},{5,6},{6... | collective-permute-start | bytes 393224 | tf_op jit(solution)/shard_map/ppermute | solution.py:540
  57.2 0.0 collective-permute-start.4
  57.2 1.6 %collective-permute-start.5 = (bf16[256,256]{1,0:T(8,128)(2,1)S(1)}, bf16[256,256]{1,0:T(8,128)(2,1)S(1)}, u32[]{:S(2)}, u32[]{:S(2)}) collective-permute-start(bf16[256,256]{1,0:T(8,128)(2,1)S(1)} %get-tuple-element.45), channel_id=1, source_target_pairs={{0,9},{1,8},{2,11},{3,10},{8,1},{9,0},{10,3},{11,2},{4,13},{5,12},... | collective-permute-start | bytes 393224 | tf_op jit(solution)/shard_map/ppermute | solution.py:540
  58.8 0.0 collective-permute-done.1.refs_1_
  58.8 0.0 collective-permute-start.6
  58.8 2.4 %collective-permute-done.2.refs_2_ = bf16[256,256]{1,0:T(8,128)(2,1)S(1)} collective-permute-done((bf16[256,256]{1,0:T(8,128)(2,1)S(1)}, bf16[256,256]{1,0:T(8,128)(2,1)S(1)}, u32[]{:S(2)}, u32[]{:S(2)}) %collective-permute-start.2) | collective-permute-done | bytes 131104 | tf_op jit(solution)/shard_map/ppermute | solution.py:540
  61.2 0.3 collective-permute-start.7
  61.6 1.6 %collective-permute-done.3.refs_3_ = bf16[256,256]{1,0:T(8,128)(2,1)S(1)} collective-permute-done((bf16[256,256]{1,0:T(8,128)(2,1)S(1)}, bf16[256,256]{1,0:T(8,128)(2,1)S(1)}, u32[]{:S(2)}, u32[]{:S(2)}) %collective-permute-start.3) | collective-permute-done | bytes 131104 | tf_op jit(solution)/shard_map/ppermute | solution.py:540
  63.1 0.0 collective-permute-done.4.refs_4_
  63.1 2.4 %collective-permute-done.5.refs_5_ = bf16[256,256]{1,0:T(8,128)(2,1)S(1)} collective-permute-done((bf16[256,256]{1,0:T(8,128)(2,1)S(1)}, bf16[256,256]{1,0:T(8,128)(2,1)S(1)}, u32[]{:S(2)}, u32[]{:S(2)}) %collective-permute-start.5) | collective-permute-done | bytes 131104 | tf_op jit(solution)/shard_map/ppermute | solution.py:540
  65.6 0.0 collective-permute-done.6.refs_6_
  65.6 3.1 %collective-permute-done.7.refs_7_ = bf16[256,256]{1,0:T(8,128)(2,1)S(1)} collective-permute-done((bf16[256,256]{1,0:T(8,128)(2,1)S(1)}, bf16[256,256]{1,0:T(8,128)(2,1)S(1)}, u32[]{:S(2)}, u32[]{:S(2)}) %collective-permute-start.7) | collective-permute-done | bytes 131104 | tf_op jit(solution)/shard_map/ppermute | solution.py:540
  68.7 4.2 %shard_map.88 = (bf16[8,256,256]{2,1,0:T(8,128)(2,1)S(1)}, f32[8,64,256]{2,1,0:T(8,128)S(1)}, f32[8,64,256]{2,1,0:T(8,128)S(1)}, bf16[8,104,256]{2,1,0:T(8,128)(...) custom-call(s32[1]{0:T(128)} %bitcast.unused_s.me_s, bf16[256,256]{1,0:T(8,128)(2,1)S(1)} %get-tuple-element.40.refs_0_, ...), custom_call_target="tpu_custom_call" | custom-call | tf_op jit(solution)/shard_map/pallas_call | solution.py:48
  72.9 11.0 %all_to_all.27.refs_5_.share_ref = bf16[8,104,256]{2,1,0:T(8,128)(2,1)S(1)} all-to-all(bf16[8,104,256]{2,1,0:T(8,128)(2,1)S(1)} %get-tuple-element.53), channel_id=1, replica_groups=mesh['a'=2,'b'=2,'c'=2,'d'=4] {'b','d'}, dimensions={0} | all-to-all | bytes 851968 | tf_op jit(solution)/shard_map/all_to_all | solution.py:470
  83.9 5.4 %shard_map.89 = (bf16[384,128]{1,0:T(8,128)(2,1)S(1)}, bf16[384,128]{1,0:T(8,128)(2,1)S(1)}, bf16[384,128]{1,0:T(8,128)(2,1)S(1)}, bf16[384,128]{1,0:T(8,128)(2,...) custom-call(s32[1]{0:T(128)} %bitcast.unused_s.me_s, ...), custom_call_target="tpu_custom_call" | custom-call | tf_op jit(solution)/shard_map/pallas_call | solution.py:48
  89.4 0.1 collective-permute-start.8
  89.4 0.5 collective-permute-start.9
  90.0 2.1 %collective-permute-start.10 = (bf16[384,128]{1,0:T(8,128)(2,1)S(1)}, bf16[384,128]{1,0:T(8,128)(2,1)S(1)}, u32[]{:S(2)}, u32[]{:S(2)}) collective-permute-start(bf16[384,128]{1,0:T(8,128)(2,1)S(1)} %get-tuple-element.57), channel_id=1, source_target_pairs={{0,3},{1,2},{2,1},{3,0},{8,11},{9,10},{10,9},{11,8},{4,7},{5,6},{6... | collective-permute-start | bytes 294920 | tf_op jit(solution)/shard_map/ppermute | solution.py:540
  92.1 1.2 collective-permute-start.11
  93.3 0.0 collective-permute-start.12
  93.3 0.1 collective-permute-done.8.refs_1_
  93.4 1.4 %collective-permute-start.13 = (bf16[384,128]{1,0:T(8,128)(2,1)S(1)}, bf16[384,128]{1,0:T(8,128)(2,1)S(1)}, u32[]{:S(2)}, u32[]{:S(2)}) collective-permute-start(bf16[384,128]{1,0:T(8,128)(2,1)S(1)} %get-tuple-element.60), channel_id=1, source_target_pairs={{0,10},{1,11},{2,8},{3,9},{8,2},{9,3},{10,0},{11,1},{4,14},{5,15},... | collective-permute-start | bytes 294920 | tf_op jit(solution)/shard_map/ppermute | solution.py:540
  94.8 0.0 collective-permute-done.9.refs_2_
  94.8 2.1 %collective-permute-start.14 = (bf16[384,128]{1,0:T(8,128)(2,1)S(1)}, bf16[384,128]{1,0:T(8,128)(2,1)S(1)}, u32[]{:S(2)}, u32[]{:S(2)}) collective-permute-start(bf16[384,128]{1,0:T(8,128)(2,1)S(1)} %get-tuple-element.61), channel_id=1, source_target_pairs={{0,11},{1,10},{2,9},{3,8},{8,3},{9,2},{10,1},{11,0},{4,15},{5,14},... | collective-permute-start | bytes 294920 | tf_op jit(solution)/shard_map/ppermute | solution.py:540
  97.0 0.4 shard_map.90
  97.4 0.0 collective-permute-done.10.refs_3_
  97.4 0.0 collective-permute-done.11.refs_4_
  97.4 1.6 %collective-permute-done.12.refs_5_ = bf16[384,128]{1,0:T(8,128)(2,1)S(1)} collective-permute-done((bf16[384,128]{1,0:T(8,128)(2,1)S(1)}, bf16[384,128]{1,0:T(8,128)(2,1)S(1)}, u32[]{:S(2)}, u32[]{:S(2)}) %collective-permute-start.12) | collective-permute-done | bytes 98336 | tf_op jit(solution)/shard_map/ppermute | solution.py:540
  99.0 0.0 collective-permute-done.13.refs_6_
  99.0 2.7 %collective-permute-done.14.refs_7_ = bf16[384,128]{1,0:T(8,128)(2,1)S(1)} collective-permute-done((bf16[384,128]{1,0:T(8,128)(2,1)S(1)}, bf16[384,128]{1,0:T(8,128)(2,1)S(1)}, u32[]{:S(2)}, u32[]{:S(2)}) %collective-permute-start.14) | collective-permute-done | bytes 98336 | tf_op jit(solution)/shard_map/ppermute | solution.py:540
  101.7 2.3 %shard_map.91 = bf16[768,512]{1,0:T(8,128)(2,1)} custom-call(s32[1]{0:T(128)} %bitcast.unused_s.me_s, bf16[384,128]{1,0:T(8,128)(2,1)S(1)} %get-tuple-element.54.refs_0_, bf16[384,128]{1,0:T(8,128)(2,1)S(1)} %collective-permute-done.8.refs_1_, bf16[384,128]{1,0:T(8,128)(2,1)S(1)} %collective-permute-done.9.refs_2_, ...), custom_call_target="tpu_custom_call" | custom-call | tf_op jit(solution)/shard_map/pallas_call | solution.py:48
  104.0 3.4 %all-to-all-start.3 = ((bf16[32,24,512]{2,1,0:T(8,128)(2,1)}), bf16[32,24,512]{2,1,0:T(8,128)(2,1)S(1)}, u32[]{:S(2)}, u32[]{:S(2)}) async-start(bf16[32,24,512]{2,1,0:T(8,128)(2,1)} %bitcast.8), calls=%async_computation.3 | async-start | bytes 1572864 | tf_op jit(solution)/shard_map/all_to_all | solution.py:470
  107.4 4.4 %collective-permute-start.15 = (bf16[256,512]{1,0:T(8,128)(2,1)S(1)}, bf16[256,512]{1,0:T(8,128)(2,1)S(1)}, u32[]{:S(2)}, u32[]{:S(2)}) collective-permute-start(bf16[256,512]{1,0:T(8,128)(2,1)S(1)} %get-tuple-element.67), channel_id=1, source_target_pairs={{0,0},{4,8},{8,4},{12,12},{1,1},{5,9},{9,5},{13,13},{2,2},{6,10},{... | collective-permute-start | bytes 786440 | tf_op jit(solution)/shard_map/ppermute | solution.py:587
  111.9 21.3 %collective-permute-done.15.layer_ref = bf16[256,512]{1,0:T(8,128)(2,1)S(1)} collective-permute-done((bf16[256,512]{1,0:T(8,128)(2,1)S(1)}, bf16[256,512]{1,0:T(8,128)(2,1)S(1)}, u32[]{:S(2)}, u32[]{:S(2)}) %collective-permute-start.15) | collective-permute-done | bytes 262176 | tf_op jit(solution)/shard_map/ppermute | solution.py:587
  133.2 0.0 all-to-all-done.3
  133.2 4.4 %table_grad.1 = (bf16[4096,512]{1,0:T(8,128)(2,1)}, bf16[256,512]{1,0:T(8,128)(2,1)}) custom-call(f32[1,768]{1,0:T(1,128)S(1)} %get-tuple-element.38.asked_ref, bf16[768,512]{1,0:T(8,128)(2,1)S(1)} %bitcast.14, bf16[256,512]{1,0:T(8,128)(2,1)S(1)} %collective-permute-done.15.layer_ref), custom_call_target="tpu_custom_call" | custom-call | tf_op jit(solution)/shard_map/table_grad/pallas_call | solution.py:619
  (1 shorter events, 0.0 us)
Async XLA Ops:
  3.7 47.7 %copy-start = (bf16[512,2048]{1,0:T(8,128)(2,1)S(1)}, bf16[512,2048]{1,0:T(8,128)(2,1)}, u32[]{:S(2)}) copy-start(bf16[512,2048]{1,0:T(8,128)(2,1)} %refs_14_.1) | copy-start | bytes 6291460
  3.7 47.7 %copy-start.1 = (bf16[512,512]{1,0:T(8,128)(2,1)S(1)}, bf16[512,512]{1,0:T(8,128)(2,1)}, u32[]{:S(2)}) copy-start(bf16[512,512]{1,0:T(8,128)(2,1)} %wo_ref.3) | copy-start | bytes 1572868
  21.3 0.9 copy-start.4
  22.2 29.2 %all-to-all-start.1 = ((bf16[32,24,512]{2,1,0:T(8,128)(2,1)}), bf16[32,24,512]{2,1,0:T(8,128)(2,1)S(1)}, u32[]{:S(2)}, u32[]{:S(2)}) async-start(bf16[32,24,512]{2,1,0:T(8,128)(2,1)} %bitcast.20), calls=%async_computation.1 | async-start | bytes 1572864 | tf_op jit(solution)/shard_map/all_to_all | solution.py:470
  24.8 25.9 %collective-permute-start = (bf16[256,512]{1,0:T(8,128)(2,1)}, bf16[256,512]{1,0:T(8,128)(2,1)S(1)}, u32[]{:S(2)}, u32[]{:S(2)}) collective-permute-start(bf16[256,512]{1,0:T(8,128)(2,1)} %bitcast.23), channel_id=1, source_target_pairs={{0,0},{4,8},{8,4},{12,12},{1,1},{5,9},{9,5},{13,13},{2,2},{6,10},{... | collective-permute-start | bytes 786440 | tf_op jit(solution)/shard_map/ppermute | solution.py:502
  50.7 0.7 copy-start.2
  51.5 1.0 copy-start.3
  54.5 4.3 %collective-permute-start.1 = (bf16[256,256]{1,0:T(8,128)(2,1)S(1)}, bf16[256,256]{1,0:T(8,128)(2,1)S(1)}, u32[]{:S(2)}, u32[]{:S(2)}) collective-permute-start(bf16[256,256]{1,0:T(8,128)(2,1)S(1)} %get-tuple-element.41), channel_id=1, source_target_pairs={{0,1},{1,0},{2,3},{3,2},{8,9},{9,8},{10,11},{11,10},{4,5},{5,4},{6... | collective-permute-start | bytes 393224 | tf_op jit(solution)/shard_map/ppermute | solution.py:540
  55.7 5.5 %collective-permute-start.2 = (bf16[256,256]{1,0:T(8,128)(2,1)S(1)}, bf16[256,256]{1,0:T(8,128)(2,1)S(1)}, u32[]{:S(2)}, u32[]{:S(2)}) collective-permute-start(bf16[256,256]{1,0:T(8,128)(2,1)S(1)} %get-tuple-element.42), channel_id=1, source_target_pairs={{0,2},{1,3},{2,0},{3,1},{8,10},{9,11},{10,8},{11,9},{4,6},{5,7},{6... | collective-permute-start | bytes 393224 | tf_op jit(solution)/shard_map/ppermute | solution.py:540
  55.7 7.4 %collective-permute-start.3 = (bf16[256,256]{1,0:T(8,128)(2,1)S(1)}, bf16[256,256]{1,0:T(8,128)(2,1)S(1)}, u32[]{:S(2)}, u32[]{:S(2)}) collective-permute-start(bf16[256,256]{1,0:T(8,128)(2,1)S(1)} %get-tuple-element.43), channel_id=1, source_target_pairs={{0,3},{1,2},{2,1},{3,0},{8,11},{9,10},{10,9},{11,8},{4,7},{5,6},{6... | collective-permute-start | bytes 393224 | tf_op jit(solution)/shard_map/ppermute | solution.py:540
  57.2 6.0 %collective-permute-start.4 = (bf16[256,256]{1,0:T(8,128)(2,1)S(1)}, bf16[256,256]{1,0:T(8,128)(2,1)S(1)}, u32[]{:S(2)}, u32[]{:S(2)}) collective-permute-start(bf16[256,256]{1,0:T(8,128)(2,1)S(1)} %get-tuple-element.44), channel_id=1, source_target_pairs={{0,8},{1,9},{2,10},{3,11},{8,0},{9,1},{10,2},{11,3},{4,12},{5,13},... | collective-permute-start | bytes 393224 | tf_op jit(solution)/shard_map/ppermute | solution.py:540
  57.2 8.4 %collective-permute-start.5 = (bf16[256,256]{1,0:T(8,128)(2,1)S(1)}, bf16[256,256]{1,0:T(8,128)(2,1)S(1)}, u32[]{:S(2)}, u32[]{:S(2)}) collective-permute-start(bf16[256,256]{1,0:T(8,128)(2,1)S(1)} %get-tuple-element.45), channel_id=1, source_target_pairs={{0,9},{1,8},{2,11},{3,10},{8,1},{9,0},{10,3},{11,2},{4,13},{5,12},... | collective-permute-start | bytes 393224 | tf_op jit(solution)/shard_map/ppermute | solution.py:540
  58.8 6.8 %collective-permute-start.6 = (bf16[256,256]{1,0:T(8,128)(2,1)S(1)}, bf16[256,256]{1,0:T(8,128)(2,1)S(1)}, u32[]{:S(2)}, u32[]{:S(2)}) collective-permute-start(bf16[256,256]{1,0:T(8,128)(2,1)S(1)} %get-tuple-element.46), channel_id=1, source_target_pairs={{0,10},{1,11},{2,8},{3,9},{8,2},{9,3},{10,0},{11,1},{4,14},{5,15},... | collective-permute-start | bytes 393224 | tf_op jit(solution)/shard_map/ppermute | solution.py:540
  61.2 7.5 %collective-permute-start.7 = (bf16[256,256]{1,0:T(8,128)(2,1)S(1)}, bf16[256,256]{1,0:T(8,128)(2,1)S(1)}, u32[]{:S(2)}, u32[]{:S(2)}) collective-permute-start(bf16[256,256]{1,0:T(8,128)(2,1)S(1)} %get-tuple-element.47), channel_id=1, source_target_pairs={{0,11},{1,10},{2,9},{3,8},{8,3},{9,2},{10,1},{11,0},{4,15},{5,14},... | collective-permute-start | bytes 393224 | tf_op jit(solution)/shard_map/ppermute | solution.py:540
  89.4 4.0 %collective-permute-start.8 = (bf16[384,128]{1,0:T(8,128)(2,1)S(1)}, bf16[384,128]{1,0:T(8,128)(2,1)S(1)}, u32[]{:S(2)}, u32[]{:S(2)}) collective-permute-start(bf16[384,128]{1,0:T(8,128)(2,1)S(1)} %get-tuple-element.55), channel_id=1, source_target_pairs={{0,1},{1,0},{2,3},{3,2},{8,9},{9,8},{10,11},{11,10},{4,5},{5,4},{6... | collective-permute-start | bytes 294920 | tf_op jit(solution)/shard_map/ppermute | solution.py:540
  89.4 5.4 %collective-permute-start.9 = (bf16[384,128]{1,0:T(8,128)(2,1)S(1)}, bf16[384,128]{1,0:T(8,128)(2,1)S(1)}, u32[]{:S(2)}, u32[]{:S(2)}) collective-permute-start(bf16[384,128]{1,0:T(8,128)(2,1)S(1)} %get-tuple-element.56), channel_id=1, source_target_pairs={{0,2},{1,3},{2,0},{3,1},{8,10},{9,11},{10,8},{11,9},{4,6},{5,7},{6... | collective-permute-start | bytes 294920 | tf_op jit(solution)/shard_map/ppermute | solution.py:540
  90.0 7.4 %collective-permute-start.10 = (bf16[384,128]{1,0:T(8,128)(2,1)S(1)}, bf16[384,128]{1,0:T(8,128)(2,1)S(1)}, u32[]{:S(2)}, u32[]{:S(2)}) collective-permute-start(bf16[384,128]{1,0:T(8,128)(2,1)S(1)} %get-tuple-element.57), channel_id=1, source_target_pairs={{0,3},{1,2},{2,1},{3,0},{8,11},{9,10},{10,9},{11,8},{4,7},{5,6},{6... | collective-permute-start | bytes 294920 | tf_op jit(solution)/shard_map/ppermute | solution.py:540
  92.1 5.3 %collective-permute-start.11 = (bf16[384,128]{1,0:T(8,128)(2,1)S(1)}, bf16[384,128]{1,0:T(8,128)(2,1)S(1)}, u32[]{:S(2)}, u32[]{:S(2)}) collective-permute-start(bf16[384,128]{1,0:T(8,128)(2,1)S(1)} %get-tuple-element.58), channel_id=1, source_target_pairs={{0,8},{1,9},{2,10},{3,11},{8,0},{9,1},{10,2},{11,3},{4,12},{5,13},... | collective-permute-start | bytes 294920 | tf_op jit(solution)/shard_map/ppermute | solution.py:540
  93.3 5.7 %collective-permute-start.12 = (bf16[384,128]{1,0:T(8,128)(2,1)S(1)}, bf16[384,128]{1,0:T(8,128)(2,1)S(1)}, u32[]{:S(2)}, u32[]{:S(2)}) collective-permute-start(bf16[384,128]{1,0:T(8,128)(2,1)S(1)} %get-tuple-element.59), channel_id=1, source_target_pairs={{0,9},{1,8},{2,11},{3,10},{8,1},{9,0},{10,3},{11,2},{4,13},{5,12},... | collective-permute-start | bytes 294920 | tf_op jit(solution)/shard_map/ppermute | solution.py:540
  93.4 5.6 %collective-permute-start.13 = (bf16[384,128]{1,0:T(8,128)(2,1)S(1)}, bf16[384,128]{1,0:T(8,128)(2,1)S(1)}, u32[]{:S(2)}, u32[]{:S(2)}) collective-permute-start(bf16[384,128]{1,0:T(8,128)(2,1)S(1)} %get-tuple-element.60), channel_id=1, source_target_pairs={{0,10},{1,11},{2,8},{3,9},{8,2},{9,3},{10,0},{11,1},{4,14},{5,15},... | collective-permute-start | bytes 294920 | tf_op jit(solution)/shard_map/ppermute | solution.py:540
  94.8 6.9 %collective-permute-start.14 = (bf16[384,128]{1,0:T(8,128)(2,1)S(1)}, bf16[384,128]{1,0:T(8,128)(2,1)S(1)}, u32[]{:S(2)}, u32[]{:S(2)}) collective-permute-start(bf16[384,128]{1,0:T(8,128)(2,1)S(1)} %get-tuple-element.61), channel_id=1, source_target_pairs={{0,11},{1,10},{2,9},{3,8},{8,3},{9,2},{10,1},{11,0},{4,15},{5,14},... | collective-permute-start | bytes 294920 | tf_op jit(solution)/shard_map/ppermute | solution.py:540
  104.0 29.2 %all-to-all-start.3 = ((bf16[32,24,512]{2,1,0:T(8,128)(2,1)}), bf16[32,24,512]{2,1,0:T(8,128)(2,1)S(1)}, u32[]{:S(2)}, u32[]{:S(2)}) async-start(bf16[32,24,512]{2,1,0:T(8,128)(2,1)} %bitcast.8), calls=%async_computation.3 | async-start | bytes 1572864 | tf_op jit(solution)/shard_map/all_to_all | solution.py:470
  107.4 25.8 %collective-permute-start.15 = (bf16[256,512]{1,0:T(8,128)(2,1)S(1)}, bf16[256,512]{1,0:T(8,128)(2,1)S(1)}, u32[]{:S(2)}, u32[]{:S(2)}) collective-permute-start(bf16[256,512]{1,0:T(8,128)(2,1)S(1)} %get-tuple-element.67), channel_id=1, source_target_pairs={{0,0},{4,8},{8,4},{12,12},{1,1},{5,9},{9,5},{13,13},{2,2},{6,10},{... | collective-permute-start | bytes 786440 | tf_op jit(solution)/shard_map/ppermute | solution.py:587

commit v4 on v3

--- a/solution.py
+++ b/solution.py
@@ -216,11 +216,11 @@
     return iota((rows, rows), 0) <= iota((rows, rows), 1)
 
 
-def forward_kernel(ready, group, me_s, *refs):
+def forward_kernel(group, me_s, *refs):
     pieces, refs = refs[:group], refs[group:]
-    x_ref, att_ref, dz_ref, share_ref, wgt_ref = refs[:5]
-    slope_ref = refs[5] if ready else None
-    vt_scr, keys_scr, stat_ref = refs[-3:]
+    x_ref, att_ref, dz_ref, wgt_ref = refs[:4]
+    shares = refs[4 : 4 + group]
+    vt_scr, keys_scr, stat_ref, share_ref = refs[-4:]
     take_in(me_s, pieces, x_ref)
     blocks, rows, cols = x_ref.shape
     head = cols // 4
@@ -234,15 +234,11 @@
         queries_t = (x_ref[b, :, 0:head].astype(f32) * (0.5 * scale)).T.astype(bf16)
         above = b * rows
         upto = above + rows
-        wgt, slope = weight_tile(keys_scr[:upto, :], queries_t)
+        wgt, _ = weight_tile(keys_scr[:upto, :], queries_t)
         place = b * (b + 1) // 2 * rows
         if above:
             wgt_ref[place : place + above, :] = wgt[:above].astype(bf16)
         wgt_ref[place + above : place + upto, :] = jnp.where(causal, wgt[above:], 0.0).astype(bf16)
-        if ready:
-            if above:
-                slope_ref[place : place + above, :] = slope[:above]
-            slope_ref[place + above : place + upto, :] = jnp.where(causal, slope[above:], 0.0)
         att = dot(vt_scr[:, :upto], wgt_ref[place : place + upto, :])
         dz = x_ref[b, :, 3 * head :].astype(f32).T
         att_ref[b] = att
@@ -261,6 +257,25 @@
     for g in range(blocks):
         for n, stat in enumerate([high, low] + others):
             share_ref[g, n * blocks : (n + 1) * blocks, :] = stat
+    hand_out(me_s, shares, share_ref)
+
+
+def slope_kernel(x_ref, slope_ref, keys_scr):
+    blocks, rows, cols = x_ref.shape
+    head = cols // 4
+    scale = head ** (-0.5)
+    causal = causal_mask(rows)
+    for b in range(blocks):
+        keys_scr[b * rows : (b + 1) * rows, :] = x_ref[b, :, head : 2 * head]
+    for b in range(blocks):
+        above = b * rows
+        upto = above + rows
+        place = b * (b + 1) // 2 * rows
+        queries_t = (x_ref[b, :, 0:head].astype(f32) * (0.5 * scale)).T.astype(bf16)
+        _, slope = weight_tile(keys_scr[:upto, :], queries_t)
+        if above:
+            slope_ref[place : place + above, :] = slope[:above]
+        slope_ref[place + above : place + upto, :] = jnp.where(causal, slope[above:], 0.0)
 
 
 def combine(stats_ref, copies, blocks, head):
@@ -284,10 +299,10 @@
     return mean, offs, inv, dz_sum * (1.0 / width), dz_att * inv * (1.0 / width)
 
 
-def output_kernel(
-    copies, me_s, share_ref, mail_ref, gate_ref, emb_ref, wo_ref, norm_ref, layer_ref, row_scr
-):
-    group = share_ref.shape[0]
+def output_kernel(copies, group, me_s, *refs):
+    pieces, refs = refs[:group], refs[group:]
+    mail_ref, gate_ref, emb_ref, wo_ref, norm_ref, layer_ref, row_scr, share_ref = refs
+    take_in(me_s, pieces, share_ref)
     width = emb_ref.shape[1]
     head = width // HEADS
     unused, offs, inv, *others = combine(share_ref, copies, group, head)
@@ -311,16 +326,17 @@
 
 
 def backward_kernel(copies, ready, group, me_s, *refs):
+    shares, refs = refs[:group], refs[group:]
     if ready:
-        x_ref, wgt_ref, slope_ref, att_ref, dz_ref, stats_ref = refs[:6]
+        x_ref, wgt_ref, slope_ref, att_ref, dz_ref = refs[:5]
     else:
-        x_ref, wgt_ref, att_ref, dz_ref, stats_ref = refs[:5]
+        x_ref, wgt_ref, att_ref, dz_ref = refs[:4]
         qt_scr = refs[-1]
-    refs = refs[5 + ready :]
+    refs = refs[4 + ready :]
     pieces = refs[:group]
-    out_ref, da_scr, dat_scr, q_scr, keys_scr, keyst_scr, values_scr, dq_scr, dk_scr, dv_scr = refs[
-        group : group + 10
-    ]
+    stats_ref, out_ref, da_scr, dat_scr, q_scr = refs[group : group + 5]
+    keys_scr, keyst_scr, values_scr, dq_scr, dk_scr, dv_scr = refs[group + 5 : group + 11]
+    take_in(me_s, shares, stats_ref)
     blocks, rows, cols = x_ref.shape
     head = cols // 4
     scale = head ** (-0.5)
@@ -558,34 +574,44 @@
     length = group * count
     tiles = group * (group + 1) // 2 * count
     ready = tiles * count * 6 <= 16 * 1024 * 1024
-    x, att, dz, share, *weights = kernel_call(
-        functools.partial(forward_kernel, ready, group),
+    share_piece = ((5 * group + head, count), bf16)
+    x, att, dz, *weights = kernel_call(
+        functools.partial(forward_kernel, group),
         (
             ((group, count, 4 * head), bf16),
             ((group, head, count), f32),
             ((group, head, count), f32),
-            ((group, 5 * group + head, count), bf16),
         )
         + (((tiles, count), bf16),)
-        + (((tiles, count), f32),) * ready,
+        + (share_piece,) * group,
         mine,
         scratch=[
             pltpu.VMEM((head, length), bf16),
             pltpu.VMEM((length, head), bf16),
             pltpu.VMEM((4, group, count), f32),
+            pltpu.VMEM((group, *share_piece[0]), bf16),
         ],
         numbers=(me,),
     )
-    stats = all_to_all(share, GROUP)
+    stats = exchange(weights[-group:])
+    weights = weights[:-group]
+    if ready:
+        weights += kernel_call(
+            slope_kernel, (((tiles, count), f32),), (x,), scratch=[pltpu.VMEM((length, head), bf16)]
+        )
     att_n, layer_out = kernel_call(
-        functools.partial(output_kernel, copies),
+        functools.partial(output_kernel, copies, group),
         (((count, width), f32), ((count, width), bf16)),
-        (stats, mail, gate, emb, output_proj),
-        scratch=[pltpu.VMEM((HEADS + 1, group, count), f32)],
+        (*stats, mail, gate, emb, output_proj),
+        scratch=[
+            pltpu.VMEM((HEADS + 1, group, count), f32),
+            pltpu.VMEM((group, *share_piece[0]), bf16),
+        ],
         numbers=(me,),
     )
     layer_out = moved(layer_out)
     scratch = [
+        pltpu.VMEM((group, *share_piece[0]), bf16),
         pltpu.VMEM((group, *back_piece[0]), bf16),
         pltpu.VMEM((group, count, head), bf16),
         pltpu.VMEM((group, head, count), bf16),
@@ -602,7 +628,7 @@
     grads = kernel_call(
         functools.partial(backward_kernel, copies, ready, group),
         (back_piece,) * group,
-        (x, *weights, att, dz, stats),
+        (*stats, x, *weights, att, dz),
         scratch=scratch,
         numbers=(me,),
     )

time: 138 us -> 138 us (level)
  blocking collectives: 25 us -> 14 us
  starting transfers between devices: 27.2 us -> 34.5 us
  Pallas kernels: 24.8 us -> 27.6 us
    all_to_all x2 -> x1, blocking collectives: 25 us -> 14 us  [all_to_all(): return lax.all_to_all(pieces, axes, split_axis=0, concat_axis=0, tiled=True)]
    ppermute x14 -> x21, starting transfers between devices: 12.2 us -> 19.2 us  [exchange(): lax.ppermute(pieces[k], GROUP, [(g, g ^ k) for g in range(group)])]
    pallas_call x6 -> x7, Pallas kernels: 17.9 us -> 20.7 us  [kernel_call(): pl.pallas_call(kernel, out_shape=tuple((pltpu.VMEM(shape, dtype) for shap...]
    ppermute x14 -> x21, waiting for transfers between devices: 13.9 us -> 14.6 us  [exchange(): lax.ppermute(pieces[k], GROUP, [(g, g ^ k) for g in range(group)])]
  transfers between devices with their start and end apart: 18 -> 25, of which waited for: 9 -> 9; matrix products, arithmetic and copies ran while one was open for 0% -> 0% of each run, Pallas kernels for 0% -> 2%
where the time goes in v4:
time: 138 us; the launch traced here: 137 us
  waiting for transfers between devices  57.1 us (41%)
  starting transfers between devices  34.5 us (25%)
  Pallas kernels  27.6 us (20%)
  blocking collectives  14 us (10%)
  local copies, waits for them, and re-layouts  2.6 us (2%)
  between operations  1.68 us (1%)
    ppermute x1, waiting for transfers between devices, local(): layer_out = moved(layer_out)  21.3 us
    ppermute x1, waiting for transfers between devices, local(): cot = moved(out_cotangent[0])  21.1 us
    pallas_call x7, Pallas kernels, kernel_call(): pl.pallas_call(kernel, out_shape=tuple((pltpu.VMEM(shape, dtype) for shap...  20.7 us
    ppermute x21, starting transfers between devices, exchange(): lax.ppermute(pieces[k], GROUP, [(g, g ^ k) for g in range(group)])  19.2 us
    ppermute x21, waiting for transfers between devices, exchange(): lax.ppermute(pieces[k], GROUP, [(g, g ^ k) for g in range(group)])  14.6 us
    all_to_all x1, blocking collectives, all_to_all(): return lax.all_to_all(pieces, axes, split_axis=0, concat_axis=0, tiled=True)  14 us
    all_to_all x2, starting transfers between devices, all_to_all(): return lax.all_to_all(pieces, axes, split_axis=0, concat_axis=0, tiled=True)  6.12 us
    ppermute x1, starting transfers between devices, local(): cot = moved(out_cotangent[0])  4.75 us
  transfers between devices with their start and end apart: 25, of which 9 were waited for; matrix products, arithmetic and copies ran while one was open for 0% of the time, Pallas kernels for 2%

profile of v4, /device:TPU:1, one launch (start us, length us, event | category | flops | bytes accessed | tf_op | source)
XLA Modules:
  0.0 137.4 jit_solution(17755323065407271600)
XLA Ops:
  1.3 2.4 %requests.1 = (s32[32,384]{1,0:T(8,128)S(1)}, bf16[4096,512]{1,0:T(8,128)(2,1)S(1)}) custom-call(s32[1]{0:T(128)} %bitcast.unused_s.me_s, s32[1]{0:T(128)} %bitcast.1.block_s, s32[1]{0:T(128)} %bitcast.2.twin_s, s32[1]{0:T(128)S(6)} %copy.13.length_s, s32[1,256]{1,0:T(1,128)} %ids_hbm.1, s32[1024,128]{1,0:T(8,128)} %bitcast.22, bf16[4096,512]{1,0:T(8,128)(2,1)} %table_hbm.1), custom_call_target="tpu_custom_call" | custom-call | tf_op jit(solution)/shard_map/requests/pallas_call | solution.py:519
  3.7 0.0 copy-start
  3.7 0.0 copy-start.1
  3.7 0.1 copy.9
  3.8 14.0 %all_to_all.21 = s32[32,1,384]{2,1,0:T(1,128)S(1)} all-to-all(s32[32,1,384]{2,1,0:T(1,128)S(1)} %copy.9), channel_id=1, replica_groups=mesh['a'=2,'b'=2,'c'=2,'d'=4] {'a','b','c','d'}, dimensions={0} | all-to-all | bytes 98304 | tf_op jit(solution)/shard_map/all_to_all | solution.py:486
  17.8 3.5 %shard_map.86 = (bf16[768,512]{1,0:T(8,128)(2,1)S(1)}, f32[1,768]{1,0:T(1,128)S(1)}) custom-call(s32[32,384]{1,0:T(8,128)S(1)} %bitcast.16, bf16[4096,512]{1,0:T(8,128)(2,1)S(1)} %get-tuple-element.43.table_ref), custom_call_target="tpu_custom_call" | custom-call | tf_op jit(solution)/shard_map/pallas_call | solution.py:48
  21.3 0.0 copy-start.5
  21.3 0.9 copy-done.5
  22.2 2.6 %all-to-all-start.1 = ((bf16[32,24,512]{2,1,0:T(8,128)(2,1)}), bf16[32,24,512]{2,1,0:T(8,128)(2,1)S(1)}, u32[]{:S(2)}, u32[]{:S(2)}) async-start(bf16[32,24,512]{2,1,0:T(8,128)(2,1)} %bitcast.20), calls=%async_computation.1 | async-start | bytes 1572864 | tf_op jit(solution)/shard_map/all_to_all | solution.py:486
  24.8 4.7 %collective-permute-start = (bf16[256,512]{1,0:T(8,128)(2,1)}, bf16[256,512]{1,0:T(8,128)(2,1)S(1)}, u32[]{:S(2)}, u32[]{:S(2)}) collective-permute-start(bf16[256,512]{1,0:T(8,128)(2,1)} %bitcast.23), channel_id=1, source_target_pairs={{0,0},{4,8},{8,4},{12,12},{1,1},{5,9},{9,5},{13,13},{2,2},{6,10},{... | collective-permute-start | bytes 786440 | tf_op jit(solution)/shard_map/ppermute | solution.py:518
  29.6 21.1 %collective-permute-done.cot_ref.refs_13_ = bf16[256,512]{1,0:T(8,128)(2,1)S(1)} collective-permute-done((bf16[256,512]{1,0:T(8,128)(2,1)}, bf16[256,512]{1,0:T(8,128)(2,1)S(1)}, u32[]{:S(2)}, u32[]{:S(2)}) %collective-permute-start) | collective-permute-done | bytes 262176 | tf_op jit(solution)/shard_map/ppermute | solution.py:518
  50.7 0.7 copy-done.2
  51.4 0.0 all-to-all-done.1
  51.5 0.0 copy-start.3
  51.5 0.9 copy-done.3
  52.4 2.0 %shard_map.87 = (bf16[256,512]{1,0:T(8,128)(2,1)S(1)}, f32[256,2048]{1,0:T(8,128)S(1)}, f32[256,512]{1,0:T(8,128)S(1)}, f32[256,512]{1,0:T(8,128)S(1)}, bf16[256...) custom-call(s32[1]{0:T(128)} %bitcast.unused_s.me_s, ...), custom_call_target="tpu_custom_call" | custom-call | tf_op jit(solution)/shard_map/pallas_call | solution.py:48
  54.4 1.3 collective-permute-start.1
  55.7 0.0 collective-permute-start.2
  55.7 1.4 %collective-permute-start.3 = (bf16[256,256]{1,0:T(8,128)(2,1)S(1)}, bf16[256,256]{1,0:T(8,128)(2,1)S(1)}, u32[]{:S(2)}, u32[]{:S(2)}) collective-permute-start(bf16[256,256]{1,0:T(8,128)(2,1)S(1)} %get-tuple-element.49), channel_id=1, source_target_pairs={{0,3},{1,2},{2,1},{3,0},{8,11},{9,10},{10,9},{11,8},{4,7},{5,6},{6... | collective-permute-start | bytes 393224 | tf_op jit(solution)/shard_map/ppermute | solution.py:556
  57.2 0.0 collective-permute-start.4
  57.2 1.6 %collective-permute-start.5 = (bf16[256,256]{1,0:T(8,128)(2,1)S(1)}, bf16[256,256]{1,0:T(8,128)(2,1)S(1)}, u32[]{:S(2)}, u32[]{:S(2)}) collective-permute-start(bf16[256,256]{1,0:T(8,128)(2,1)S(1)} %get-tuple-element.51), channel_id=1, source_target_pairs={{0,9},{1,8},{2,11},{3,10},{8,1},{9,0},{10,3},{11,2},{4,13},{5,12},... | collective-permute-start | bytes 393224 | tf_op jit(solution)/shard_map/ppermute | solution.py:556
  58.8 0.0 collective-permute-done.1.refs_1_
  58.8 0.0 collective-permute-start.6
  58.8 2.4 %collective-permute-done.2.refs_2_ = bf16[256,256]{1,0:T(8,128)(2,1)S(1)} collective-permute-done((bf16[256,256]{1,0:T(8,128)(2,1)S(1)}, bf16[256,256]{1,0:T(8,128)(2,1)S(1)}, u32[]{:S(2)}, u32[]{:S(2)}) %collective-permute-start.2) | collective-permute-done | bytes 131104 | tf_op jit(solution)/shard_map/ppermute | solution.py:556
  61.2 0.4 collective-permute-start.7
  61.6 1.5 %collective-permute-done.3.refs_3_ = bf16[256,256]{1,0:T(8,128)(2,1)S(1)} collective-permute-done((bf16[256,256]{1,0:T(8,128)(2,1)S(1)}, bf16[256,256]{1,0:T(8,128)(2,1)S(1)}, u32[]{:S(2)}, u32[]{:S(2)}) %collective-permute-start.3) | collective-permute-done | bytes 131104 | tf_op jit(solution)/shard_map/ppermute | solution.py:556
  63.1 0.0 collective-permute-done.4.refs_4_
  63.1 2.4 %collective-permute-done.5.refs_5_ = bf16[256,256]{1,0:T(8,128)(2,1)S(1)} collective-permute-done((bf16[256,256]{1,0:T(8,128)(2,1)S(1)}, bf16[256,256]{1,0:T(8,128)(2,1)S(1)}, u32[]{:S(2)}, u32[]{:S(2)}) %collective-permute-start.5) | collective-permute-done | bytes 131104 | tf_op jit(solution)/shard_map/ppermute | solution.py:556
  65.5 0.0 collective-permute-done.6.refs_6_
  65.5 3.2 %collective-permute-done.7.refs_7_ = bf16[256,256]{1,0:T(8,128)(2,1)S(1)} collective-permute-done((bf16[256,256]{1,0:T(8,128)(2,1)S(1)}, bf16[256,256]{1,0:T(8,128)(2,1)S(1)}, u32[]{:S(2)}, u32[]{:S(2)}) %collective-permute-start.7) | collective-permute-done | bytes 131104 | tf_op jit(solution)/shard_map/ppermute | solution.py:556
  68.7 4.0 %shard_map.88 = (bf16[8,256,256]{2,1,0:T(8,128)(2,1)S(1)}, f32[8,64,256]{2,1,0:T(8,128)S(1)}, f32[8,64,256]{2,1,0:T(8,128)S(1)}, bf16[9216,256]{1,0:T(8,128)(2,1...) custom-call(s32[1]{0:T(128)} %bitcast.unused_s.me_s, ...), custom_call_target="tpu_custom_call" | custom-call | tf_op jit(solution)/shard_map/pallas_call | solution.py:48
  72.7 0.2 collective-permute-start.8
  72.9 0.2 collective-permute-start.9
  73.0 2.4 %collective-permute-start.10 = (bf16[104,256]{1,0:T(8,128)(2,1)S(1)}, bf16[104,256]{1,0:T(8,128)(2,1)S(1)}, u32[]{:S(2)}, u32[]{:S(2)}) collective-permute-start(bf16[104,256]{1,0:T(8,128)(2,1)S(1)} %get-tuple-element.57), channel_id=1, source_target_pairs={{0,3},{1,2},{2,1},{3,0},{8,11},{9,10},{10,9},{11,8},{4,7},{5,6},{6... | collective-permute-start | bytes 159752 | tf_op jit(solution)/shard_map/ppermute | solution.py:556
  75.4 1.4 %collective-permute-start.11 = (bf16[104,256]{1,0:T(8,128)(2,1)S(1)}, bf16[104,256]{1,0:T(8,128)(2,1)S(1)}, u32[]{:S(2)}, u32[]{:S(2)}) collective-permute-start(bf16[104,256]{1,0:T(8,128)(2,1)S(1)} %get-tuple-element.58), channel_id=1, source_target_pairs={{0,8},{1,9},{2,10},{3,11},{8,0},{9,1},{10,2},{11,3},{4,12},{5,13},... | collective-permute-start | bytes 159752 | tf_op jit(solution)/shard_map/ppermute | solution.py:556
  76.8 0.4 collective-permute-start.12
  77.2 0.0 collective-permute-done.8.refs_1_
  77.2 0.5 collective-permute-start.13
  77.7 0.0 collective-permute-done.9.refs_2_
  77.7 1.9 %collective-permute-start.14 = (bf16[104,256]{1,0:T(8,128)(2,1)S(1)}, bf16[104,256]{1,0:T(8,128)(2,1)S(1)}, u32[]{:S(2)}, u32[]{:S(2)}) collective-permute-start(bf16[104,256]{1,0:T(8,128)(2,1)S(1)} %get-tuple-element.61), channel_id=1, source_target_pairs={{0,11},{1,10},{2,9},{3,8},{8,3},{9,2},{10,1},{11,0},{4,15},{5,14},... | collective-permute-start | bytes 159752 | tf_op jit(solution)/shard_map/ppermute | solution.py:556
  79.6 2.7 %shard_map.89.refs_10_ = f32[9216,256]{1,0:T(8,128)S(1)} custom-call(bf16[8,256,256]{2,1,0:T(8,128)(2,1)S(1)} %get-tuple-element.62.x_ref.refs_8_), custom_call_target="tpu_custom_call" | custom-call | tf_op jit(solution)/shard_map/pallas_call | solution.py:48
  82.3 0.0 collective-permute-done.10.refs_3_
  82.3 0.0 collective-permute-done.11.refs_4_
  82.3 0.0 collective-permute-done.12.refs_5_
  82.3 0.0 collective-permute-done.13.refs_6_
  82.3 0.7 collective-permute-done.14.refs_7_
  83.1 5.7 %shard_map.90 = (bf16[384,128]{1,0:T(8,128)(2,1)S(1)}, bf16[384,128]{1,0:T(8,128)(2,1)S(1)}, bf16[384,128]{1,0:T(8,128)(2,1)S(1)}, bf16[384,128]{1,0:T(8,128)(2,...) custom-call(s32[1]{0:T(128)} %bitcast.unused_s.me_s, ...), custom_call_target="tpu_custom_call" | custom-call | tf_op jit(solution)/shard_map/pallas_call | solution.py:48
  88.8 0.5 collective-permute-start.15
  89.3 1.0 collective-permute-start.16
  90.3 1.2 collective-permute-start.17
  91.5 1.2 collective-permute-start.18
  92.7 0.3 collective-permute-start.19
  93.0 0.0 collective-permute-done.15.refs_1_
  93.0 1.4 %collective-permute-start.20 = (bf16[384,128]{1,0:T(8,128)(2,1)S(1)}, bf16[384,128]{1,0:T(8,128)(2,1)S(1)}, u32[]{:S(2)}, u32[]{:S(2)}) collective-permute-start(bf16[384,128]{1,0:T(8,128)(2,1)S(1)} %get-tuple-element.72), channel_id=1, source_target_pairs={{0,10},{1,11},{2,8},{3,9},{8,2},{9,3},{10,0},{11,1},{4,14},{5,15},... | collective-permute-start | bytes 294920 | tf_op jit(solution)/shard_map/ppermute | solution.py:556
  94.4 1.9 %collective-permute-start.21 = (bf16[384,128]{1,0:T(8,128)(2,1)S(1)}, bf16[384,128]{1,0:T(8,128)(2,1)S(1)}, u32[]{:S(2)}, u32[]{:S(2)}) collective-permute-start(bf16[384,128]{1,0:T(8,128)(2,1)S(1)} %get-tuple-element.73), channel_id=1, source_target_pairs={{0,11},{1,10},{2,9},{3,8},{8,3},{9,2},{10,1},{11,0},{4,15},{5,14},... | collective-permute-start | bytes 294920 | tf_op jit(solution)/shard_map/ppermute | solution.py:556
  96.3 0.4 shard_map.91
  96.8 1.7 %collective-permute-done.19.refs_5_ = bf16[384,128]{1,0:T(8,128)(2,1)S(1)} collective-permute-done((bf16[384,128]{1,0:T(8,128)(2,1)S(1)}, bf16[384,128]{1,0:T(8,128)(2,1)S(1)}, u32[]{:S(2)}, u32[]{:S(2)}) %collective-permute-start.19) | collective-permute-done | bytes 98336 | tf_op jit(solution)/shard_map/ppermute | solution.py:556
  98.5 0.0 collective-permute-done.20.refs_6_
  98.5 2.6 %collective-permute-done.21.refs_7_ = bf16[384,128]{1,0:T(8,128)(2,1)S(1)} collective-permute-done((bf16[384,128]{1,0:T(8,128)(2,1)S(1)}, bf16[384,128]{1,0:T(8,128)(2,1)S(1)}, u32[]{:S(2)}, u32[]{:S(2)}) %collective-permute-start.21) | collective-permute-done | bytes 98336 | tf_op jit(solution)/shard_map/ppermute | solution.py:556
  101.1 2.4 %shard_map.92 = bf16[768,512]{1,0:T(8,128)(2,1)} custom-call(s32[1]{0:T(128)} %bitcast.unused_s.me_s, bf16[384,128]{1,0:T(8,128)(2,1)S(1)} %get-tuple-element.66.refs_0_, bf16[384,128]{1,0:T(8,128)(2,1)S(1)} %collective-permute-done.15.refs_1_, bf16[384,128]{1,0:T(8,128)(2,1)S(1)} %collective-permute-done.16.refs_2_, ...), custom_call_target="tpu_custom_call" | custom-call | tf_op jit(solution)/shard_map/pallas_call | solution.py:48
  103.5 3.5 %all-to-all-start.2 = ((bf16[32,24,512]{2,1,0:T(8,128)(2,1)}), bf16[32,24,512]{2,1,0:T(8,128)(2,1)S(1)}, u32[]{:S(2)}, u32[]{:S(2)}) async-start(bf16[32,24,512]{2,1,0:T(8,128)(2,1)} %bitcast.8), calls=%async_computation.2 | async-start | bytes 1572864 | tf_op jit(solution)/shard_map/all_to_all | solution.py:486
  107.0 4.4 %collective-permute-start.22 = (bf16[256,512]{1,0:T(8,128)(2,1)}, bf16[256,512]{1,0:T(8,128)(2,1)S(1)}, u32[]{:S(2)}, u32[]{:S(2)}) collective-permute-start(bf16[256,512]{1,0:T(8,128)(2,1)} %copy-done.6), channel_id=1, source_target_pairs={{0,0},{4,8},{8,4},{12,12},{1,1},{5,9},{9,5},{13,13},{2,2},{6,10},{... | collective-permute-start | bytes 786440 | tf_op jit(solution)/shard_map/ppermute | solution.py:612
  111.5 21.3 %collective-permute-done.22.layer_ref = bf16[256,512]{1,0:T(8,128)(2,1)S(1)} collective-permute-done((bf16[256,512]{1,0:T(8,128)(2,1)}, bf16[256,512]{1,0:T(8,128)(2,1)S(1)}, u32[]{:S(2)}, u32[]{:S(2)}) %collective-permute-start.22) | collective-permute-done | bytes 262176 | tf_op jit(solution)/shard_map/ppermute | solution.py:612
  132.8 4.4 %table_grad.1 = (bf16[4096,512]{1,0:T(8,128)(2,1)}, bf16[256,512]{1,0:T(8,128)(2,1)}) custom-call(f32[1,768]{1,0:T(1,128)S(1)} %get-tuple-element.44.asked_ref, bf16[768,512]{1,0:T(8,128)(2,1)S(1)} %bitcast.14, bf16[256,512]{1,0:T(8,128)(2,1)S(1)} %collective-permute-done.22.layer_ref), custom_call_target="tpu_custom_call" | custom-call | tf_op jit(solution)/shard_map/table_grad/pallas_call | solution.py:645
  (12 shorter events, 0.0 us)
Async XLA Ops:
  3.7 47.8 %copy-start = (bf16[512,2048]{1,0:T(8,128)(2,1)S(1)}, bf16[512,2048]{1,0:T(8,128)(2,1)}, u32[]{:S(2)}) copy-start(bf16[512,2048]{1,0:T(8,128)(2,1)} %refs_14_.1) | copy-start | bytes 6291460
  3.7 47.7 %copy-start.1 = (bf16[512,512]{1,0:T(8,128)(2,1)S(1)}, bf16[512,512]{1,0:T(8,128)(2,1)}, u32[]{:S(2)}) copy-start(bf16[512,512]{1,0:T(8,128)(2,1)} %refs_11_.1) | copy-start | bytes 1572868
  21.3 0.9 copy-start.5
  22.2 29.2 %all-to-all-start.1 = ((bf16[32,24,512]{2,1,0:T(8,128)(2,1)}), bf16[32,24,512]{2,1,0:T(8,128)(2,1)S(1)}, u32[]{:S(2)}, u32[]{:S(2)}) async-start(bf16[32,24,512]{2,1,0:T(8,128)(2,1)} %bitcast.20), calls=%async_computation.1 | async-start | bytes 1572864 | tf_op jit(solution)/shard_map/all_to_all | solution.py:486
  24.8 25.9 %collective-permute-start = (bf16[256,512]{1,0:T(8,128)(2,1)}, bf16[256,512]{1,0:T(8,128)(2,1)S(1)}, u32[]{:S(2)}, u32[]{:S(2)}) collective-permute-start(bf16[256,512]{1,0:T(8,128)(2,1)} %bitcast.23), channel_id=1, source_target_pairs={{0,0},{4,8},{8,4},{12,12},{1,1},{5,9},{9,5},{13,13},{2,2},{6,10},{... | collective-permute-start | bytes 786440 | tf_op jit(solution)/shard_map/ppermute | solution.py:518
  50.7 0.7 copy-start.2
  51.5 1.0 copy-start.3
  54.4 4.3 %collective-permute-start.1 = (bf16[256,256]{1,0:T(8,128)(2,1)S(1)}, bf16[256,256]{1,0:T(8,128)(2,1)S(1)}, u32[]{:S(2)}, u32[]{:S(2)}) collective-permute-start(bf16[256,256]{1,0:T(8,128)(2,1)S(1)} %get-tuple-element.47), channel_id=1, source_target_pairs={{0,1},{1,0},{2,3},{3,2},{8,9},{9,8},{10,11},{11,10},{4,5},{5,4},{6... | collective-permute-start | bytes 393224 | tf_op jit(solution)/shard_map/ppermute | solution.py:556
  55.7 5.5 %collective-permute-start.2 = (bf16[256,256]{1,0:T(8,128)(2,1)S(1)}, bf16[256,256]{1,0:T(8,128)(2,1)S(1)}, u32[]{:S(2)}, u32[]{:S(2)}) collective-permute-start(bf16[256,256]{1,0:T(8,128)(2,1)S(1)} %get-tuple-element.48), channel_id=1, source_target_pairs={{0,2},{1,3},{2,0},{3,1},{8,10},{9,11},{10,8},{11,9},{4,6},{5,7},{6... | collective-permute-start | bytes 393224 | tf_op jit(solution)/shard_map/ppermute | solution.py:556
  55.7 7.4 %collective-permute-start.3 = (bf16[256,256]{1,0:T(8,128)(2,1)S(1)}, bf16[256,256]{1,0:T(8,128)(2,1)S(1)}, u32[]{:S(2)}, u32[]{:S(2)}) collective-permute-start(bf16[256,256]{1,0:T(8,128)(2,1)S(1)} %get-tuple-element.49), channel_id=1, source_target_pairs={{0,3},{1,2},{2,1},{3,0},{8,11},{9,10},{10,9},{11,8},{4,7},{5,6},{6... | collective-permute-start | bytes 393224 | tf_op jit(solution)/shard_map/ppermute | solution.py:556
  57.2 6.0 %collective-permute-start.4 = (bf16[256,256]{1,0:T(8,128)(2,1)S(1)}, bf16[256,256]{1,0:T(8,128)(2,1)S(1)}, u32[]{:S(2)}, u32[]{:S(2)}) collective-permute-start(bf16[256,256]{1,0:T(8,128)(2,1)S(1)} %get-tuple-element.50), channel_id=1, source_target_pairs={{0,8},{1,9},{2,10},{3,11},{8,0},{9,1},{10,2},{11,3},{4,12},{5,13},... | collective-permute-start | bytes 393224 | tf_op jit(solution)/shard_map/ppermute | solution.py:556
  57.2 8.4 %collective-permute-start.5 = (bf16[256,256]{1,0:T(8,128)(2,1)S(1)}, bf16[256,256]{1,0:T(8,128)(2,1)S(1)}, u32[]{:S(2)}, u32[]{:S(2)}) collective-permute-start(bf16[256,256]{1,0:T(8,128)(2,1)S(1)} %get-tuple-element.51), channel_id=1, source_target_pairs={{0,9},{1,8},{2,11},{3,10},{8,1},{9,0},{10,3},{11,2},{4,13},{5,12},... | collective-permute-start | bytes 393224 | tf_op jit(solution)/shard_map/ppermute | solution.py:556
  58.8 6.8 %collective-permute-start.6 = (bf16[256,256]{1,0:T(8,128)(2,1)S(1)}, bf16[256,256]{1,0:T(8,128)(2,1)S(1)}, u32[]{:S(2)}, u32[]{:S(2)}) collective-permute-start(bf16[256,256]{1,0:T(8,128)(2,1)S(1)} %get-tuple-element.52), channel_id=1, source_target_pairs={{0,10},{1,11},{2,8},{3,9},{8,2},{9,3},{10,0},{11,1},{4,14},{5,15},... | collective-permute-start | bytes 393224 | tf_op jit(solution)/shard_map/ppermute | solution.py:556
  61.2 7.5 %collective-permute-start.7 = (bf16[256,256]{1,0:T(8,128)(2,1)S(1)}, bf16[256,256]{1,0:T(8,128)(2,1)S(1)}, u32[]{:S(2)}, u32[]{:S(2)}) collective-permute-start(bf16[256,256]{1,0:T(8,128)(2,1)S(1)} %get-tuple-element.53), channel_id=1, source_target_pairs={{0,11},{1,10},{2,9},{3,8},{8,3},{9,2},{10,1},{11,0},{4,15},{5,14},... | collective-permute-start | bytes 393224 | tf_op jit(solution)/shard_map/ppermute | solution.py:556
  72.7 4.5 %collective-permute-start.8 = (bf16[104,256]{1,0:T(8,128)(2,1)S(1)}, bf16[104,256]{1,0:T(8,128)(2,1)S(1)}, u32[]{:S(2)}, u32[]{:S(2)}) collective-permute-start(bf16[104,256]{1,0:T(8,128)(2,1)S(1)} %get-tuple-element.55), channel_id=1, source_target_pairs={{0,1},{1,0},{2,3},{3,2},{8,9},{9,8},{10,11},{11,10},{4,5},{5,4},{6... | collective-permute-start | bytes 159752 | tf_op jit(solution)/shard_map/ppermute | solution.py:556
  72.9 4.8 %collective-permute-start.9 = (bf16[104,256]{1,0:T(8,128)(2,1)S(1)}, bf16[104,256]{1,0:T(8,128)(2,1)S(1)}, u32[]{:S(2)}, u32[]{:S(2)}) collective-permute-start(bf16[104,256]{1,0:T(8,128)(2,1)S(1)} %get-tuple-element.56), channel_id=1, source_target_pairs={{0,2},{1,3},{2,0},{3,1},{8,10},{9,11},{10,8},{11,9},{4,6},{5,7},{6... | collective-permute-start | bytes 159752 | tf_op jit(solution)/shard_map/ppermute | solution.py:556
  73.0 9.3 %collective-permute-start.10 = (bf16[104,256]{1,0:T(8,128)(2,1)S(1)}, bf16[104,256]{1,0:T(8,128)(2,1)S(1)}, u32[]{:S(2)}, u32[]{:S(2)}) collective-permute-start(bf16[104,256]{1,0:T(8,128)(2,1)S(1)} %get-tuple-element.57), channel_id=1, source_target_pairs={{0,3},{1,2},{2,1},{3,0},{8,11},{9,10},{10,9},{11,8},{4,7},{5,6},{6... | collective-permute-start | bytes 159752 | tf_op jit(solution)/shard_map/ppermute | solution.py:556
  75.4 6.9 %collective-permute-start.11 = (bf16[104,256]{1,0:T(8,128)(2,1)S(1)}, bf16[104,256]{1,0:T(8,128)(2,1)S(1)}, u32[]{:S(2)}, u32[]{:S(2)}) collective-permute-start(bf16[104,256]{1,0:T(8,128)(2,1)S(1)} %get-tuple-element.58), channel_id=1, source_target_pairs={{0,8},{1,9},{2,10},{3,11},{8,0},{9,1},{10,2},{11,3},{4,12},{5,13},... | collective-permute-start | bytes 159752 | tf_op jit(solution)/shard_map/ppermute | solution.py:556
  76.8 5.5 %collective-permute-start.12 = (bf16[104,256]{1,0:T(8,128)(2,1)S(1)}, bf16[104,256]{1,0:T(8,128)(2,1)S(1)}, u32[]{:S(2)}, u32[]{:S(2)}) collective-permute-start(bf16[104,256]{1,0:T(8,128)(2,1)S(1)} %get-tuple-element.59), channel_id=1, source_target_pairs={{0,9},{1,8},{2,11},{3,10},{8,1},{9,0},{10,3},{11,2},{4,13},{5,12},... | collective-permute-start | bytes 159752 | tf_op jit(solution)/shard_map/ppermute | solution.py:556
  77.2 5.1 %collective-permute-start.13 = (bf16[104,256]{1,0:T(8,128)(2,1)S(1)}, bf16[104,256]{1,0:T(8,128)(2,1)S(1)}, u32[]{:S(2)}, u32[]{:S(2)}) collective-permute-start(bf16[104,256]{1,0:T(8,128)(2,1)S(1)} %get-tuple-element.60), channel_id=1, source_target_pairs={{0,10},{1,11},{2,8},{3,9},{8,2},{9,3},{10,0},{11,1},{4,14},{5,15},... | collective-permute-start | bytes 159752 | tf_op jit(solution)/shard_map/ppermute | solution.py:556
  77.7 5.4 %collective-permute-start.14 = (bf16[104,256]{1,0:T(8,128)(2,1)S(1)}, bf16[104,256]{1,0:T(8,128)(2,1)S(1)}, u32[]{:S(2)}, u32[]{:S(2)}) collective-permute-start(bf16[104,256]{1,0:T(8,128)(2,1)S(1)} %get-tuple-element.61), channel_id=1, source_target_pairs={{0,11},{1,10},{2,9},{3,8},{8,3},{9,2},{10,1},{11,0},{4,15},{5,14},... | collective-permute-start | bytes 159752 | tf_op jit(solution)/shard_map/ppermute | solution.py:556
  83.1 18.1 %copy-start.4 = (bf16[256,512]{1,0:T(8,128)(2,1)S(1)}, bf16[256,512]{1,0:T(8,128)(2,1)}, u32[]{:S(2)}) copy-start(bf16[256,512]{1,0:T(8,128)(2,1)} %copy-done.2) | copy-start | bytes 786436
  88.8 4.2 %collective-permute-start.15 = (bf16[384,128]{1,0:T(8,128)(2,1)S(1)}, bf16[384,128]{1,0:T(8,128)(2,1)S(1)}, u32[]{:S(2)}, u32[]{:S(2)}) collective-permute-start(bf16[384,128]{1,0:T(8,128)(2,1)S(1)} %get-tuple-element.67), channel_id=1, source_target_pairs={{0,1},{1,0},{2,3},{3,2},{8,9},{9,8},{10,11},{11,10},{4,5},{5,4},{6... | collective-permute-start | bytes 294920 | tf_op jit(solution)/shard_map/ppermute | solution.py:556
  89.3 5.1 %collective-permute-start.16 = (bf16[384,128]{1,0:T(8,128)(2,1)S(1)}, bf16[384,128]{1,0:T(8,128)(2,1)S(1)}, u32[]{:S(2)}, u32[]{:S(2)}) collective-permute-start(bf16[384,128]{1,0:T(8,128)(2,1)S(1)} %get-tuple-element.68), channel_id=1, source_target_pairs={{0,2},{1,3},{2,0},{3,1},{8,10},{9,11},{10,8},{11,9},{4,6},{5,7},{6... | collective-permute-start | bytes 294920 | tf_op jit(solution)/shard_map/ppermute | solution.py:556
  90.3 6.5 %collective-permute-start.17 = (bf16[384,128]{1,0:T(8,128)(2,1)S(1)}, bf16[384,128]{1,0:T(8,128)(2,1)S(1)}, u32[]{:S(2)}, u32[]{:S(2)}) collective-permute-start(bf16[384,128]{1,0:T(8,128)(2,1)S(1)} %get-tuple-element.69), channel_id=1, source_target_pairs={{0,3},{1,2},{2,1},{3,0},{8,11},{9,10},{10,9},{11,8},{4,7},{5,6},{6... | collective-permute-start | bytes 294920 | tf_op jit(solution)/shard_map/ppermute | solution.py:556
  91.5 5.3 %collective-permute-start.18 = (bf16[384,128]{1,0:T(8,128)(2,1)S(1)}, bf16[384,128]{1,0:T(8,128)(2,1)S(1)}, u32[]{:S(2)}, u32[]{:S(2)}) collective-permute-start(bf16[384,128]{1,0:T(8,128)(2,1)S(1)} %get-tuple-element.70), channel_id=1, source_target_pairs={{0,8},{1,9},{2,10},{3,11},{8,0},{9,1},{10,2},{11,3},{4,12},{5,13},... | collective-permute-start | bytes 294920 | tf_op jit(solution)/shard_map/ppermute | solution.py:556
  92.7 5.8 %collective-permute-start.19 = (bf16[384,128]{1,0:T(8,128)(2,1)S(1)}, bf16[384,128]{1,0:T(8,128)(2,1)S(1)}, u32[]{:S(2)}, u32[]{:S(2)}) collective-permute-start(bf16[384,128]{1,0:T(8,128)(2,1)S(1)} %get-tuple-element.71), channel_id=1, source_target_pairs={{0,9},{1,8},{2,11},{3,10},{8,1},{9,0},{10,3},{11,2},{4,13},{5,12},... | collective-permute-start | bytes 294920 | tf_op jit(solution)/shard_map/ppermute | solution.py:556
  93.0 5.5 %collective-permute-start.20 = (bf16[384,128]{1,0:T(8,128)(2,1)S(1)}, bf16[384,128]{1,0:T(8,128)(2,1)S(1)}, u32[]{:S(2)}, u32[]{:S(2)}) collective-permute-start(bf16[384,128]{1,0:T(8,128)(2,1)S(1)} %get-tuple-element.72), channel_id=1, source_target_pairs={{0,10},{1,11},{2,8},{3,9},{8,2},{9,3},{10,0},{11,1},{4,14},{5,15},... | collective-permute-start | bytes 294920 | tf_op jit(solution)/shard_map/ppermute | solution.py:556
  94.4 6.7 %collective-permute-start.21 = (bf16[384,128]{1,0:T(8,128)(2,1)S(1)}, bf16[384,128]{1,0:T(8,128)(2,1)S(1)}, u32[]{:S(2)}, u32[]{:S(2)}) collective-permute-start(bf16[384,128]{1,0:T(8,128)(2,1)S(1)} %get-tuple-element.73), channel_id=1, source_target_pairs={{0,11},{1,10},{2,9},{3,8},{8,3},{9,2},{10,1},{11,0},{4,15},{5,14},... | collective-permute-start | bytes 294920 | tf_op jit(solution)/shard_map/ppermute | solution.py:556
  96.8 6.7 %copy-start.6 = (bf16[256,512]{1,0:T(8,128)(2,1)}, bf16[256,512]{1,0:T(8,128)(2,1)S(1)}, u32[]{:S(2)}) copy-start(bf16[256,512]{1,0:T(8,128)(2,1)S(1)} %get-tuple-element.79) | copy-start | bytes 786436
  103.5 29.3 %all-to-all-start.2 = ((bf16[32,24,512]{2,1,0:T(8,128)(2,1)}), bf16[32,24,512]{2,1,0:T(8,128)(2,1)S(1)}, u32[]{:S(2)}, u32[]{:S(2)}) async-start(bf16[32,24,512]{2,1,0:T(8,128)(2,1)} %bitcast.8), calls=%async_computation.2 | async-start | bytes 1572864 | tf_op jit(solution)/shard_map/all_to_all | solution.py:486
  107.0 25.8 %collective-permute-start.22 = (bf16[256,512]{1,0:T(8,128)(2,1)}, bf16[256,512]{1,0:T(8,128)(2,1)S(1)}, u32[]{:S(2)}, u32[]{:S(2)}) collective-permute-start(bf16[256,512]{1,0:T(8,128)(2,1)} %copy-done.6), channel_id=1, source_target_pairs={{0,0},{4,8},{8,4},{12,12},{1,1},{5,9},{9,5},{13,13},{2,2},{6,10},{... | collective-permute-start | bytes 786440 | tf_op jit(solution)/shard_map/ppermute | solution.py:612

commit v5 on v4

--- a/solution.py
+++ b/solution.py
@@ -395,15 +395,23 @@
     hand_out(me_s, pieces, out_ref)
 
 
+def prepare_kernel(mail_ref, emb_ref, cot_ref, places_ref, scaled_ref, inv_ref, mask_ref):
+    slot_row, live_row = read_note(mail_ref)
+    slots, count = places_ref.shape
+    places_ref[...] = jnp.where(iota((slots, count), 0) == slot_row, 1.0, 0.0).astype(bf16)
+    normed, spread = normalize(emb_ref[...].astype(f32))
+    scaled_ref[...] = normed
+    inv_ref[...] = jnp.broadcast_to(1.0 / spread, inv_ref.shape)
+    mask_ref[...] = jnp.where(to_col(live_row) > 0.0, cot_ref[...].astype(f32), 0.0)
+
+
 def finish_kernel(copies, group, me_s, *refs):
     pieces, refs = refs[:group], refs[group:]
-    mail_ref, slope_ref, norm_ref, mgrad_ref, emb_ref, cot_ref, w_ref, out_ref, grad_ref = refs
+    places_ref, normed_ref, inv_ref, cot_ref, slope_ref, norm_ref, mgrad_ref, w_ref = refs[:8]
+    out_ref, grad_ref = refs[8:]
     take_in(me_s, pieces, grad_ref)
-    slot_row, live_row = read_note(mail_ref)
-    count, width = emb_ref.shape
-    slots = out_ref.shape[0]
+    count, width = normed_ref.shape
     head = width // HEADS
-    live_col = to_col(live_row)
     heads = range(0, HEADS * copies, copies)
 
     def part(h, span, lanes):
@@ -423,13 +431,11 @@
     act_grad = jnp.concatenate([mgrad_ref[...] * norm_ref[...], values, queries, keys], axis=1)
     pre_grad = (act_grad * slope_ref[...]).astype(bf16)
     norm_grad = dot(pre_grad, w_ref[...], ((1,), (1,)))
-    normed, spread = normalize(emb_ref[...].astype(f32))
+    normed = normed_ref[...]
     mean_grad = jnp.mean(norm_grad, axis=-1, keepdims=True)
     mean_prod = jnp.mean(norm_grad * normed, axis=-1, keepdims=True)
-    cot = jnp.where(live_col > 0.0, cot_ref[...].astype(f32), 0.0)
-    emb_grad = cot + (norm_grad - mean_grad - normed * mean_prod) / spread
-    places = jnp.where(iota((slots, count), 0) == slot_row, 1.0, 0.0).astype(bf16)
-    out_ref[...] = dot(places, emb_grad.astype(bf16)).astype(bf16)
+    emb_grad = cot_ref[...] + (norm_grad - mean_grad - normed * mean_prod) * inv_ref[:, 0:1]
+    out_ref[...] = dot(places_ref[...], emb_grad.astype(bf16)).astype(bf16)
 
 
 def pick_kernel(cap, part, askers, mail_ref, table_ref, out_ref, asked_ref, lane_scr, block_scr):
@@ -571,6 +577,16 @@
         numbers=(me,),
     )
     mine = exchange(sent)
+    prepared = kernel_call(
+        prepare_kernel,
+        (
+            ((slots, count), bf16),
+            ((count, width), f32),
+            ((count, LANES), f32),
+            ((count, width), f32),
+        ),
+        (mail, emb, cot),
+    )
     length = group * count
     tiles = group * (group + 1) // 2 * count
     ready = tiles * count * 6 <= 16 * 1024 * 1024
@@ -636,7 +652,7 @@
     (outgoing,) = kernel_call(
         functools.partial(finish_kernel, copies, group),
         (((slots, width), bf16),),
-        (*back, mail, slope, att_n, mgrad, emb, cot, input_proj),
+        (*back, *prepared, slope, att_n, mgrad, input_proj),
         scratch=[pltpu.VMEM((group, *back_piece[0]), bf16)],
         numbers=(me,),
     )

time: 138 us -> 138 us (level)
    pallas_call x7 -> x8, Pallas kernels: 20.7 us -> 20.9 us  [kernel_call(): pl.pallas_call(kernel, out_shape=tuple((pltpu.VMEM(shape, dtype) for shap...]
  transfers between devices with their start and end apart: 25 -> 25, of which waited for: 9 -> 9; matrix products, arithmetic and copies ran while one was open for 0% -> 0% of each run, Pallas kernels for 2% -> 3%
where the time goes in v5:
time: 138 us; the launch traced here: 137 us
  waiting for transfers between devices  56.7 us (41%)
  starting transfers between devices  34.5 us (25%)
  Pallas kernels  27.8 us (20%)
  blocking collectives  14 us (10%)
  local copies, waits for them, and re-layouts  2.59 us (2%)
  between operations  1.67 us (1%)
    ppermute x1, waiting for transfers between devices, local(): layer_out = moved(layer_out)  21.3 us
    ppermute x1, waiting for transfers between devices, local(): cot = moved(out_cotangent[0])  21.1 us
    pallas_call x8, Pallas kernels, kernel_call(): pl.pallas_call(kernel, out_shape=tuple((pltpu.VMEM(shape, dtype) for shap...  20.9 us
    ppermute x21, starting transfers between devices, exchange(): lax.ppermute(pieces[k], GROUP, [(g, g ^ k) for g in range(group)])  19.2 us
    ppermute x21, waiting for transfers between devices, exchange(): lax.ppermute(pieces[k], GROUP, [(g, g ^ k) for g in range(group)])  14.3 us
    all_to_all x1, blocking collectives, all_to_all(): return lax.all_to_all(pieces, axes, split_axis=0, concat_axis=0, tiled=True)  14 us
    all_to_all x2, starting transfers between devices, all_to_all(): return lax.all_to_all(pieces, axes, split_axis=0, concat_axis=0, tiled=True)  6.11 us
    ppermute x1, starting transfers between devices, local(): cot = moved(out_cotangent[0])  4.75 us
  transfers between devices with their start and end apart: 25, of which 9 were waited for; matrix products, arithmetic and copies ran while one was open for 0% of the time, Pallas kernels for 3%

profile of v5, /device:TPU:1, one launch (start us, length us, event | category | flops | bytes accessed | tf_op | source)
XLA Modules:
  0.0 137.2 jit_solution(5392364581312886061)
XLA Ops:
  1.3 2.4 %requests.1 = (s32[32,384]{1,0:T(8,128)S(1)}, bf16[4096,512]{1,0:T(8,128)(2,1)S(1)}) custom-call(s32[1]{0:T(128)} %bitcast.unused_s.me_s, s32[1]{0:T(128)} %bitcast.1.block_s, s32[1]{0:T(128)} %bitcast.2.twin_s, s32[1]{0:T(128)S(6)} %copy.13.length_s, s32[1,256]{1,0:T(1,128)} %ids_hbm.1, s32[1024,128]{1,0:T(8,128)} %bitcast.22, bf16[4096,512]{1,0:T(8,128)(2,1)} %table_hbm.1), custom_call_target="tpu_custom_call" | custom-call | tf_op jit(solution)/shard_map/requests/pallas_call | solution.py:525
  3.7 0.0 copy-start
  3.7 0.0 copy-start.1
  3.7 0.1 copy.9
  3.8 14.0 %all_to_all.21 = s32[32,1,384]{2,1,0:T(1,128)S(1)} all-to-all(s32[32,1,384]{2,1,0:T(1,128)S(1)} %copy.9), channel_id=1, replica_groups=mesh['a'=2,'b'=2,'c'=2,'d'=4] {'a','b','c','d'}, dimensions={0} | all-to-all | bytes 98304 | tf_op jit(solution)/shard_map/all_to_all | solution.py:492
  17.8 3.5 %shard_map.86 = (bf16[768,512]{1,0:T(8,128)(2,1)S(1)}, f32[1,768]{1,0:T(1,128)S(1)}) custom-call(s32[32,384]{1,0:T(8,128)S(1)} %bitcast.16, bf16[4096,512]{1,0:T(8,128)(2,1)S(1)} %get-tuple-element.47.table_ref), custom_call_target="tpu_custom_call" | custom-call | tf_op jit(solution)/shard_map/pallas_call | solution.py:48
  21.3 0.0 copy-start.5
  21.3 0.9 copy-done.5
  22.2 2.6 %all-to-all-start.1 = ((bf16[32,24,512]{2,1,0:T(8,128)(2,1)}), bf16[32,24,512]{2,1,0:T(8,128)(2,1)S(1)}, u32[]{:S(2)}, u32[]{:S(2)}) async-start(bf16[32,24,512]{2,1,0:T(8,128)(2,1)} %bitcast.20), calls=%async_computation.1 | async-start | bytes 1572864 | tf_op jit(solution)/shard_map/all_to_all | solution.py:492
  24.8 4.7 %collective-permute-start = (bf16[256,512]{1,0:T(8,128)(2,1)}, bf16[256,512]{1,0:T(8,128)(2,1)S(1)}, u32[]{:S(2)}, u32[]{:S(2)}) collective-permute-start(bf16[256,512]{1,0:T(8,128)(2,1)} %bitcast.23), channel_id=1, source_target_pairs={{0,0},{4,8},{8,4},{12,12},{1,1},{5,9},{9,5},{13,13},{2,2},{6,10},{... | collective-permute-start | bytes 786440 | tf_op jit(solution)/shard_map/ppermute | solution.py:524
  29.6 21.1 %collective-permute-done.cot_ref = bf16[256,512]{1,0:T(8,128)(2,1)S(1)} collective-permute-done((bf16[256,512]{1,0:T(8,128)(2,1)}, bf16[256,512]{1,0:T(8,128)(2,1)S(1)}, u32[]{:S(2)}, u32[]{:S(2)}) %collective-permute-start) | collective-permute-done | bytes 262176 | tf_op jit(solution)/shard_map/ppermute | solution.py:524
  50.7 0.7 copy-done.2
  51.4 0.0 all-to-all-done.1
  51.5 0.0 copy-start.3
  51.5 0.9 copy-done.3
  52.4 2.0 %shard_map.87 = (bf16[256,512]{1,0:T(8,128)(2,1)S(1)}, f32[256,2048]{1,0:T(8,128)S(1)}, f32[256,512]{1,0:T(8,128)S(1)}, f32[256,512]{1,0:T(8,128)S(1)}, bf16[256...) custom-call(s32[1]{0:T(128)} %bitcast.unused_s.me_s, ...), custom_call_target="tpu_custom_call" | custom-call | tf_op jit(solution)/shard_map/pallas_call | solution.py:48
  54.4 1.3 collective-permute-start.1
  55.7 0.0 collective-permute-start.2
  55.7 1.4 %collective-permute-start.3 = (bf16[256,256]{1,0:T(8,128)(2,1)S(1)}, bf16[256,256]{1,0:T(8,128)(2,1)S(1)}, u32[]{:S(2)}, u32[]{:S(2)}) collective-permute-start(bf16[256,256]{1,0:T(8,128)(2,1)S(1)} %get-tuple-element.53), channel_id=1, source_target_pairs={{0,3},{1,2},{2,1},{3,0},{8,11},{9,10},{10,9},{11,8},{4,7},{5,6},{6... | collective-permute-start | bytes 393224 | tf_op jit(solution)/shard_map/ppermute | solution.py:562
  57.2 0.0 collective-permute-start.4
  57.2 1.6 %collective-permute-start.5 = (bf16[256,256]{1,0:T(8,128)(2,1)S(1)}, bf16[256,256]{1,0:T(8,128)(2,1)S(1)}, u32[]{:S(2)}, u32[]{:S(2)}) collective-permute-start(bf16[256,256]{1,0:T(8,128)(2,1)S(1)} %get-tuple-element.55), channel_id=1, source_target_pairs={{0,9},{1,8},{2,11},{3,10},{8,1},{9,0},{10,3},{11,2},{4,13},{5,12},... | collective-permute-start | bytes 393224 | tf_op jit(solution)/shard_map/ppermute | solution.py:562
  58.8 0.0 collective-permute-done.1.refs_1_
  58.8 0.0 collective-permute-start.6
  58.8 2.4 %collective-permute-done.2.refs_2_ = bf16[256,256]{1,0:T(8,128)(2,1)S(1)} collective-permute-done((bf16[256,256]{1,0:T(8,128)(2,1)S(1)}, bf16[256,256]{1,0:T(8,128)(2,1)S(1)}, u32[]{:S(2)}, u32[]{:S(2)}) %collective-permute-start.2) | collective-permute-done | bytes 131104 | tf_op jit(solution)/shard_map/ppermute | solution.py:562
  61.2 0.4 collective-permute-start.7
  61.6 1.5 %collective-permute-done.3.refs_3_ = bf16[256,256]{1,0:T(8,128)(2,1)S(1)} collective-permute-done((bf16[256,256]{1,0:T(8,128)(2,1)S(1)}, bf16[256,256]{1,0:T(8,128)(2,1)S(1)}, u32[]{:S(2)}, u32[]{:S(2)}) %collective-permute-start.3) | collective-permute-done | bytes 131104 | tf_op jit(solution)/shard_map/ppermute | solution.py:562
  63.1 0.0 collective-permute-done.4.refs_4_
  63.1 2.4 %collective-permute-done.5.refs_5_ = bf16[256,256]{1,0:T(8,128)(2,1)S(1)} collective-permute-done((bf16[256,256]{1,0:T(8,128)(2,1)S(1)}, bf16[256,256]{1,0:T(8,128)(2,1)S(1)}, u32[]{:S(2)}, u32[]{:S(2)}) %collective-permute-start.5) | collective-permute-done | bytes 131104 | tf_op jit(solution)/shard_map/ppermute | solution.py:562
  65.5 0.0 collective-permute-done.6.refs_6_
  65.5 3.2 %collective-permute-done.7.refs_7_ = bf16[256,256]{1,0:T(8,128)(2,1)S(1)} collective-permute-done((bf16[256,256]{1,0:T(8,128)(2,1)S(1)}, bf16[256,256]{1,0:T(8,128)(2,1)S(1)}, u32[]{:S(2)}, u32[]{:S(2)}) %collective-permute-start.7) | collective-permute-done | bytes 131104 | tf_op jit(solution)/shard_map/ppermute | solution.py:562
  68.7 4.0 %shard_map.88 = (bf16[8,256,256]{2,1,0:T(8,128)(2,1)S(1)}, f32[8,64,256]{2,1,0:T(8,128)S(1)}, f32[8,64,256]{2,1,0:T(8,128)S(1)}, bf16[9216,256]{1,0:T(8,128)(2,1...) custom-call(s32[1]{0:T(128)} %bitcast.unused_s.me_s, ...), custom_call_target="tpu_custom_call" | custom-call | tf_op jit(solution)/shard_map/pallas_call | solution.py:48
  72.7 0.2 collective-permute-start.8
  72.9 0.2 collective-permute-start.9
  73.0 2.4 %collective-permute-start.10 = (bf16[104,256]{1,0:T(8,128)(2,1)S(1)}, bf16[104,256]{1,0:T(8,128)(2,1)S(1)}, u32[]{:S(2)}, u32[]{:S(2)}) collective-permute-start(bf16[104,256]{1,0:T(8,128)(2,1)S(1)} %get-tuple-element.61), channel_id=1, source_target_pairs={{0,3},{1,2},{2,1},{3,0},{8,11},{9,10},{10,9},{11,8},{4,7},{5,6},{6... | collective-permute-start | bytes 159752 | tf_op jit(solution)/shard_map/ppermute | solution.py:562
  75.4 1.4 %collective-permute-start.11 = (bf16[104,256]{1,0:T(8,128)(2,1)S(1)}, bf16[104,256]{1,0:T(8,128)(2,1)S(1)}, u32[]{:S(2)}, u32[]{:S(2)}) collective-permute-start(bf16[104,256]{1,0:T(8,128)(2,1)S(1)} %get-tuple-element.62), channel_id=1, source_target_pairs={{0,8},{1,9},{2,10},{3,11},{8,0},{9,1},{10,2},{11,3},{4,12},{5,13},... | collective-permute-start | bytes 159752 | tf_op jit(solution)/shard_map/ppermute | solution.py:562
  76.8 0.4 collective-permute-start.12
  77.2 0.0 collective-permute-done.8.refs_1_
  77.2 0.5 collective-permute-start.13
  77.7 0.0 collective-permute-done.9.refs_2_
  77.7 1.9 %collective-permute-start.14 = (bf16[104,256]{1,0:T(8,128)(2,1)S(1)}, bf16[104,256]{1,0:T(8,128)(2,1)S(1)}, u32[]{:S(2)}, u32[]{:S(2)}) collective-permute-start(bf16[104,256]{1,0:T(8,128)(2,1)S(1)} %get-tuple-element.65), channel_id=1, source_target_pairs={{0,11},{1,10},{2,9},{3,8},{8,3},{9,2},{10,1},{11,0},{4,15},{5,14},... | collective-permute-start | bytes 159752 | tf_op jit(solution)/shard_map/ppermute | solution.py:562
  79.6 2.7 %shard_map.89.refs_10_ = f32[9216,256]{1,0:T(8,128)S(1)} custom-call(bf16[8,256,256]{2,1,0:T(8,128)(2,1)S(1)} %get-tuple-element.66.x_ref.refs_8_), custom_call_target="tpu_custom_call" | custom-call | tf_op jit(solution)/shard_map/pallas_call | solution.py:48
  82.3 0.0 collective-permute-done.12.refs_5_
  82.3 0.7 collective-permute-done.14.refs_7_
  83.1 5.7 %shard_map.90 = (bf16[384,128]{1,0:T(8,128)(2,1)S(1)}, bf16[384,128]{1,0:T(8,128)(2,1)S(1)}, bf16[384,128]{1,0:T(8,128)(2,1)S(1)}, bf16[384,128]{1,0:T(8,128)(2,...) custom-call(s32[1]{0:T(128)} %bitcast.unused_s.me_s, ...), custom_call_target="tpu_custom_call" | custom-call | tf_op jit(solution)/shard_map/pallas_call | solution.py:48
  88.8 0.5 collective-permute-start.15
  89.3 1.0 collective-permute-start.16
  90.3 1.2 collective-permute-start.17
  91.5 1.2 collective-permute-start.18
  92.7 0.3 collective-permute-start.19
  93.0 0.0 collective-permute-done.15.refs_1_
  93.0 1.4 %collective-permute-start.20 = (bf16[384,128]{1,0:T(8,128)(2,1)S(1)}, bf16[384,128]{1,0:T(8,128)(2,1)S(1)}, u32[]{:S(2)}, u32[]{:S(2)}) collective-permute-start(bf16[384,128]{1,0:T(8,128)(2,1)S(1)} %get-tuple-element.76), channel_id=1, source_target_pairs={{0,10},{1,11},{2,8},{3,9},{8,2},{9,3},{10,0},{11,1},{4,14},{5,15},... | collective-permute-start | bytes 294920 | tf_op jit(solution)/shard_map/ppermute | solution.py:562
  94.4 1.9 %collective-permute-start.21 = (bf16[384,128]{1,0:T(8,128)(2,1)S(1)}, bf16[384,128]{1,0:T(8,128)(2,1)S(1)}, u32[]{:S(2)}, u32[]{:S(2)}) collective-permute-start(bf16[384,128]{1,0:T(8,128)(2,1)S(1)} %get-tuple-element.77), channel_id=1, source_target_pairs={{0,11},{1,10},{2,9},{3,8},{8,3},{9,2},{10,1},{11,0},{4,15},{5,14},... | collective-permute-start | bytes 294920 | tf_op jit(solution)/shard_map/ppermute | solution.py:562
  96.3 0.4 shard_map.91
  96.7 0.4 shard_map.92
  97.2 0.0 collective-permute-done.17.refs_3_
  97.2 1.3 collective-permute-done.19.refs_5_
  98.5 0.0 collective-permute-done.20.refs_6_
  98.5 2.6 %collective-permute-done.21.refs_7_ = bf16[384,128]{1,0:T(8,128)(2,1)S(1)} collective-permute-done((bf16[384,128]{1,0:T(8,128)(2,1)S(1)}, bf16[384,128]{1,0:T(8,128)(2,1)S(1)}, u32[]{:S(2)}, u32[]{:S(2)}) %collective-permute-start.21) | collective-permute-done | bytes 98336 | tf_op jit(solution)/shard_map/ppermute | solution.py:562
  101.1 2.2 %shard_map.93 = bf16[768,512]{1,0:T(8,128)(2,1)} custom-call(s32[1]{0:T(128)} %bitcast.unused_s.me_s, bf16[384,128]{1,0:T(8,128)(2,1)S(1)} %get-tuple-element.70.refs_0_, bf16[384,128]{1,0:T(8,128)(2,1)S(1)} %collective-permute-done.15.refs_1_, bf16[384,128]{1,0:T(8,128)(2,1)S(1)} %collective-permute-done.16.refs_2_, ...), custom_call_target="tpu_custom_call" | custom-call | tf_op jit(solution)/shard_map/pallas_call | solution.py:48
  103.4 3.5 %all-to-all-start.2 = ((bf16[32,24,512]{2,1,0:T(8,128)(2,1)}), bf16[32,24,512]{2,1,0:T(8,128)(2,1)S(1)}, u32[]{:S(2)}, u32[]{:S(2)}) async-start(bf16[32,24,512]{2,1,0:T(8,128)(2,1)} %bitcast.8), calls=%async_computation.2 | async-start | bytes 1572864 | tf_op jit(solution)/shard_map/all_to_all | solution.py:492
  106.8 4.4 %collective-permute-start.22 = (bf16[256,512]{1,0:T(8,128)(2,1)S(1)}, bf16[256,512]{1,0:T(8,128)(2,1)S(1)}, u32[]{:S(2)}, u32[]{:S(2)}) collective-permute-start(bf16[256,512]{1,0:T(8,128)(2,1)S(1)} %get-tuple-element.87), channel_id=1, source_target_pairs={{0,0},{4,8},{8,4},{12,12},{1,1},{5,9},{9,5},{13,13},{2,2},{6,10},{... | collective-permute-start | bytes 786440 | tf_op jit(solution)/shard_map/ppermute | solution.py:628
  111.3 21.3 %collective-permute-done.22.layer_ref = bf16[256,512]{1,0:T(8,128)(2,1)S(1)} collective-permute-done((bf16[256,512]{1,0:T(8,128)(2,1)S(1)}, bf16[256,512]{1,0:T(8,128)(2,1)S(1)}, u32[]{:S(2)}, u32[]{:S(2)}) %collective-permute-start.22) | collective-permute-done | bytes 262176 | tf_op jit(solution)/shard_map/ppermute | solution.py:628
  132.6 0.0 all-to-all-done.2
  132.6 4.4 %table_grad.1 = (bf16[4096,512]{1,0:T(8,128)(2,1)}, bf16[256,512]{1,0:T(8,128)(2,1)}) custom-call(f32[1,768]{1,0:T(1,128)S(1)} %get-tuple-element.48.asked_ref, bf16[768,512]{1,0:T(8,128)(2,1)S(1)} %bitcast.14, bf16[256,512]{1,0:T(8,128)(2,1)S(1)} %collective-permute-done.22.layer_ref), custom_call_target="tpu_custom_call" | custom-call | tf_op jit(solution)/shard_map/table_grad/pallas_call | solution.py:661
  (11 shorter events, 0.0 us)
Async XLA Ops:
  3.7 47.8 %copy-start = (bf16[512,2048]{1,0:T(8,128)(2,1)S(1)}, bf16[512,2048]{1,0:T(8,128)(2,1)}, u32[]{:S(2)}) copy-start(bf16[512,2048]{1,0:T(8,128)(2,1)} %refs_15_.1) | copy-start | bytes 6291460
  3.7 47.7 %copy-start.1 = (bf16[512,512]{1,0:T(8,128)(2,1)S(1)}, bf16[512,512]{1,0:T(8,128)(2,1)}, u32[]{:S(2)}) copy-start(bf16[512,512]{1,0:T(8,128)(2,1)} %refs_11_.1) | copy-start | bytes 1572868
  21.3 0.9 copy-start.5
  22.2 29.2 %all-to-all-start.1 = ((bf16[32,24,512]{2,1,0:T(8,128)(2,1)}), bf16[32,24,512]{2,1,0:T(8,128)(2,1)S(1)}, u32[]{:S(2)}, u32[]{:S(2)}) async-start(bf16[32,24,512]{2,1,0:T(8,128)(2,1)} %bitcast.20), calls=%async_computation.1 | async-start | bytes 1572864 | tf_op jit(solution)/shard_map/all_to_all | solution.py:492
  24.8 25.9 %collective-permute-start = (bf16[256,512]{1,0:T(8,128)(2,1)}, bf16[256,512]{1,0:T(8,128)(2,1)S(1)}, u32[]{:S(2)}, u32[]{:S(2)}) collective-permute-start(bf16[256,512]{1,0:T(8,128)(2,1)} %bitcast.23), channel_id=1, source_target_pairs={{0,0},{4,8},{8,4},{12,12},{1,1},{5,9},{9,5},{13,13},{2,2},{6,10},{... | collective-permute-start | bytes 786440 | tf_op jit(solution)/shard_map/ppermute | solution.py:524
  50.7 0.7 copy-start.2
  51.5 1.0 copy-start.3
  54.4 4.3 %collective-permute-start.1 = (bf16[256,256]{1,0:T(8,128)(2,1)S(1)}, bf16[256,256]{1,0:T(8,128)(2,1)S(1)}, u32[]{:S(2)}, u32[]{:S(2)}) collective-permute-start(bf16[256,256]{1,0:T(8,128)(2,1)S(1)} %get-tuple-element.51), channel_id=1, source_target_pairs={{0,1},{1,0},{2,3},{3,2},{8,9},{9,8},{10,11},{11,10},{4,5},{5,4},{6... | collective-permute-start | bytes 393224 | tf_op jit(solution)/shard_map/ppermute | solution.py:562
  55.7 5.5 %collective-permute-start.2 = (bf16[256,256]{1,0:T(8,128)(2,1)S(1)}, bf16[256,256]{1,0:T(8,128)(2,1)S(1)}, u32[]{:S(2)}, u32[]{:S(2)}) collective-permute-start(bf16[256,256]{1,0:T(8,128)(2,1)S(1)} %get-tuple-element.52), channel_id=1, source_target_pairs={{0,2},{1,3},{2,0},{3,1},{8,10},{9,11},{10,8},{11,9},{4,6},{5,7},{6... | collective-permute-start | bytes 393224 | tf_op jit(solution)/shard_map/ppermute | solution.py:562
  55.7 7.4 %collective-permute-start.3 = (bf16[256,256]{1,0:T(8,128)(2,1)S(1)}, bf16[256,256]{1,0:T(8,128)(2,1)S(1)}, u32[]{:S(2)}, u32[]{:S(2)}) collective-permute-start(bf16[256,256]{1,0:T(8,128)(2,1)S(1)} %get-tuple-element.53), channel_id=1, source_target_pairs={{0,3},{1,2},{2,1},{3,0},{8,11},{9,10},{10,9},{11,8},{4,7},{5,6},{6... | collective-permute-start | bytes 393224 | tf_op jit(solution)/shard_map/ppermute | solution.py:562
  57.2 6.0 %collective-permute-start.4 = (bf16[256,256]{1,0:T(8,128)(2,1)S(1)}, bf16[256,256]{1,0:T(8,128)(2,1)S(1)}, u32[]{:S(2)}, u32[]{:S(2)}) collective-permute-start(bf16[256,256]{1,0:T(8,128)(2,1)S(1)} %get-tuple-element.54), channel_id=1, source_target_pairs={{0,8},{1,9},{2,10},{3,11},{8,0},{9,1},{10,2},{11,3},{4,12},{5,13},... | collective-permute-start | bytes 393224 | tf_op jit(solution)/shard_map/ppermute | solution.py:562
  57.2 8.4 %collective-permute-start.5 = (bf16[256,256]{1,0:T(8,128)(2,1)S(1)}, bf16[256,256]{1,0:T(8,128)(2,1)S(1)}, u32[]{:S(2)}, u32[]{:S(2)}) collective-permute-start(bf16[256,256]{1,0:T(8,128)(2,1)S(1)} %get-tuple-element.55), channel_id=1, source_target_pairs={{0,9},{1,8},{2,11},{3,10},{8,1},{9,0},{10,3},{11,2},{4,13},{5,12},... | collective-permute-start | bytes 393224 | tf_op jit(solution)/shard_map/ppermute | solution.py:562
  58.8 6.8 %collective-permute-start.6 = (bf16[256,256]{1,0:T(8,128)(2,1)S(1)}, bf16[256,256]{1,0:T(8,128)(2,1)S(1)}, u32[]{:S(2)}, u32[]{:S(2)}) collective-permute-start(bf16[256,256]{1,0:T(8,128)(2,1)S(1)} %get-tuple-element.56), channel_id=1, source_target_pairs={{0,10},{1,11},{2,8},{3,9},{8,2},{9,3},{10,0},{11,1},{4,14},{5,15},... | collective-permute-start | bytes 393224 | tf_op jit(solution)/shard_map/ppermute | solution.py:562
  61.2 7.5 %collective-permute-start.7 = (bf16[256,256]{1,0:T(8,128)(2,1)S(1)}, bf16[256,256]{1,0:T(8,128)(2,1)S(1)}, u32[]{:S(2)}, u32[]{:S(2)}) collective-permute-start(bf16[256,256]{1,0:T(8,128)(2,1)S(1)} %get-tuple-element.57), channel_id=1, source_target_pairs={{0,11},{1,10},{2,9},{3,8},{8,3},{9,2},{10,1},{11,0},{4,15},{5,14},... | collective-permute-start | bytes 393224 | tf_op jit(solution)/shard_map/ppermute | solution.py:562
  72.7 4.5 %collective-permute-start.8 = (bf16[104,256]{1,0:T(8,128)(2,1)S(1)}, bf16[104,256]{1,0:T(8,128)(2,1)S(1)}, u32[]{:S(2)}, u32[]{:S(2)}) collective-permute-start(bf16[104,256]{1,0:T(8,128)(2,1)S(1)} %get-tuple-element.59), channel_id=1, source_target_pairs={{0,1},{1,0},{2,3},{3,2},{8,9},{9,8},{10,11},{11,10},{4,5},{5,4},{6... | collective-permute-start | bytes 159752 | tf_op jit(solution)/shard_map/ppermute | solution.py:562
  72.9 4.8 %collective-permute-start.9 = (bf16[104,256]{1,0:T(8,128)(2,1)S(1)}, bf16[104,256]{1,0:T(8,128)(2,1)S(1)}, u32[]{:S(2)}, u32[]{:S(2)}) collective-permute-start(bf16[104,256]{1,0:T(8,128)(2,1)S(1)} %get-tuple-element.60), channel_id=1, source_target_pairs={{0,2},{1,3},{2,0},{3,1},{8,10},{9,11},{10,8},{11,9},{4,6},{5,7},{6... | collective-permute-start | bytes 159752 | tf_op jit(solution)/shard_map/ppermute | solution.py:562
  73.0 9.3 %collective-permute-start.10 = (bf16[104,256]{1,0:T(8,128)(2,1)S(1)}, bf16[104,256]{1,0:T(8,128)(2,1)S(1)}, u32[]{:S(2)}, u32[]{:S(2)}) collective-permute-start(bf16[104,256]{1,0:T(8,128)(2,1)S(1)} %get-tuple-element.61), channel_id=1, source_target_pairs={{0,3},{1,2},{2,1},{3,0},{8,11},{9,10},{10,9},{11,8},{4,7},{5,6},{6... | collective-permute-start | bytes 159752 | tf_op jit(solution)/shard_map/ppermute | solution.py:562
  75.4 6.9 %collective-permute-start.11 = (bf16[104,256]{1,0:T(8,128)(2,1)S(1)}, bf16[104,256]{1,0:T(8,128)(2,1)S(1)}, u32[]{:S(2)}, u32[]{:S(2)}) collective-permute-start(bf16[104,256]{1,0:T(8,128)(2,1)S(1)} %get-tuple-element.62), channel_id=1, source_target_pairs={{0,8},{1,9},{2,10},{3,11},{8,0},{9,1},{10,2},{11,3},{4,12},{5,13},... | collective-permute-start | bytes 159752 | tf_op jit(solution)/shard_map/ppermute | solution.py:562
  76.8 5.5 %collective-permute-start.12 = (bf16[104,256]{1,0:T(8,128)(2,1)S(1)}, bf16[104,256]{1,0:T(8,128)(2,1)S(1)}, u32[]{:S(2)}, u32[]{:S(2)}) collective-permute-start(bf16[104,256]{1,0:T(8,128)(2,1)S(1)} %get-tuple-element.63), channel_id=1, source_target_pairs={{0,9},{1,8},{2,11},{3,10},{8,1},{9,0},{10,3},{11,2},{4,13},{5,12},... | collective-permute-start | bytes 159752 | tf_op jit(solution)/shard_map/ppermute | solution.py:562
  77.2 5.1 %collective-permute-start.13 = (bf16[104,256]{1,0:T(8,128)(2,1)S(1)}, bf16[104,256]{1,0:T(8,128)(2,1)S(1)}, u32[]{:S(2)}, u32[]{:S(2)}) collective-permute-start(bf16[104,256]{1,0:T(8,128)(2,1)S(1)} %get-tuple-element.64), channel_id=1, source_target_pairs={{0,10},{1,11},{2,8},{3,9},{8,2},{9,3},{10,0},{11,1},{4,14},{5,15},... | collective-permute-start | bytes 159752 | tf_op jit(solution)/shard_map/ppermute | solution.py:562
  77.7 5.4 %collective-permute-start.14 = (bf16[104,256]{1,0:T(8,128)(2,1)S(1)}, bf16[104,256]{1,0:T(8,128)(2,1)S(1)}, u32[]{:S(2)}, u32[]{:S(2)}) collective-permute-start(bf16[104,256]{1,0:T(8,128)(2,1)S(1)} %get-tuple-element.65), channel_id=1, source_target_pairs={{0,11},{1,10},{2,9},{3,8},{8,3},{9,2},{10,1},{11,0},{4,15},{5,14},... | collective-permute-start | bytes 159752 | tf_op jit(solution)/shard_map/ppermute | solution.py:562
  83.1 13.3 %copy-start.4 = (bf16[256,512]{1,0:T(8,128)(2,1)S(1)}, bf16[256,512]{1,0:T(8,128)(2,1)}, u32[]{:S(2)}) copy-start(bf16[256,512]{1,0:T(8,128)(2,1)} %copy-done.2) | copy-start | bytes 786436
  88.8 4.2 %collective-permute-start.15 = (bf16[384,128]{1,0:T(8,128)(2,1)S(1)}, bf16[384,128]{1,0:T(8,128)(2,1)S(1)}, u32[]{:S(2)}, u32[]{:S(2)}) collective-permute-start(bf16[384,128]{1,0:T(8,128)(2,1)S(1)} %get-tuple-element.71), channel_id=1, source_target_pairs={{0,1},{1,0},{2,3},{3,2},{8,9},{9,8},{10,11},{11,10},{4,5},{5,4},{6... | collective-permute-start | bytes 294920 | tf_op jit(solution)/shard_map/ppermute | solution.py:562
  89.3 5.1 %collective-permute-start.16 = (bf16[384,128]{1,0:T(8,128)(2,1)S(1)}, bf16[384,128]{1,0:T(8,128)(2,1)S(1)}, u32[]{:S(2)}, u32[]{:S(2)}) collective-permute-start(bf16[384,128]{1,0:T(8,128)(2,1)S(1)} %get-tuple-element.72), channel_id=1, source_target_pairs={{0,2},{1,3},{2,0},{3,1},{8,10},{9,11},{10,8},{11,9},{4,6},{5,7},{6... | collective-permute-start | bytes 294920 | tf_op jit(solution)/shard_map/ppermute | solution.py:562
  90.3 6.9 %collective-permute-start.17 = (bf16[384,128]{1,0:T(8,128)(2,1)S(1)}, bf16[384,128]{1,0:T(8,128)(2,1)S(1)}, u32[]{:S(2)}, u32[]{:S(2)}) collective-permute-start(bf16[384,128]{1,0:T(8,128)(2,1)S(1)} %get-tuple-element.73), channel_id=1, source_target_pairs={{0,3},{1,2},{2,1},{3,0},{8,11},{9,10},{10,9},{11,8},{4,7},{5,6},{6... | collective-permute-start | bytes 294920 | tf_op jit(solution)/shard_map/ppermute | solution.py:562
  91.5 5.7 %collective-permute-start.18 = (bf16[384,128]{1,0:T(8,128)(2,1)S(1)}, bf16[384,128]{1,0:T(8,128)(2,1)S(1)}, u32[]{:S(2)}, u32[]{:S(2)}) collective-permute-start(bf16[384,128]{1,0:T(8,128)(2,1)S(1)} %get-tuple-element.74), channel_id=1, source_target_pairs={{0,8},{1,9},{2,10},{3,11},{8,0},{9,1},{10,2},{11,3},{4,12},{5,13},... | collective-permute-start | bytes 294920 | tf_op jit(solution)/shard_map/ppermute | solution.py:562
  92.7 5.8 %collective-permute-start.19 = (bf16[384,128]{1,0:T(8,128)(2,1)S(1)}, bf16[384,128]{1,0:T(8,128)(2,1)S(1)}, u32[]{:S(2)}, u32[]{:S(2)}) collective-permute-start(bf16[384,128]{1,0:T(8,128)(2,1)S(1)} %get-tuple-element.75), channel_id=1, source_target_pairs={{0,9},{1,8},{2,11},{3,10},{8,1},{9,0},{10,3},{11,2},{4,13},{5,12},... | collective-permute-start | bytes 294920 | tf_op jit(solution)/shard_map/ppermute | solution.py:562
  93.0 5.5 %collective-permute-start.20 = (bf16[384,128]{1,0:T(8,128)(2,1)S(1)}, bf16[384,128]{1,0:T(8,128)(2,1)S(1)}, u32[]{:S(2)}, u32[]{:S(2)}) collective-permute-start(bf16[384,128]{1,0:T(8,128)(2,1)S(1)} %get-tuple-element.76), channel_id=1, source_target_pairs={{0,10},{1,11},{2,8},{3,9},{8,2},{9,3},{10,0},{11,1},{4,14},{5,15},... | collective-permute-start | bytes 294920 | tf_op jit(solution)/shard_map/ppermute | solution.py:562
  94.4 6.7 %collective-permute-start.21 = (bf16[384,128]{1,0:T(8,128)(2,1)S(1)}, bf16[384,128]{1,0:T(8,128)(2,1)S(1)}, u32[]{:S(2)}, u32[]{:S(2)}) collective-permute-start(bf16[384,128]{1,0:T(8,128)(2,1)S(1)} %get-tuple-element.77), channel_id=1, source_target_pairs={{0,11},{1,10},{2,9},{3,8},{8,3},{9,2},{10,1},{11,0},{4,15},{5,14},... | collective-permute-start | bytes 294920 | tf_op jit(solution)/shard_map/ppermute | solution.py:562
  103.4 29.3 %all-to-all-start.2 = ((bf16[32,24,512]{2,1,0:T(8,128)(2,1)}), bf16[32,24,512]{2,1,0:T(8,128)(2,1)S(1)}, u32[]{:S(2)}, u32[]{:S(2)}) async-start(bf16[32,24,512]{2,1,0:T(8,128)(2,1)} %bitcast.8), calls=%async_computation.2 | async-start | bytes 1572864 | tf_op jit(solution)/shard_map/all_to_all | solution.py:492
  106.8 25.8 %collective-permute-start.22 = (bf16[256,512]{1,0:T(8,128)(2,1)S(1)}, bf16[256,512]{1,0:T(8,128)(2,1)S(1)}, u32[]{:S(2)}, u32[]{:S(2)}) collective-permute-start(bf16[256,512]{1,0:T(8,128)(2,1)S(1)} %get-tuple-element.87), channel_id=1, source_target_pairs={{0,0},{4,8},{8,4},{12,12},{1,1},{5,9},{9,5},{13,13},{2,2},{6,10},{... | collective-permute-start | bytes 786440 | tf_op jit(solution)/shard_map/ppermute | solution.py:628
